TPU v7x, 128 devices: a whole 4x4x4 slice. The times are simulated.
128 devices in a mesh: lon: 16 (over x_hi, z, core), lat: 8 (over y, x_lo).
Axes of the slice: x: 4 (x_hi: 2, x_lo: 2; x = x_hi * 2 + x_lo), y: 4, z: 4, core: 2. Of those that a mesh axis runs over, the one named last changes fastest.
Arguments:
- state: float32 [150, 256, 2048], P(None, 'lat', 'lon'), may hold values from -6 to 6
- diffusivity: float32 [150, 256, 2048], P(None, 'lat', 'lon'), may hold values from 0.02 to 0.24
- sea_mask: int32 [75, 256, 2048], P(None, 'lat', 'lon'), may hold values 0 or 1
- send_cols: int32 [128, 3072], P(('lon', 'lat')), may hold values from 0 to 4096, as said below
- obs_slots: int32 [4, 262144], P(None, ('lon', 'lat')), may hold values from 0 to 3071, as said below
- obs_weights: float32 [4, 262144], P(None, ('lon', 'lat')), may hold values from 0.05 to 0.5
- obs_precision: float32 [150, 262144], P(None, ('lon', 'lat')), may hold values from 0.25 to 4
Outputs:
- product: float32 [150, 256, 2048], P(None, 'lat', 'lon')
- equivalents: float32 [150, 262144], P(None, ('lon', 'lat'))
Inputs may be any that keep to these rules, and one draw needn't show every extreme that they name: `send_cols`: for each device s and owner o the first n entries of the owner's 24 entries are local column indices below 4096, the rest are 4096; n is at least 1 and at most 24; every device has some owner with n = 24, and some owner receives 24 columns from every device. `obs_slots`: every slot named refers to a live entry: for owner o, slot s * 24 + p with p below the number of live entries of device s for owner o.
All inputs are finite; a program needn't handle non-finite values. No bound on the sum of `sea_mask` on one device may be relied on, other than what follows from the above.
Results may differ from a plain program's by a relative error of at most 0.00002.
Values sent between devices are 32-bit elements; how exact they have to be, the bound alone decides.
A program may use at most 128 MiB of HBM per device.

v0:
```python
import functools

import jax
import jax.numpy as jnp
from jax import lax
from jax.experimental import pallas as pl
from jax.experimental.pallas import tpu as pltpu
from jax.sharding import PartitionSpec as P

SWEEPS = 2
GROUP = 30


def shift_lat(edge, down):
    count = lax.axis_size("lat")
    if down:
        pairs = [(i, i + 1) for i in range(count - 1)]
    else:
        pairs = [(i + 1, i) for i in range(count - 1)]
    return lax.ppermute(edge, "lat", pairs)


def shift_lon(edge, east):
    count = lax.axis_size("lon")
    if east:
        pairs = [(i, (i + 1) % count) for i in range(count)]
    else:
        pairs = [((i + 1) % count, i) for i in range(count)]
    return lax.ppermute(edge, "lon", pairs)


def halos(top, bottom, left, right):
    return (
        shift_lat(bottom, True),
        shift_lat(top, False),
        shift_lon(right, True),
        shift_lon(left, False),
    )


def sweep_kernel(rows, v_ref, c_ref, vn_ref, vs_ref, vw_ref, ve_ref, cn_ref, cs_ref, cw_ref, ce_ref,
                 w_ref, top_ref, bot_ref, left_ref, right_ref):
    group = vn_ref.shape[1]
    lanes = v_ref.shape[2]
    lane = lax.broadcasted_iota(jnp.int32, (group, lanes), 1)
    col = lax.broadcasted_iota(jnp.int32, (group, rows), 1)

    def slab(ref, r):
        return ref[0, pl.ds(r, group, stride=rows), :]

    vw = vw_ref[0]
    ve = ve_ref[0]
    cw = cw_ref[0]
    ce = ce_ref[0]
    left = jnp.zeros((group, rows), jnp.float32)
    right = jnp.zeros((group, rows), jnp.float32)
    x_up, c_up = vn_ref[0], cn_ref[0]
    x_mid, c_mid = slab(v_ref, 0), slab(c_ref, 0)
    for r in range(rows):
        if r + 1 < rows:
            x_dn, c_dn = slab(v_ref, r + 1), slab(c_ref, r + 1)
        else:
            x_dn, c_dn = vs_ref[0], cs_ref[0]
        x_w = jnp.where(lane == 0, vw[:, r : r + 1], pltpu.roll(x_mid, 1, 1))
        x_e = jnp.where(lane == lanes - 1, ve[:, r : r + 1], pltpu.roll(x_mid, lanes - 1, 1))
        c_w = jnp.where(lane == 0, cw[:, r : r + 1], pltpu.roll(c_mid, 1, 1))
        c_e = jnp.where(lane == lanes - 1, ce[:, r : r + 1], pltpu.roll(c_mid, lanes - 1, 1))
        total = jnp.minimum(c_mid, c_up) * (x_up - x_mid)
        total = total + jnp.minimum(c_mid, c_dn) * (x_dn - x_mid)
        total = total + jnp.minimum(c_mid, c_w) * (x_w - x_mid)
        total = total + jnp.minimum(c_mid, c_e) * (x_e - x_mid)
        out = x_mid + total
        w_ref[0, pl.ds(r, group, stride=rows), :] = out
        if r == 0:
            top_ref[0] = out
        if r == rows - 1:
            bot_ref[0] = out
        left = jnp.where(col == r, out[:, 0:1], left)
        right = jnp.where(col == r, out[:, lanes - 1 : lanes], right)
        x_up, c_up = x_mid, c_mid
        x_mid, c_mid = x_dn, c_dn
    left_ref[0] = left
    right_ref[0] = right


def sweep(field, conduct, field_halos, coef_halos):
    steps, span, lanes = field.shape
    rows = span // GROUP
    big = pl.BlockSpec((1, span, lanes), lambda i: (i, 0, 0))
    row_edge = pl.BlockSpec((1, GROUP, lanes), lambda i: (i, 0, 0))
    col_edge = pl.BlockSpec((1, GROUP, rows), lambda i: (i, 0, 0))
    edge_specs = [row_edge, row_edge, col_edge, col_edge]
    return pl.pallas_call(
        functools.partial(sweep_kernel, rows),
        grid=(steps,),
        in_specs=[big, big] + edge_specs + edge_specs,
        out_specs=[big] + edge_specs,
        out_shape=[
            jax.ShapeDtypeStruct(field.shape, jnp.float32),
            jax.ShapeDtypeStruct((steps, GROUP, lanes), jnp.float32),
            jax.ShapeDtypeStruct((steps, GROUP, lanes), jnp.float32),
            jax.ShapeDtypeStruct((steps, GROUP, rows), jnp.float32),
            jax.ShapeDtypeStruct((steps, GROUP, rows), jnp.float32),
        ],
        cost_estimate=pl.CostEstimate(
            flops=20 * field.size, bytes_accessed=12 * field.size, transcendentals=0
        ),
    )(field, conduct, *field_halos, *coef_halos)


def edges_of(field):
    vals, rows, lanes = field.shape
    steps = vals // GROUP
    top = field[:, 0, :].reshape(steps, GROUP, lanes)
    bottom = field[:, rows - 1, :].reshape(steps, GROUP, lanes)
    left = field[:, :, 0].reshape(steps, GROUP, rows)
    right = field[:, :, lanes - 1].reshape(steps, GROUP, rows)
    return top, bottom, left, right


def diffuse(field, conduct_blocks, coef_halos):
    vals, rows, lanes = field.shape
    steps = vals // GROUP
    edges = edges_of(field)
    current = field.reshape(steps, GROUP * rows, lanes)
    for _ in range(SWEEPS):
        current, *edges = sweep(current, conduct_blocks, halos(*edges), coef_halos)
    return current.reshape(vals, rows, lanes)


def select_kernel(index_ref, rows_ref, out_ref):
    cells = rows_ref.shape[0]

    def body(q, carry):
        source = index_ref[q]
        row = rows_ref[pl.ds(jnp.minimum(source, cells - 1), 1), :]
        out_ref[pl.ds(q, 1), :] = jnp.where(source < cells, row, 0.0)
        return carry

    lax.fori_loop(0, out_ref.shape[0], body, 0, unroll=8)


def place_kernel(index_ref, rows_ref, out_ref):
    cells = out_ref.shape[0]
    out_ref[...] = jnp.zeros_like(out_ref)

    def body(q, carry):
        target = index_ref[q]
        spot = pl.ds(jnp.minimum(target, cells - 1), 1)
        row = rows_ref[pl.ds(q, 1), :]
        out_ref[spot, :] = out_ref[spot, :] + jnp.where(target < cells, row, 0.0)
        return carry

    lax.fori_loop(0, rows_ref.shape[0], body, 0, unroll=8)


def interp_kernel(slot_ref, weight_ref, received_ref, precision_ref, equiv_ref, returned_ref):
    taps, obs_count = slot_ref.shape
    returned_ref[...] = jnp.zeros_like(returned_ref)

    def body(j, carry):
        slots = [slot_ref[k, j] for k in range(taps)]
        weights = [weight_ref[k, j] for k in range(taps)]
        total = received_ref[pl.ds(slots[0], 1), :] * weights[0]
        for k in range(1, taps):
            total = total + received_ref[pl.ds(slots[k], 1), :] * weights[k]
        equiv_ref[pl.ds(j, 1), :] = total
        weighted = precision_ref[pl.ds(j, 1), :] * total
        for k in range(taps):
            spot = pl.ds(slots[k], 1)
            returned_ref[spot, :] = returned_ref[spot, :] + weighted * weights[k]
        return carry

    lax.fori_loop(0, obs_count, body, 0, unroll=4)


SMEM = pl.BlockSpec(memory_space=pltpu.SMEM)
VMEM = pl.BlockSpec(memory_space=pltpu.VMEM)


def select_rows(index, rows, count):
    return pl.pallas_call(
        select_kernel,
        in_specs=[SMEM, VMEM],
        out_specs=VMEM,
        out_shape=jax.ShapeDtypeStruct((count, rows.shape[1]), jnp.float32),
    )(index, rows)


def place_rows(index, rows, cells):
    return pl.pallas_call(
        place_kernel,
        in_specs=[SMEM, VMEM],
        out_specs=VMEM,
        out_shape=jax.ShapeDtypeStruct((cells, rows.shape[1]), jnp.float32),
    )(index, rows)


def interpolate(obs_slots, obs_weights, received, precision_rows):
    obs_count = obs_slots.shape[1]
    return pl.pallas_call(
        interp_kernel,
        in_specs=[SMEM, SMEM, VMEM, VMEM],
        out_specs=[VMEM, VMEM],
        out_shape=[
            jax.ShapeDtypeStruct((obs_count, received.shape[1]), jnp.float32),
            jax.ShapeDtypeStruct(received.shape, jnp.float32),
        ],
    )(obs_slots, obs_weights, received, precision_rows)


def to_owners(outgoing):
    return lax.all_to_all(outgoing, ("lon", "lat"), split_axis=0, concat_axis=0, tiled=True)


def to_sources(returned):
    return lax.all_to_all(returned, ("lon", "lat"), split_axis=0, concat_axis=0, tiled=True)


def on_device(state, diffusivity, sea_mask, send_cols, obs_slots, obs_weights, obs_precision):
    vals, rows, lanes = state.shape
    cell_count = rows * lanes
    steps = vals // GROUP
    sea_float = sea_mask.astype(jnp.float32)
    conduct = diffusivity * jnp.concatenate([sea_float, sea_float], axis=0)
    coef_halos = halos(*edges_of(conduct))
    conduct_blocks = conduct.reshape(steps, GROUP * rows, lanes)
    smooth = diffuse(state, conduct_blocks, coef_halos)
    rows_of = smooth.reshape(vals, cell_count).T
    send_index = send_cols[0]
    outgoing = select_rows(send_index, rows_of, send_index.shape[0])
    received = to_owners(outgoing)
    equivalent_rows, returned = interpolate(obs_slots, obs_weights, received, obs_precision.T)
    equivalents = equivalent_rows.T
    incoming = to_sources(returned)
    adjoint_rows = place_rows(send_index, incoming, cell_count)
    adjoint_field = adjoint_rows.T.reshape(state.shape)
    product = state + diffuse(adjoint_field, conduct_blocks, coef_halos)
    return (product, equivalents)


def solution(mesh):
    placed = (
        P(None, "lat", "lon"),
        P(None, "lat", "lon"),
        P(None, "lat", "lon"),
        P(("lon", "lat"), None),
        P(None, ("lon", "lat")),
        P(None, ("lon", "lat")),
        P(None, ("lon", "lat")),
    )
    return jax.shard_map(
        on_device,
        mesh=mesh,
        in_specs=placed,
        out_specs=(P(None, "lat", "lon"), P(None, ("lon", "lat"))),
        check_vma=False,
    )
```

profile of v0, /device:TPU:8, one launch (start us, length us, event | category | flops | bytes accessed | tf_op | source)
XLA Modules:
  0.0 373.7 jit_solution(17354568680322727691)
XLA Ops:
  2.3 3.4 collective-permute-start
  5.8 3.5 collective-permute-start.1
  9.2 4.5 %slice_reduce_fusion.2 = (f32[150,32]{1,0:T(8,128)S(1)}, f32[150,32]{1,0:T(8,128)S(1)}) fusion(f32[150,32,128]{2,1,0:T(8,128)} %param.7), kind=kLoop, calls=%fused_computation.3 | loop fusion | bytes 76800 | tf_op jit(solution)/shard_map/slice | solution.py:116
  13.9 5.4 %collective-permute-start.3 = (f32[5,30,32]{2,1,0:T(8,128)S(1)}, f32[5,30,32]{2,1,0:T(8,128)}, u32[]{:S(2)}, u32[]{:S(2)}) collective-permute-start(f32[5,30,32]{2,1,0:T(8,128)S(1)} %reshape_squeeze.39), channel_id=1, source_target_pairs={{8,0},{16,8},{24,16},{32,24},{40,32},{48,40},{56,48},{64,56},{72,6... | collective-permute-start | bytes 57608 | tf_op jit(solution)/shard_map/ppermute | solution.py:29
  24.5 4.3 %collective-permute-start.5 = (f32[5,30,128]{2,1,0:T(8,128)S(1)}, f32[5,30,128]{2,1,0:T(8,128)S(1)}, u32[]{:S(2)}, u32[]{:S(2)}) collective-permute-start(f32[5,30,128]{2,1,0:T(8,128)S(1)} %reshape_squeeze.41), channel_id=1, source_target_pairs={{1,0},{2,1},{3,2},{4,3},{5,4},{6,5},{7,6},{9,8},{10,9},{11,10},{12... | collective-permute-start | bytes 230408 | tf_op jit(solution)/shard_map/ppermute | solution.py:20
  30.9 7.5 %collective-permute-done.6.cw_ref = f32[5,30,32]{2,1,0:T(8,128)S(1)} collective-permute-done((f32[5,30,32]{2,1,0:T(8,128)S(1)}, f32[5,30,32]{2,1,0:T(8,128)S(1)}, u32[]{:S(2)}, u32[]{:S(2)}) %collective-permute-start.6) | collective-permute-done | bytes 19232 | tf_op jit(solution)/shard_map/ppermute | solution.py:29
  41.2 22.1 %shard_map.86 = (f32[5,960,128]{2,1,0:T(8,128)}, f32[5,30,128]{2,1,0:T(8,128)}, f32[5,30,128]{2,1,0:T(8,128)}, f32[5,30,32]{2,1,0:T(8,128)}, f32[5,30,32]{2,1,0:T(8,128)}) custom-call(f32[5,960,128]{2,1,0:T(8,128)} %bitcast.26, f32[5,960,128]{2,1,0:T(8,128)} %bitcast.22, f32[5,30,128]{2,1,0:T(8,128)} %copy-done.9, ...), custom_call_target="tpu_custom_call" | custom-call | flops 12288000 | bytes 7372800 | tf_op jit(solution)/shard_map/pallas_call | solution.py:93
  65.3 4.7 %collective-permute-start.9 = (f32[5,30,128]{2,1,0:T(8,128)}, f32[5,30,128]{2,1,0:T(8,128)S(1)}, u32[]{:S(2)}, u32[]{:S(2)}) collective-permute-start(f32[5,30,128]{2,1,0:T(8,128)} %get-tuple-element.18), channel_id=1, source_target_pairs={{1,0},{2,1},{3,2},{4,3},{5,4},{6,5},{7,6},{9,8},{10,9},{11,10},{12... | collective-permute-start | bytes 230408 | tf_op jit(solution)/shard_map/ppermute | solution.py:20
  70.1 5.3 %collective-permute-start.11 = (f32[5,30,32]{2,1,0:T(8,128)}, f32[5,30,32]{2,1,0:T(8,128)S(1)}, u32[]{:S(2)}, u32[]{:S(2)}) collective-permute-start(f32[5,30,32]{2,1,0:T(8,128)} %get-tuple-element.20), channel_id=1, source_target_pairs={{8,0},{16,8},{24,16},{32,24},{40,32},{48,40},{56,48},{64,56},{72,6... | collective-permute-start | bytes 57608 | tf_op jit(solution)/shard_map/ppermute | solution.py:29
  78.8 22.1 %shard_map.87 = (f32[5,960,128]{2,1,0:T(8,128)}, f32[5,30,128]{2,1,0:T(8,128)}, f32[5,30,128]{2,1,0:T(8,128)}, f32[5,30,32]{2,1,0:T(8,128)}, f32[5,30,32]{2,1,0:T(8,128)}) custom-call(f32[5,960,128]{2,1,0:T(8,128)} %get-tuple-element.16.v_ref, f32[5,960,128]{2,1,0:T(8,128)} %bitcast.23, f32[5,30,128]{2,1,0:T(8,128)} %copy-done.15, f32[5,30,128]{2,1,0:T(8,128)} %copy-done.17, ...), custom_call_target="tpu_custom_call" | custom-call | flops 12288000 | bytes 7372800 | tf_op jit(solution)/shard_map/pallas_call | solution.py:93
  106.6 18.8 %shard_map.88 = f32[3072,150]{1,0:T(8,128)} custom-call(s32[3072]{0:T(1024)} %bitcast.38, f32[4096,150]{1,0:T(8,128)} %bitcast.30), custom_call_target="tpu_custom_call" | custom-call | tf_op jit(solution)/shard_map/pallas_call | solution.py:182
  125.4 9.0 %all-to-all-start = ((f32[128,24,150]{2,1,0:T(8,128)}), f32[128,24,150]{2,1,0:T(8,128)S(1)}, u32[]{:S(2)}, u32[]{:S(2)}) async-start(f32[128,24,150]{2,1,0:T(8,128)} %bitcast.32), calls=%async_computation | async-start | bytes 6291456 | tf_op jit(solution)/shard_map/all_to_all | solution.py:213
  137.2 38.3 %all-to-all-done = f32[128,24,150]{2,1,0:T(8,128)S(1)} async-done(((f32[128,24,150]{2,1,0:T(8,128)}), f32[128,24,150]{2,1,0:T(8,128)S(1)}, u32[]{:S(2)}, u32[]{:S(2)}) %all-to-all-start) | async-done | bytes 1843232 | tf_op jit(solution)/shard_map/all_to_all | solution.py:213
  177.2 43.0 %shard_map.89 = (f32[2048,150]{1,0:T(8,128)}, f32[3072,150]{1,0:T(8,128)}) custom-call(s32[4,2048]{1,0:T(4,128)} %slot_ref.1, f32[4,2048]{1,0:T(4,128)} %weight_ref.1, f32[3072,150]{1,0:T(8,128)} %bitcast.31, f32[2048,150]{1,0:T(8,128)} %bitcast.34), custom_call_target="tpu_custom_call" | custom-call | tf_op jit(solution)/shard_map/pallas_call | solution.py:201
  220.2 47.0 %all_to_all.22 = f32[128,24,150]{2,1,0:T(8,128)} all-to-all(f32[128,24,150]{2,1,0:T(8,128)} %bitcast.35), channel_id=1, replica_groups=mesh['lon'=16,'lat'=8] {'lon','lat'}, dimensions={0} | all-to-all | bytes 3686400 | tf_op jit(solution)/shard_map/all_to_all | solution.py:217
  267.2 21.6 %shard_map.90 = f32[4096,150]{1,0:T(8,128)} custom-call(s32[3072]{0:T(1024)} %bitcast.39, f32[3072,150]{1,0:T(8,128)} %bitcast.33), custom_call_target="tpu_custom_call" | custom-call | tf_op jit(solution)/shard_map/pallas_call | solution.py:191
  292.7 4.1 %collective-permute-start.13 = (f32[5,30,128]{2,1,0:T(8,128)S(1)}, f32[5,30,128]{2,1,0:T(8,128)S(1)}, u32[]{:S(2)}, u32[]{:S(2)}) collective-permute-start(f32[5,30,128]{2,1,0:T(8,128)S(1)} %reshape_squeeze.45), channel_id=1, source_target_pairs={{1,0},{2,1},{3,2},{4,3},{5,4},{6,5},{7,6},{9,8},{10,9},{11,10},{12... | collective-permute-start | bytes 230408 | tf_op jit(solution)/shard_map/ppermute | solution.py:20
  298.2 5.3 %collective-permute-start.15 = (f32[5,30,32]{2,1,0:T(8,128)S(1)}, f32[5,30,32]{2,1,0:T(8,128)S(1)}, u32[]{:S(2)}, u32[]{:S(2)}) collective-permute-start(f32[5,30,32]{2,1,0:T(8,128)S(1)} %reshape_squeeze.47), channel_id=1, source_target_pairs={{8,0},{16,8},{24,16},{32,24},{40,32},{48,40},{56,48},{64,56},{72,6... | collective-permute-start | bytes 57608 | tf_op jit(solution)/shard_map/ppermute | solution.py:29
  303.6 3.7 copy.18
  310.4 22.0 %shard_map.91 = (f32[5,960,128]{2,1,0:T(8,128)}, f32[5,30,128]{2,1,0:T(8,128)}, f32[5,30,128]{2,1,0:T(8,128)}, f32[5,30,32]{2,1,0:T(8,128)}, f32[5,30,32]{2,1,0:T(8,128)}) custom-call(f32[5,960,128]{2,1,0:T(8,128)} %reshape_reshape.7.v_ref, f32[5,960,128]{2,1,0:T(8,128)} %bitcast.24, f32[5,30,128]{2,1,0:T(8,128)} %copy-done.10, f32[5,30,128]{2,1,0:T(8,128)} %copy-done.11, ...), custom_call_target="tpu_custom_call" | custom-call | flops 12288000 | bytes 7372800 | tf_op jit(solution)/shard_map/pallas_call | solution.py:93
  334.4 4.8 %collective-permute-start.17 = (f32[5,30,128]{2,1,0:T(8,128)}, f32[5,30,128]{2,1,0:T(8,128)S(1)}, u32[]{:S(2)}, u32[]{:S(2)}) collective-permute-start(f32[5,30,128]{2,1,0:T(8,128)} %get-tuple-element.25), channel_id=1, source_target_pairs={{1,0},{2,1},{3,2},{4,3},{5,4},{6,5},{7,6},{9,8},{10,9},{11,10},{12... | collective-permute-start | bytes 230408 | tf_op jit(solution)/shard_map/ppermute | solution.py:20
  339.3 5.3 %collective-permute-start.19 = (f32[5,30,32]{2,1,0:T(8,128)}, f32[5,30,32]{2,1,0:T(8,128)S(1)}, u32[]{:S(2)}, u32[]{:S(2)}) collective-permute-start(f32[5,30,32]{2,1,0:T(8,128)} %get-tuple-element.27), channel_id=1, source_target_pairs={{8,0},{16,8},{24,16},{32,24},{40,32},{48,40},{56,48},{64,56},{72,6... | collective-permute-start | bytes 57608 | tf_op jit(solution)/shard_map/ppermute | solution.py:29
  347.7 22.2 %shard_map.92 = (f32[5,960,128]{2,1,0:T(8,128)}, f32[5,30,128]{2,1,0:T(8,128)}, f32[5,30,128]{2,1,0:T(8,128)}, f32[5,30,32]{2,1,0:T(8,128)}, f32[5,30,32]{2,1,0:T(8,128)}) custom-call(f32[5,960,128]{2,1,0:T(8,128)} %get-tuple-element.23.v_ref, f32[5,960,128]{2,1,0:T(8,128)} %bitcast.25, f32[5,30,128]{2,1,0:T(8,128)} %copy-done.12, f32[5,30,128]{2,1,0:T(8,128)} %copy-done.13, ...), custom_call_target="tpu_custom_call" | custom-call | flops 12288000 | bytes 7372800 | tf_op jit(solution)/shard_map/pallas_call | solution.py:93
  370.0 3.7 add.3
  (101 shorter events, 40.8 us)
Async XLA Ops:
  2.3 38.1 %collective-permute-start = (f32[5,30,128]{2,1,0:T(8,128)S(1)}, f32[5,30,128]{2,1,0:T(8,128)S(1)}, u32[]{:S(2)}, u32[]{:S(2)}) collective-permute-start(f32[5,30,128]{2,1,0:T(8,128)S(1)} %reshape_squeeze.36), channel_id=1, source_target_pairs={{0,1},{1,2},{2,3},{3,4},{4,5},{5,6},{6,7},{8,9},{9,10},{10,11},{11... | collective-permute-start | bytes 230408 | tf_op jit(solution)/shard_map/ppermute | solution.py:20
  5.7 13.6 %copy-start.8 = (s32[75,32,128]{2,1,0:T(8,128)S(1)}, s32[75,32,128]{2,1,0:T(8,128)}, u32[]{:S(2)}) copy-start(s32[75,32,128]{2,1,0:T(8,128)} %param.9) | copy-start | bytes 3686404
  5.8 34.7 %collective-permute-start.1 = (f32[5,30,128]{2,1,0:T(8,128)S(1)}, f32[5,30,128]{2,1,0:T(8,128)}, u32[]{:S(2)}, u32[]{:S(2)}) collective-permute-start(f32[5,30,128]{2,1,0:T(8,128)S(1)} %reshape_squeeze.37), channel_id=1, source_target_pairs={{1,0},{2,1},{3,2},{4,3},{5,4},{6,5},{7,6},{9,8},{10,9},{11,10},{12... | collective-permute-start | bytes 230408 | tf_op jit(solution)/shard_map/ppermute | solution.py:20
  13.8 10.7 %collective-permute-start.2 = (f32[5,30,32]{2,1,0:T(8,128)S(1)}, f32[5,30,32]{2,1,0:T(8,128)}, u32[]{:S(2)}, u32[]{:S(2)}) collective-permute-start(f32[5,30,32]{2,1,0:T(8,128)S(1)} %reshape_squeeze.38), channel_id=1, source_target_pairs={{0,8},{8,16},{16,24},{24,32},{32,40},{40,48},{48,56},{56,64},{64,7... | collective-permute-start | bytes 57608 | tf_op jit(solution)/shard_map/ppermute | solution.py:29
  13.9 16.9 %collective-permute-start.3 = (f32[5,30,32]{2,1,0:T(8,128)S(1)}, f32[5,30,32]{2,1,0:T(8,128)}, u32[]{:S(2)}, u32[]{:S(2)}) collective-permute-start(f32[5,30,32]{2,1,0:T(8,128)S(1)} %reshape_squeeze.39), channel_id=1, source_target_pairs={{8,0},{16,8},{24,16},{32,24},{40,32},{48,40},{56,48},{64,56},{72,6... | collective-permute-start | bytes 57608 | tf_op jit(solution)/shard_map/ppermute | solution.py:29
  22.0 18.4 %collective-permute-start.4 = (f32[5,30,128]{2,1,0:T(8,128)S(1)}, f32[5,30,128]{2,1,0:T(8,128)S(1)}, u32[]{:S(2)}, u32[]{:S(2)}) collective-permute-start(f32[5,30,128]{2,1,0:T(8,128)S(1)} %reshape_squeeze.40), channel_id=1, source_target_pairs={{0,1},{1,2},{2,3},{3,4},{4,5},{5,6},{6,7},{8,9},{9,10},{10,11},{11... | collective-permute-start | bytes 230408 | tf_op jit(solution)/shard_map/ppermute | solution.py:20
  24.5 16.0 %collective-permute-start.5 = (f32[5,30,128]{2,1,0:T(8,128)S(1)}, f32[5,30,128]{2,1,0:T(8,128)S(1)}, u32[]{:S(2)}, u32[]{:S(2)}) collective-permute-start(f32[5,30,128]{2,1,0:T(8,128)S(1)} %reshape_squeeze.41), channel_id=1, source_target_pairs={{1,0},{2,1},{3,2},{4,3},{5,4},{6,5},{7,6},{9,8},{10,9},{11,10},{12... | collective-permute-start | bytes 230408 | tf_op jit(solution)/shard_map/ppermute | solution.py:20
  30.8 7.5 %collective-permute-start.6 = (f32[5,30,32]{2,1,0:T(8,128)S(1)}, f32[5,30,32]{2,1,0:T(8,128)S(1)}, u32[]{:S(2)}, u32[]{:S(2)}) collective-permute-start(f32[5,30,32]{2,1,0:T(8,128)S(1)} %reshape_squeeze.42), channel_id=1, source_target_pairs={{0,8},{8,16},{16,24},{24,32},{32,40},{40,48},{48,56},{56,64},{64,7... | collective-permute-start | bytes 57608 | tf_op jit(solution)/shard_map/ppermute | solution.py:29
  38.4 2.1 collective-permute-start.7
  63.2 14.8 %collective-permute-start.8 = (f32[5,30,128]{2,1,0:T(8,128)}, f32[5,30,128]{2,1,0:T(8,128)S(1)}, u32[]{:S(2)}, u32[]{:S(2)}) collective-permute-start(f32[5,30,128]{2,1,0:T(8,128)} %get-tuple-element.17), channel_id=1, source_target_pairs={{0,1},{1,2},{2,3},{3,4},{4,5},{5,6},{6,7},{8,9},{9,10},{10,11},{11... | collective-permute-start | bytes 230408 | tf_op jit(solution)/shard_map/ppermute | solution.py:20
  65.3 12.8 %collective-permute-start.9 = (f32[5,30,128]{2,1,0:T(8,128)}, f32[5,30,128]{2,1,0:T(8,128)S(1)}, u32[]{:S(2)}, u32[]{:S(2)}) collective-permute-start(f32[5,30,128]{2,1,0:T(8,128)} %get-tuple-element.18), channel_id=1, source_target_pairs={{1,0},{2,1},{3,2},{4,3},{5,4},{6,5},{7,6},{9,8},{10,9},{11,10},{12... | collective-permute-start | bytes 230408 | tf_op jit(solution)/shard_map/ppermute | solution.py:20
  70.0 8.0 %collective-permute-start.10 = (f32[5,30,32]{2,1,0:T(8,128)}, f32[5,30,32]{2,1,0:T(8,128)S(1)}, u32[]{:S(2)}, u32[]{:S(2)}) collective-permute-start(f32[5,30,32]{2,1,0:T(8,128)} %get-tuple-element.19), channel_id=1, source_target_pairs={{0,8},{8,16},{16,24},{24,32},{32,40},{40,48},{48,56},{56,64},{64,7... | collective-permute-start | bytes 57608 | tf_op jit(solution)/shard_map/ppermute | solution.py:29
  70.1 8.0 %collective-permute-start.11 = (f32[5,30,32]{2,1,0:T(8,128)}, f32[5,30,32]{2,1,0:T(8,128)S(1)}, u32[]{:S(2)}, u32[]{:S(2)}) collective-permute-start(f32[5,30,32]{2,1,0:T(8,128)} %get-tuple-element.20), channel_id=1, source_target_pairs={{8,0},{16,8},{24,16},{32,24},{40,32},{48,40},{56,48},{64,56},{72,6... | collective-permute-start | bytes 57608 | tf_op jit(solution)/shard_map/ppermute | solution.py:29
  125.4 50.1 %all-to-all-start = ((f32[128,24,150]{2,1,0:T(8,128)}), f32[128,24,150]{2,1,0:T(8,128)S(1)}, u32[]{:S(2)}, u32[]{:S(2)}) async-start(f32[128,24,150]{2,1,0:T(8,128)} %bitcast.32), calls=%async_computation | async-start | bytes 6291456 | tf_op jit(solution)/shard_map/all_to_all | solution.py:213
  290.1 19.0 %collective-permute-start.12 = (f32[5,30,128]{2,1,0:T(8,128)S(1)}, f32[5,30,128]{2,1,0:T(8,128)S(1)}, u32[]{:S(2)}, u32[]{:S(2)}) collective-permute-start(f32[5,30,128]{2,1,0:T(8,128)S(1)} %reshape_squeeze.44), channel_id=1, source_target_pairs={{0,1},{1,2},{2,3},{3,4},{4,5},{5,6},{6,7},{8,9},{9,10},{10,11},{11... | collective-permute-start | bytes 230408 | tf_op jit(solution)/shard_map/ppermute | solution.py:20
  292.7 16.4 %collective-permute-start.13 = (f32[5,30,128]{2,1,0:T(8,128)S(1)}, f32[5,30,128]{2,1,0:T(8,128)S(1)}, u32[]{:S(2)}, u32[]{:S(2)}) collective-permute-start(f32[5,30,128]{2,1,0:T(8,128)S(1)} %reshape_squeeze.45), channel_id=1, source_target_pairs={{1,0},{2,1},{3,2},{4,3},{5,4},{6,5},{7,6},{9,8},{10,9},{11,10},{12... | collective-permute-start | bytes 230408 | tf_op jit(solution)/shard_map/ppermute | solution.py:20
  298.1 11.0 %collective-permute-start.14 = (f32[5,30,32]{2,1,0:T(8,128)S(1)}, f32[5,30,32]{2,1,0:T(8,128)S(1)}, u32[]{:S(2)}, u32[]{:S(2)}) collective-permute-start(f32[5,30,32]{2,1,0:T(8,128)S(1)} %reshape_squeeze.46), channel_id=1, source_target_pairs={{0,8},{8,16},{16,24},{24,32},{32,40},{40,48},{48,56},{56,64},{64,7... | collective-permute-start | bytes 57608 | tf_op jit(solution)/shard_map/ppermute | solution.py:29
  298.2 10.9 %collective-permute-start.15 = (f32[5,30,32]{2,1,0:T(8,128)S(1)}, f32[5,30,32]{2,1,0:T(8,128)S(1)}, u32[]{:S(2)}, u32[]{:S(2)}) collective-permute-start(f32[5,30,32]{2,1,0:T(8,128)S(1)} %reshape_squeeze.47), channel_id=1, source_target_pairs={{8,0},{16,8},{24,16},{32,24},{40,32},{48,40},{56,48},{64,56},{72,6... | collective-permute-start | bytes 57608 | tf_op jit(solution)/shard_map/ppermute | solution.py:29
  309.1 35.6 %copy-start.3 = (f32[2048,150]{1,0:T(8,128)S(1)}, f32[2048,150]{1,0:T(8,128)}, u32[]{:S(2)}) copy-start(f32[2048,150]{1,0:T(8,128)} %get-tuple-element.29) | copy-start | bytes 3686404
  332.4 14.6 %collective-permute-start.16 = (f32[5,30,128]{2,1,0:T(8,128)}, f32[5,30,128]{2,1,0:T(8,128)S(1)}, u32[]{:S(2)}, u32[]{:S(2)}) collective-permute-start(f32[5,30,128]{2,1,0:T(8,128)} %get-tuple-element.24), channel_id=1, source_target_pairs={{0,1},{1,2},{2,3},{3,4},{4,5},{5,6},{6,7},{8,9},{9,10},{10,11},{11... | collective-permute-start | bytes 230408 | tf_op jit(solution)/shard_map/ppermute | solution.py:20
  334.4 12.6 %collective-permute-start.17 = (f32[5,30,128]{2,1,0:T(8,128)}, f32[5,30,128]{2,1,0:T(8,128)S(1)}, u32[]{:S(2)}, u32[]{:S(2)}) collective-permute-start(f32[5,30,128]{2,1,0:T(8,128)} %get-tuple-element.25), channel_id=1, source_target_pairs={{1,0},{2,1},{3,2},{4,3},{5,4},{6,5},{7,6},{9,8},{10,9},{11,10},{12... | collective-permute-start | bytes 230408 | tf_op jit(solution)/shard_map/ppermute | solution.py:20
  339.2 7.8 %collective-permute-start.18 = (f32[5,30,32]{2,1,0:T(8,128)}, f32[5,30,32]{2,1,0:T(8,128)S(1)}, u32[]{:S(2)}, u32[]{:S(2)}) collective-permute-start(f32[5,30,32]{2,1,0:T(8,128)} %get-tuple-element.26), channel_id=1, source_target_pairs={{0,8},{8,16},{16,24},{24,32},{32,40},{40,48},{48,56},{56,64},{64,7... | collective-permute-start | bytes 57608 | tf_op jit(solution)/shard_map/ppermute | solution.py:29
  339.3 7.7 %collective-permute-start.19 = (f32[5,30,32]{2,1,0:T(8,128)}, f32[5,30,32]{2,1,0:T(8,128)S(1)}, u32[]{:S(2)}, u32[]{:S(2)}) collective-permute-start(f32[5,30,32]{2,1,0:T(8,128)} %get-tuple-element.27), channel_id=1, source_target_pairs={{8,0},{16,8},{24,16},{32,24},{40,32},{48,40},{56,48},{64,56},{72,6... | collective-permute-start | bytes 57608 | tf_op jit(solution)/shard_map/ppermute | solution.py:29
  347.7 22.2 %copy-start.1 = (f32[150,32,128]{2,1,0:T(8,128)S(1)}, f32[150,32,128]{2,1,0:T(8,128)}, u32[]{:S(2)}) copy-start(f32[150,32,128]{2,1,0:T(8,128)} %param.7) | copy-start | bytes 7372804
  (19 other events, 23.5 us)
where the time goes:
time: 375 us; the launch traced here: 374 us
  Pallas kernels  172 us (46%)
  starting transfers between devices  64.7 us (17%)
  waiting for transfers between devices  51.2 us (14%)
  blocking collectives  47 us (13%)
  local copies, waits for them, and re-layouts  31.8 us (8%)
  other arithmetic  5.95 us (2%)
    pallas_call x4, Pallas kernels, sweep(): pl.pallas_call(functools.partial(sweep_kernel, rows), grid=(steps,), in_s...  88.4 us
    all_to_all x1, blocking collectives, to_sources(): lax.all_to_all(returned, ('lon', 'lat'), split_axis=0, concat_axis=0, til...  47 us
    pallas_call x1, Pallas kernels, interpolate(): pl.pallas_call(interp_kernel, in_specs=[SMEM, SMEM, VMEM, VMEM], out_spec...  43 us
    all_to_all x1, waiting for transfers between devices, to_owners(): lax.all_to_all(outgoing, ('lon', 'lat'), split_axis=0, concat_axis=0, til...  38.3 us
    ppermute x10, starting transfers between devices, shift_lat(): return lax.ppermute(edge, 'lat', pairs)  33.8 us
    ppermute x10, starting transfers between devices, shift_lon(): return lax.ppermute(edge, 'lon', pairs)  21.9 us
    pallas_call x1, Pallas kernels, place_rows(): pl.pallas_call(place_kernel, in_specs=[SMEM, VMEM], out_specs=VMEM, out_s...  21.6 us
    pallas_call x1, Pallas kernels, select_rows(): pl.pallas_call(select_kernel, in_specs=[SMEM, VMEM], out_specs=VMEM, out_...  18.8 us
  transfers between devices with their start and end apart: 21, of which 5 were waited for; matrix products, arithmetic and copies ran while one was open for 5% of the time, Pallas kernels for 0%

commit v1 on v0

v1 whole, which is shorter than its diff:
```python
import functools

import jax
import jax.numpy as jnp
from jax import lax
from jax.experimental import pallas as pl
from jax.experimental.pallas import tpu as pltpu
from jax.sharding import PartitionSpec as P

SWEEPS = 2
GROUP = 30
SMEM = pl.BlockSpec(memory_space=pltpu.SMEM)
VMEM = pl.BlockSpec(memory_space=pltpu.VMEM)


def slab_pass(rows, src_ref, conduct_ref, field_halo, coef_halo, scales, dst_ref, edges):
    groups, span, lanes = src_ref.shape
    group = span // rows
    north_ok, south_ok = scales
    row_halo, col_halo = field_halo
    coef_rows, coef_cols = coef_halo

    def body(g, carry):
        lane = lax.broadcasted_iota(jnp.int32, (group, lanes), 1)
        col = lax.broadcasted_iota(jnp.int32, (group, rows), 1)

        def slab(ref, r):
            return ref[g, pl.ds(r, group, stride=rows), :]

        vw = col_halo[0, g]
        ve = col_halo[1, g]
        cw = coef_cols[0, g]
        ce = coef_cols[1, g]
        left = jnp.zeros((group, rows), jnp.float32)
        right = jnp.zeros((group, rows), jnp.float32)
        x_up = row_halo[0, g] * north_ok
        c_up = coef_rows[0, g] * north_ok
        x_mid, c_mid = slab(src_ref, 0), slab(conduct_ref, 0)
        for r in range(rows):
            if r + 1 < rows:
                x_dn, c_dn = slab(src_ref, r + 1), slab(conduct_ref, r + 1)
            else:
                x_dn = row_halo[1, g] * south_ok
                c_dn = coef_rows[1, g] * south_ok
            x_w = jnp.where(lane == 0, vw[:, r : r + 1], pltpu.roll(x_mid, 1, 1))
            x_e = jnp.where(lane == lanes - 1, ve[:, r : r + 1], pltpu.roll(x_mid, lanes - 1, 1))
            c_w = jnp.where(lane == 0, cw[:, r : r + 1], pltpu.roll(c_mid, 1, 1))
            c_e = jnp.where(lane == lanes - 1, ce[:, r : r + 1], pltpu.roll(c_mid, lanes - 1, 1))
            total = jnp.minimum(c_mid, c_up) * (x_up - x_mid)
            total = total + jnp.minimum(c_mid, c_dn) * (x_dn - x_mid)
            total = total + jnp.minimum(c_mid, c_w) * (x_w - x_mid)
            total = total + jnp.minimum(c_mid, c_e) * (x_e - x_mid)
            out = x_mid + total
            dst_ref[g, pl.ds(r, group, stride=rows), :] = out
            if edges is not None:
                if r == 0:
                    edges[0][0, g] = out
                if r == rows - 1:
                    edges[0][1, g] = out
                left = jnp.where(col == r, out[:, 0:1], left)
                right = jnp.where(col == r, out[:, lanes - 1 : lanes], right)
            x_up, c_up = x_mid, c_mid
            x_mid, c_mid = x_dn, c_dn
        if edges is not None:
            edges[1][0, g] = left
            edges[1][1, g] = right
        return carry

    lax.fori_loop(0, groups, body, 0)


def edge_pass(rows, src_ref, row_out, col_out):
    groups, span, lanes = src_ref.shape
    group = span // rows

    def body(g, carry):
        col = lax.broadcasted_iota(jnp.int32, (group, rows), 1)
        left = jnp.zeros((group, rows), jnp.float32)
        right = jnp.zeros((group, rows), jnp.float32)
        for r in range(rows):
            x = src_ref[g, pl.ds(r, group, stride=rows), :]
            if r == 0:
                row_out[0, g] = x
            if r == rows - 1:
                row_out[1, g] = x
            left = jnp.where(col == r, x[:, 0:1], left)
            right = jnp.where(col == r, x[:, lanes - 1 : lanes], right)
        col_out[0, g] = left
        col_out[1, g] = right
        return carry

    lax.fori_loop(0, groups, body, 0)


def diffuse_kernel(rows, v_ref, c_ref, out_ref, mid_ref, row_edge, col_edge, row_halo, col_halo,
                   send_sem, recv_sem):
    lon = lax.axis_index("lon")
    lat = lax.axis_index("lat")
    n_lon = lax.axis_size("lon")
    n_lat = lax.axis_size("lat")
    north = {"lat": (lat + n_lat - 1) % n_lat}
    south = {"lat": (lat + 1) % n_lat}
    west = {"lon": (lon + n_lon - 1) % n_lon}
    east = {"lon": (lon + 1) % n_lon}
    mesh_id = pl.DeviceIdType.MESH

    barrier = pltpu.get_barrier_semaphore()
    for peer in (north, south, west, east):
        pl.semaphore_signal(barrier, inc=1, device_id=peer, device_id_type=mesh_id)
    pl.semaphore_wait(barrier, 4)

    def exchange(rd):
        plan = [
            (row_edge.at[rd, 0], row_halo.at[rd, 1], north, 0),
            (row_edge.at[rd, 1], row_halo.at[rd, 0], south, 1),
            (col_edge.at[rd, 0], col_halo.at[rd, 1], west, 2),
            (col_edge.at[rd, 1], col_halo.at[rd, 0], east, 3),
        ]
        copies = []
        for src, dst, peer, k in plan:
            copy = pltpu.make_async_remote_copy(
                src_ref=src, dst_ref=dst, send_sem=send_sem.at[rd, k], recv_sem=recv_sem.at[rd, k],
                device_id=peer, device_id_type=mesh_id,
            )
            copy.start()
            copies.append(copy)
        return copies

    edge_pass(rows, c_ref, row_edge.at[0], col_edge.at[0])
    edge_pass(rows, v_ref, row_edge.at[1], col_edge.at[1])
    first = exchange(0) + exchange(1)
    for copy in first:
        copy.wait()
    north_ok = jnp.minimum(lat, 1).astype(jnp.float32)
    south_ok = jnp.minimum(n_lat - 1 - lat, 1).astype(jnp.float32)
    scales = (north_ok, south_ok)
    coef_halo = (row_halo.at[0], col_halo.at[0])
    slab_pass(rows, v_ref, c_ref, (row_halo.at[1], col_halo.at[1]), coef_halo, scales, mid_ref,
              (row_edge.at[2], col_edge.at[2]))
    for copy in exchange(2):
        copy.wait()
    slab_pass(rows, mid_ref, c_ref, (row_halo.at[2], col_halo.at[2]), coef_halo, scales, out_ref, None)


def diffuse(field, conduct_blocks):
    vals, rows, lanes = field.shape
    groups = vals // GROUP
    blocks = field.reshape(groups, GROUP * rows, lanes)
    rounds = SWEEPS + 1
    out = pl.pallas_call(
        functools.partial(diffuse_kernel, rows),
        in_specs=[VMEM, VMEM],
        out_specs=VMEM,
        out_shape=jax.ShapeDtypeStruct(blocks.shape, jnp.float32),
        scratch_shapes=[
            pltpu.VMEM(blocks.shape, jnp.float32),
            pltpu.VMEM((rounds, 2, groups, GROUP, lanes), jnp.float32),
            pltpu.VMEM((rounds, 2, groups, GROUP, rows), jnp.float32),
            pltpu.VMEM((rounds, 2, groups, GROUP, lanes), jnp.float32),
            pltpu.VMEM((rounds, 2, groups, GROUP, rows), jnp.float32),
            pltpu.SemaphoreType.DMA((rounds, 4)),
            pltpu.SemaphoreType.DMA((rounds, 4)),
        ],
        compiler_params=pltpu.CompilerParams(collective_id=0, has_side_effects=True),
        cost_estimate=pl.CostEstimate(
            flops=50 * field.size, bytes_accessed=12 * field.size, transcendentals=0
        ),
    )(blocks, conduct_blocks)
    return out.reshape(vals, rows, lanes)


def select_kernel(index_ref, rows_ref, out_ref):
    cells = rows_ref.shape[0]

    def body(q, carry):
        source = index_ref[q]
        row = rows_ref[pl.ds(jnp.minimum(source, cells - 1), 1), :]
        out_ref[pl.ds(q, 1), :] = jnp.where(source < cells, row, 0.0)
        return carry

    lax.fori_loop(0, out_ref.shape[0], body, 0, unroll=8)


def place_kernel(index_ref, rows_ref, out_ref):
    cells = out_ref.shape[0]
    out_ref[...] = jnp.zeros_like(out_ref)

    def body(q, carry):
        target = index_ref[q]
        spot = pl.ds(jnp.minimum(target, cells - 1), 1)
        row = rows_ref[pl.ds(q, 1), :]
        out_ref[spot, :] = out_ref[spot, :] + jnp.where(target < cells, row, 0.0)
        return carry

    lax.fori_loop(0, rows_ref.shape[0], body, 0, unroll=8)


def interp_kernel(slot_ref, weight_ref, received_ref, precision_ref, equiv_ref, returned_ref):
    taps, obs_count = slot_ref.shape
    returned_ref[...] = jnp.zeros_like(returned_ref)

    def body(j, carry):
        slots = [slot_ref[k, j] for k in range(taps)]
        weights = [weight_ref[k, j] for k in range(taps)]
        total = received_ref[pl.ds(slots[0], 1), :] * weights[0]
        for k in range(1, taps):
            total = total + received_ref[pl.ds(slots[k], 1), :] * weights[k]
        equiv_ref[pl.ds(j, 1), :] = total
        weighted = precision_ref[pl.ds(j, 1), :] * total
        for k in range(taps):
            spot = pl.ds(slots[k], 1)
            returned_ref[spot, :] = returned_ref[spot, :] + weighted * weights[k]
        return carry

    lax.fori_loop(0, obs_count, body, 0, unroll=4)


def select_rows(index, rows, count):
    return pl.pallas_call(
        select_kernel,
        in_specs=[SMEM, VMEM],
        out_specs=VMEM,
        out_shape=jax.ShapeDtypeStruct((count, rows.shape[1]), jnp.float32),
    )(index, rows)


def place_rows(index, rows, cells):
    return pl.pallas_call(
        place_kernel,
        in_specs=[SMEM, VMEM],
        out_specs=VMEM,
        out_shape=jax.ShapeDtypeStruct((cells, rows.shape[1]), jnp.float32),
    )(index, rows)


def interpolate(obs_slots, obs_weights, received, precision_rows):
    obs_count = obs_slots.shape[1]
    return pl.pallas_call(
        interp_kernel,
        in_specs=[SMEM, SMEM, VMEM, VMEM],
        out_specs=[VMEM, VMEM],
        out_shape=[
            jax.ShapeDtypeStruct((obs_count, received.shape[1]), jnp.float32),
            jax.ShapeDtypeStruct(received.shape, jnp.float32),
        ],
    )(obs_slots, obs_weights, received, precision_rows)


def to_owners(outgoing):
    return lax.all_to_all(outgoing, ("lon", "lat"), split_axis=0, concat_axis=0, tiled=True)


def to_sources(returned):
    return lax.all_to_all(returned, ("lon", "lat"), split_axis=0, concat_axis=0, tiled=True)


def on_device(state, diffusivity, sea_mask, send_cols, obs_slots, obs_weights, obs_precision):
    vals, rows, lanes = state.shape
    cell_count = rows * lanes
    steps = vals // GROUP
    sea_float = sea_mask.astype(jnp.float32)
    conduct = diffusivity * jnp.concatenate([sea_float, sea_float], axis=0)
    conduct_blocks = conduct.reshape(steps, GROUP * rows, lanes)
    smooth = diffuse(state, conduct_blocks)
    rows_of = smooth.reshape(vals, cell_count).T
    send_index = send_cols[0]
    outgoing = select_rows(send_index, rows_of, send_index.shape[0])
    received = to_owners(outgoing)
    equivalent_rows, returned = interpolate(obs_slots, obs_weights, received, obs_precision.T)
    equivalents = equivalent_rows.T
    incoming = to_sources(returned)
    adjoint_rows = place_rows(send_index, incoming, cell_count)
    adjoint_field = adjoint_rows.T.reshape(state.shape)
    product = state + diffuse(adjoint_field, conduct_blocks)
    return (product, equivalents)


def solution(mesh):
    placed = (
        P(None, "lat", "lon"),
        P(None, "lat", "lon"),
        P(None, "lat", "lon"),
        P(("lon", "lat"), None),
        P(None, ("lon", "lat")),
        P(None, ("lon", "lat")),
        P(None, ("lon", "lat")),
    )
    return jax.shard_map(
        on_device,
        mesh=mesh,
        in_specs=placed,
        out_specs=(P(None, "lat", "lon"), P(None, ("lon", "lat"))),
        check_vma=False,
    )
```

time: 375 us -> 316 us (0.84)
  starting transfers between devices: 64.7 us -> 11.5 us
  blocking collectives: 47 us -> 0 us
  waiting for transfers between devices: 51.2 us -> 76.7 us
  Pallas kernels: 172 us -> 197 us
  local copies, waits for them, and re-layouts: 31.8 us -> 20.8 us
    ppermute x20 -> x0, starting transfers between devices: 55.7 us -> none  [the longest x10 33.8 us: shift_lat(): return lax.ppermute(edge, 'lat', pairs)]
    all_to_all x1 -> x0, blocking collectives: 47 us -> none  [to_sources(): lax.all_to_all(returned, ('lon', 'lat'), split_axis=0, concat_axis=0, til...]
    all_to_all x0 -> x1, waiting for transfers between devices: none -> 38.4 us  [to_sources(): lax.all_to_all(returned, ('lon', 'lat'), split_axis=0, concat_axis=0, til...]
    pallas_call x4 -> x2, Pallas kernels: 88.4 us -> 113 us  [diffuse(): pl.pallas_call(functools.partial(diffuse_kernel, rows), in_specs=[VMEM, V...]
    ppermute x20 -> x0, waiting for transfers between devices: 12.9 us -> none  [the longest x10 12.9 us: shift_lon(): return lax.ppermute(edge, 'lon', pairs)]
    slice x6 -> x0, local copies, waits for them, and re-layouts: 10.6 us -> none  [the longest x3 7.6 us: edges_of(): left = field[:, :, 0].reshape(steps, GROUP, rows)]
    all_to_all x0 -> x1, starting transfers between devices: none -> 4.93 us  [to_sources(): lax.all_to_all(returned, ('lon', 'lat'), split_axis=0, concat_axis=0, til...]
    unnamed x50 -> x10, local copies, waits for them, and re-layouts: 9.74 us -> 9.31 us
  transfers between devices with their start and end apart: 21 -> 2, of which waited for: 5 -> 2; matrix products, arithmetic and copies ran while one was open for 5% -> 2% of each run, Pallas kernels for 0% -> 0%
where the time goes in v1:
time: 316 us; the launch traced here: 313 us
  Pallas kernels  197 us (62%)
  waiting for transfers between devices  76.7 us (24%)
  local copies, waits for them, and re-layouts  20.8 us (7%)
  starting transfers between devices  11.5 us (4%)
  other arithmetic  7.13 us (2%)
    pallas_call x2, Pallas kernels, diffuse(): pl.pallas_call(functools.partial(diffuse_kernel, rows), in_specs=[VMEM, V...  113 us
    pallas_call x1, Pallas kernels, interpolate(): pl.pallas_call(interp_kernel, in_specs=[SMEM, SMEM, VMEM, VMEM], out_spec...  43.1 us
    all_to_all x1, waiting for transfers between devices, to_sources(): lax.all_to_all(returned, ('lon', 'lat'), split_axis=0, concat_axis=0, til...  38.4 us
    all_to_all x1, waiting for transfers between devices, to_owners(): lax.all_to_all(outgoing, ('lon', 'lat'), split_axis=0, concat_axis=0, til...  38.2 us
    pallas_call x1, Pallas kernels, place_rows(): pl.pallas_call(place_kernel, in_specs=[SMEM, VMEM], out_specs=VMEM, out_s...  21.7 us
    pallas_call x1, Pallas kernels, select_rows(): pl.pallas_call(select_kernel, in_specs=[SMEM, VMEM], out_specs=VMEM, out_...  18.8 us
    unnamed x10, local copies, waits for them, and re-layouts  9.31 us
    all_to_all x1, starting transfers between devices, to_owners(): lax.all_to_all(outgoing, ('lon', 'lat'), split_axis=0, concat_axis=0, til...  6.59 us
  transfers between devices with their start and end apart: 2, of which 2 were waited for; matrix products, arithmetic and copies ran while one was open for 2% of the time, Pallas kernels for 0%

profile of v1, /device:TPU:8, one launch (start us, length us, event | category | flops | bytes accessed | tf_op | source)
XLA Modules:
  0.0 313.4 jit_solution(17205492681042346936)
XLA Ops:
  0.6 0.0 copy-start.3
  0.6 1.6 convert_element_type.3
  2.2 0.5 copy-done.3
  2.7 1.9 maximum_multiply_fusion
  4.6 58.7 %shard_map.86 = f32[5,960,128]{2,1,0:T(8,128)} custom-call(f32[5,960,128]{2,1,0:T(8,128)} %bitcast.19, f32[5,960,128]{2,1,0:T(8,128)} %bitcast.12), custom_call_target="tpu_custom_call" | custom-call | flops 30720000 | bytes 7372800 | tf_op jit(solution)/shard_map/pallas_call | solution.py:150
  63.2 2.5 reshape_reshape.6
  65.8 3.4 %copy.12 = f32[150,4096]{0,1:T(8,128)} copy(f32[150,4096]{1,0:T(8,128)S(1)} %reshape_reshape.6) | data formatting | bytes 4915200 | tf_op jit(solution)/shard_map/reshape;reshape | solution.py:265
  69.2 18.8 %shard_map.87 = f32[3072,150]{1,0:T(8,128)} custom-call(s32[3072]{0:T(1024)} %bitcast.24, f32[4096,150]{1,0:T(8,128)} %bitcast.14), custom_call_target="tpu_custom_call" | custom-call | tf_op jit(solution)/shard_map/pallas_call | solution.py:219
  88.0 6.6 %all-to-all-start = ((f32[128,24,150]{2,1,0:T(8,128)}), f32[128,24,150]{2,1,0:T(8,128)S(1)}, u32[]{:S(2)}, u32[]{:S(2)}) async-start(f32[128,24,150]{2,1,0:T(8,128)} %bitcast.18), calls=%async_computation | async-start | bytes 6291456 | tf_op jit(solution)/shard_map/all_to_all | solution.py:250
  94.6 2.8 copy.13
  97.4 38.2 %all-to-all-done = f32[128,24,150]{2,1,0:T(8,128)S(1)} async-done(((f32[128,24,150]{2,1,0:T(8,128)}), f32[128,24,150]{2,1,0:T(8,128)S(1)}, u32[]{:S(2)}, u32[]{:S(2)}) %all-to-all-start) | async-done | bytes 1843232 | tf_op jit(solution)/shard_map/all_to_all | solution.py:250
  135.7 0.0 copy-start
  135.7 1.7 copy-done
  137.3 43.1 %shard_map.88 = (f32[2048,150]{1,0:T(8,128)}, f32[3072,150]{1,0:T(8,128)}) custom-call(s32[4,2048]{1,0:T(4,128)} %slot_ref.1, f32[4,2048]{1,0:T(4,128)} %weight_ref.1, f32[3072,150]{1,0:T(8,128)} %bitcast.16, f32[2048,150]{1,0:T(8,128)} %bitcast.21), custom_call_target="tpu_custom_call" | custom-call | tf_op jit(solution)/shard_map/pallas_call | solution.py:238
  180.4 4.9 %all-to-all-start.1 = ((f32[128,24,150]{2,1,0:T(8,128)}), f32[128,24,150]{2,1,0:T(8,128)S(1)}, u32[]{:S(2)}, u32[]{:S(2)}) async-start(f32[128,24,150]{2,1,0:T(8,128)} %bitcast.22), calls=%async_computation.1 | async-start | bytes 6291456 | tf_op jit(solution)/shard_map/all_to_all | solution.py:254
  185.3 2.7 copy.15
  188.0 38.4 %all-to-all-done.1 = f32[128,24,150]{2,1,0:T(8,128)S(1)} async-done(((f32[128,24,150]{2,1,0:T(8,128)}), f32[128,24,150]{2,1,0:T(8,128)S(1)}, u32[]{:S(2)}, u32[]{:S(2)}) %all-to-all-start.1) | async-done | bytes 1843232 | tf_op jit(solution)/shard_map/all_to_all | solution.py:254
  226.4 1.7 copy-done.1
  228.1 21.7 %shard_map.89 = f32[4096,150]{1,0:T(8,128)} custom-call(s32[3072]{0:T(1024)} %bitcast.25, f32[3072,150]{1,0:T(8,128)} %bitcast.17), custom_call_target="tpu_custom_call" | custom-call | tf_op jit(solution)/shard_map/pallas_call | solution.py:228
  249.8 3.7 %copy.14 = f32[150,4096]{1,0:T(8,128)S(1)} copy(f32[150,4096]{0,1:T(8,128)} %bitcast.15) | data formatting | bytes 4915200 | tf_op jit(solution)/shard_map/transpose | solution.py:273
  253.5 1.8 reshape_reshape.7.v_ref
  255.3 54.3 %shard_map.90 = f32[5,960,128]{2,1,0:T(8,128)} custom-call(f32[5,960,128]{2,1,0:T(8,128)} %reshape_reshape.7.v_ref, f32[5,960,128]{2,1,0:T(8,128)} %bitcast.13), custom_call_target="tpu_custom_call" | custom-call | flops 30720000 | bytes 7372800 | tf_op jit(solution)/shard_map/pallas_call | solution.py:150
  309.6 0.0 copy-done.2
  309.6 3.7 %add.3 = f32[150,32,128]{2,1,0:T(8,128)} add(f32[150,32,128]{2,1,0:T(8,128)S(1)} %copy-done.2, f32[150,32,128]{2,1,0:T(8,128)} %bitcast.20) | non-fusion elementwise | flops 614400 | bytes 7372800 | tf_op jit(solution)/shard_map/add | solution.py:274
  (2 shorter events, 0.0 us)
Async XLA Ops:
  0.6 2.1 copy-start.3
  88.0 47.6 %all-to-all-start = ((f32[128,24,150]{2,1,0:T(8,128)}), f32[128,24,150]{2,1,0:T(8,128)S(1)}, u32[]{:S(2)}, u32[]{:S(2)}) async-start(f32[128,24,150]{2,1,0:T(8,128)} %bitcast.18), calls=%async_computation | async-start | bytes 6291456 | tf_op jit(solution)/shard_map/all_to_all | solution.py:250
  135.7 1.7 copy-start
  180.4 46.1 %all-to-all-start.1 = ((f32[128,24,150]{2,1,0:T(8,128)}), f32[128,24,150]{2,1,0:T(8,128)S(1)}, u32[]{:S(2)}, u32[]{:S(2)}) async-start(f32[128,24,150]{2,1,0:T(8,128)} %bitcast.22), calls=%async_computation.1 | async-start | bytes 6291456 | tf_op jit(solution)/shard_map/all_to_all | solution.py:254
  226.4 1.7 copy-start.1
  255.3 54.3 %copy-start.2 = (f32[150,32,128]{2,1,0:T(8,128)S(1)}, f32[150,32,128]{2,1,0:T(8,128)}, u32[]{:S(2)}) copy-start(f32[150,32,128]{2,1,0:T(8,128)} %param.7) | copy-start | bytes 7372804

commit v2 on v1

--- a/solution.py
+++ b/solution.py
@@ -169,50 +169,80 @@
     return out.reshape(vals, rows, lanes)
 
 
+def load_row(ref, index):
+    return ref[pl.ds(index, 1), :]
+
+
+def add_row(ref, index, value):
+    spot = pl.ds(index, 1)
+    ref[spot, :] = ref[spot, :] + value
+
+
 def select_kernel(index_ref, rows_ref, out_ref):
     cells = rows_ref.shape[0]
-
-    def body(q, carry):
-        source = index_ref[q]
-        row = rows_ref[pl.ds(jnp.minimum(source, cells - 1), 1), :]
-        out_ref[pl.ds(q, 1), :] = jnp.where(source < cells, row, 0.0)
-        return carry
-
-    lax.fori_loop(0, out_ref.shape[0], body, 0, unroll=8)
-
-
-def place_kernel(index_ref, rows_ref, out_ref):
+    width = out_ref.shape[1]
+    sub = lax.broadcasted_iota(jnp.int32, (8, width), 0)
+
+    def body(t, carry):
+        tile = jnp.zeros((8, width), jnp.float32)
+        for i in range(8):
+            source = index_ref[t * 8 + i]
+            row = load_row(rows_ref, jnp.minimum(source, cells - 1))
+            tile = jnp.where((sub == i) & (source < cells), jnp.broadcast_to(row, (8, width)), tile)
+        out_ref[pl.ds(pl.multiple_of(t * 8, 8), 8), :] = tile
+        return carry
+
+    lax.fori_loop(0, out_ref.shape[0] // 8, body, 0, unroll=2)
+
+
+def place_kernel(index_ref, rows_ref, out_ref, *parts):
     cells = out_ref.shape[0]
-    out_ref[...] = jnp.zeros_like(out_ref)
-
-    def body(q, carry):
-        target = index_ref[q]
-        spot = pl.ds(jnp.minimum(target, cells - 1), 1)
-        row = rows_ref[pl.ds(q, 1), :]
-        out_ref[spot, :] = out_ref[spot, :] + jnp.where(target < cells, row, 0.0)
-        return carry
-
-    lax.fori_loop(0, rows_ref.shape[0], body, 0, unroll=8)
-
-
-def interp_kernel(slot_ref, weight_ref, received_ref, precision_ref, equiv_ref, returned_ref):
+    for part in parts:
+        part[...] = jnp.zeros_like(part)
+
+    def body(t, carry):
+        for i, part in enumerate(parts):
+            q = t * len(parts) + i
+            target = index_ref[q]
+            row = load_row(rows_ref, q)
+            add_row(part, jnp.minimum(target, cells - 1), jnp.where(target < cells, row, 0.0))
+        return carry
+
+    lax.fori_loop(0, rows_ref.shape[0] // len(parts), body, 0, unroll=2)
+    total = parts[0][...]
+    for part in parts[1:]:
+        total = total + part[...]
+    out_ref[...] = total
+
+
+def interp_kernel(slot_ref, weight_ref, received_ref, precision_ref, equiv_ref, returned_ref, *parts):
     taps, obs_count = slot_ref.shape
-    returned_ref[...] = jnp.zeros_like(returned_ref)
-
-    def body(j, carry):
-        slots = [slot_ref[k, j] for k in range(taps)]
-        weights = [weight_ref[k, j] for k in range(taps)]
-        total = received_ref[pl.ds(slots[0], 1), :] * weights[0]
-        for k in range(1, taps):
-            total = total + received_ref[pl.ds(slots[k], 1), :] * weights[k]
-        equiv_ref[pl.ds(j, 1), :] = total
-        weighted = precision_ref[pl.ds(j, 1), :] * total
-        for k in range(taps):
-            spot = pl.ds(slots[k], 1)
-            returned_ref[spot, :] = returned_ref[spot, :] + weighted * weights[k]
-        return carry
-
-    lax.fori_loop(0, obs_count, body, 0, unroll=4)
+    width = equiv_ref.shape[1]
+    sub = lax.broadcasted_iota(jnp.int32, (8, width), 0)
+    for part in parts:
+        part[...] = jnp.zeros_like(part)
+
+    def body(t, carry):
+        tile = jnp.zeros((8, width), jnp.float32)
+        for i in range(8):
+            j = t * 8 + i
+            slots = [slot_ref[k, j] for k in range(taps)]
+            weights = [weight_ref[k, j] for k in range(taps)]
+            total = load_row(received_ref, slots[0]) * weights[0]
+            for k in range(1, taps):
+                total = total + load_row(received_ref, slots[k]) * weights[k]
+            tile = jnp.where(sub == i, jnp.broadcast_to(total, (8, width)), tile)
+            weighted = load_row(precision_ref, j) * total
+            for k in range(taps):
+                add_row(parts[(i % 2) * taps + k], slots[k], weighted * weights[k])
+        equiv_ref[pl.ds(pl.multiple_of(t * 8, 8), 8), :] = tile
+        return carry
+
+    lax.fori_loop(0, obs_count // 8, body, 0)
+    total = parts[0][...]
+    for part in parts[1:]:
+        total = total + part[...]
+    returned_ref[...] = total
 
 
 def select_rows(index, rows, count):
@@ -230,6 +260,8 @@
         in_specs=[SMEM, VMEM],
         out_specs=VMEM,
         out_shape=jax.ShapeDtypeStruct((cells, rows.shape[1]), jnp.float32),
+        scratch_shapes=[pltpu.VMEM((cells, rows.shape[1]), jnp.float32) for _ in range(4)],
+        compiler_params=pltpu.CompilerParams(vmem_limit_bytes=60 * 1024 * 1024),
     )(index, rows)
 
 
@@ -243,6 +275,10 @@
             jax.ShapeDtypeStruct((obs_count, received.shape[1]), jnp.float32),
             jax.ShapeDtypeStruct(received.shape, jnp.float32),
         ],
+        scratch_shapes=[
+            pltpu.VMEM(received.shape, jnp.float32) for _ in range(2 * obs_slots.shape[0])
+        ],
+        compiler_params=pltpu.CompilerParams(vmem_limit_bytes=60 * 1024 * 1024),
     )(obs_slots, obs_weights, received, precision_rows)
 
 

time: 316 us -> 305 us (0.965)
  Pallas kernels: 197 us -> 186 us
    pallas_call x1, Pallas kernels: 43.1 us -> 36.4 us  [interpolate(): pl.pallas_call(interp_kernel, in_specs=[SMEM, SMEM, VMEM, VMEM], out_spec...]
    pallas_call x1, Pallas kernels: 18.8 us -> 15.2 us  [select_rows(): pl.pallas_call(select_kernel, in_specs=[SMEM, VMEM], out_specs=VMEM, out_...]
where the time goes in v2:
time: 305 us; the launch traced here: 303 us
  Pallas kernels  186 us (61%)
  waiting for transfers between devices  76.7 us (25%)
  local copies, waits for them, and re-layouts  20.8 us (7%)
  starting transfers between devices  11.5 us (4%)
  other arithmetic  7.13 us (2%)
    pallas_call x2, Pallas kernels, diffuse(): pl.pallas_call(functools.partial(diffuse_kernel, rows), in_specs=[VMEM, V...  113 us
    all_to_all x1, waiting for transfers between devices, to_sources(): lax.all_to_all(returned, ('lon', 'lat'), split_axis=0, concat_axis=0, til...  38.4 us
    all_to_all x1, waiting for transfers between devices, to_owners(): lax.all_to_all(outgoing, ('lon', 'lat'), split_axis=0, concat_axis=0, til...  38.2 us
    pallas_call x1, Pallas kernels, interpolate(): pl.pallas_call(interp_kernel, in_specs=[SMEM, SMEM, VMEM, VMEM], out_spec...  36.4 us
    pallas_call x1, Pallas kernels, place_rows(): pl.pallas_call(place_kernel, in_specs=[SMEM, VMEM], out_specs=VMEM, out_s...  21.4 us
    pallas_call x1, Pallas kernels, select_rows(): pl.pallas_call(select_kernel, in_specs=[SMEM, VMEM], out_specs=VMEM, out_...  15.2 us
    unnamed x10, local copies, waits for them, and re-layouts  9.31 us
    all_to_all x1, starting transfers between devices, to_owners(): lax.all_to_all(outgoing, ('lon', 'lat'), split_axis=0, concat_axis=0, til...  6.59 us
  transfers between devices with their start and end apart: 2, of which 2 were waited for; matrix products, arithmetic and copies ran while one was open for 2% of the time, Pallas kernels for 0%

profile of v2, /device:TPU:8, one launch (start us, length us, event | category | flops | bytes accessed | tf_op | source)
XLA Modules:
  0.0 302.8 jit_solution(3741238112503476084)
XLA Ops:
  0.6 0.0 copy-start.3
  0.6 1.6 convert_element_type.3
  2.2 0.5 copy-done.3
  2.7 1.9 maximum_multiply_fusion
  4.6 58.7 %shard_map.86 = f32[5,960,128]{2,1,0:T(8,128)} custom-call(f32[5,960,128]{2,1,0:T(8,128)} %bitcast.19, f32[5,960,128]{2,1,0:T(8,128)} %bitcast.12), custom_call_target="tpu_custom_call" | custom-call | flops 30720000 | bytes 7372800 | tf_op jit(solution)/shard_map/pallas_call | solution.py:150
  63.2 2.5 reshape_reshape.6
  65.8 3.4 %copy.12 = f32[150,4096]{0,1:T(8,128)} copy(f32[150,4096]{1,0:T(8,128)S(1)} %reshape_reshape.6) | data formatting | bytes 4915200 | tf_op jit(solution)/shard_map/reshape;reshape | solution.py:301
  69.2 15.2 %shard_map.87 = f32[3072,150]{1,0:T(8,128)} custom-call(s32[3072]{0:T(1024)} %bitcast.24, f32[4096,150]{1,0:T(8,128)} %bitcast.14), custom_call_target="tpu_custom_call" | custom-call | tf_op jit(solution)/shard_map/pallas_call | solution.py:249
  84.4 6.6 %all-to-all-start = ((f32[128,24,150]{2,1,0:T(8,128)}), f32[128,24,150]{2,1,0:T(8,128)S(1)}, u32[]{:S(2)}, u32[]{:S(2)}) async-start(f32[128,24,150]{2,1,0:T(8,128)} %bitcast.18), calls=%async_computation | async-start | bytes 6291456 | tf_op jit(solution)/shard_map/all_to_all | solution.py:286
  91.0 2.8 copy.13
  93.8 38.2 %all-to-all-done = f32[128,24,150]{2,1,0:T(8,128)S(1)} async-done(((f32[128,24,150]{2,1,0:T(8,128)}), f32[128,24,150]{2,1,0:T(8,128)S(1)}, u32[]{:S(2)}, u32[]{:S(2)}) %all-to-all-start) | async-done | bytes 1843232 | tf_op jit(solution)/shard_map/all_to_all | solution.py:286
  132.0 0.0 copy-start
  132.0 1.7 copy-done
  133.7 36.4 %shard_map.88 = (f32[2048,150]{1,0:T(8,128)}, f32[3072,150]{1,0:T(8,128)}) custom-call(s32[4,2048]{1,0:T(4,128)} %slot_ref.1, f32[4,2048]{1,0:T(4,128)} %weight_ref.1, f32[3072,150]{1,0:T(8,128)} %bitcast.16, f32[2048,150]{1,0:T(8,128)} %bitcast.21), custom_call_target="tpu_custom_call" | custom-call | tf_op jit(solution)/shard_map/pallas_call | solution.py:270
  170.1 4.9 %all-to-all-start.1 = ((f32[128,24,150]{2,1,0:T(8,128)}), f32[128,24,150]{2,1,0:T(8,128)S(1)}, u32[]{:S(2)}, u32[]{:S(2)}) async-start(f32[128,24,150]{2,1,0:T(8,128)} %bitcast.22), calls=%async_computation.1 | async-start | bytes 6291456 | tf_op jit(solution)/shard_map/all_to_all | solution.py:290
  175.0 2.7 copy.15
  177.7 38.4 %all-to-all-done.1 = f32[128,24,150]{2,1,0:T(8,128)S(1)} async-done(((f32[128,24,150]{2,1,0:T(8,128)}), f32[128,24,150]{2,1,0:T(8,128)S(1)}, u32[]{:S(2)}, u32[]{:S(2)}) %all-to-all-start.1) | async-done | bytes 1843232 | tf_op jit(solution)/shard_map/all_to_all | solution.py:290
  216.2 1.7 copy-done.1
  217.8 21.4 %shard_map.89 = f32[4096,150]{1,0:T(8,128)} custom-call(s32[3072]{0:T(1024)} %bitcast.25, f32[3072,150]{1,0:T(8,128)} %bitcast.17), custom_call_target="tpu_custom_call" | custom-call | tf_op jit(solution)/shard_map/pallas_call | solution.py:258
  239.2 3.7 %copy.14 = f32[150,4096]{1,0:T(8,128)S(1)} copy(f32[150,4096]{0,1:T(8,128)} %bitcast.15) | data formatting | bytes 4915200 | tf_op jit(solution)/shard_map/transpose | solution.py:309
  242.9 1.8 reshape_reshape.7.v_ref
  244.7 54.3 %shard_map.90 = f32[5,960,128]{2,1,0:T(8,128)} custom-call(f32[5,960,128]{2,1,0:T(8,128)} %reshape_reshape.7.v_ref, f32[5,960,128]{2,1,0:T(8,128)} %bitcast.13), custom_call_target="tpu_custom_call" | custom-call | flops 30720000 | bytes 7372800 | tf_op jit(solution)/shard_map/pallas_call | solution.py:150
  299.1 0.0 copy-done.2
  299.1 3.7 %add.3 = f32[150,32,128]{2,1,0:T(8,128)} add(f32[150,32,128]{2,1,0:T(8,128)S(1)} %copy-done.2, f32[150,32,128]{2,1,0:T(8,128)} %bitcast.20) | non-fusion elementwise | flops 614400 | bytes 7372800 | tf_op jit(solution)/shard_map/add | solution.py:310
  (2 shorter events, 0.0 us)
Async XLA Ops:
  0.6 2.1 copy-start.3
  84.4 47.6 %all-to-all-start = ((f32[128,24,150]{2,1,0:T(8,128)}), f32[128,24,150]{2,1,0:T(8,128)S(1)}, u32[]{:S(2)}, u32[]{:S(2)}) async-start(f32[128,24,150]{2,1,0:T(8,128)} %bitcast.18), calls=%async_computation | async-start | bytes 6291456 | tf_op jit(solution)/shard_map/all_to_all | solution.py:286
  132.0 1.7 copy-start
  170.1 46.1 %all-to-all-start.1 = ((f32[128,24,150]{2,1,0:T(8,128)}), f32[128,24,150]{2,1,0:T(8,128)S(1)}, u32[]{:S(2)}, u32[]{:S(2)}) async-start(f32[128,24,150]{2,1,0:T(8,128)} %bitcast.22), calls=%async_computation.1 | async-start | bytes 6291456 | tf_op jit(solution)/shard_map/all_to_all | solution.py:290
  216.2 1.7 copy-start.1
  244.7 54.3 %copy-start.2 = (f32[150,32,128]{2,1,0:T(8,128)S(1)}, f32[150,32,128]{2,1,0:T(8,128)}, u32[]{:S(2)}) copy-start(f32[150,32,128]{2,1,0:T(8,128)} %param.7) | copy-start | bytes 7372804

commit v3 on v2

--- a/solution.py
+++ b/solution.py
@@ -282,12 +282,55 @@
     )(obs_slots, obs_weights, received, precision_rows)
 
 
-def to_owners(outgoing):
-    return lax.all_to_all(outgoing, ("lon", "lat"), split_axis=0, concat_axis=0, tiled=True)
-
-
-def to_sources(returned):
-    return lax.all_to_all(returned, ("lon", "lat"), split_axis=0, concat_axis=0, tiled=True)
+def exchange_kernel(x_ref, out_ref, landed, send_sem, recv_sem, local_sem):
+    n_lat = lax.axis_size("lat")
+    count = lax.axis_size("lon") * n_lat
+    chunk = x_ref.shape[0] // count
+    me = lax.axis_index("lon") * n_lat + lax.axis_index("lat")
+    mine = pl.ds(me * chunk, chunk)
+    local = pltpu.make_async_copy(x_ref.at[mine], landed.at[mine], local_sem)
+    local.start()
+
+    def body(step, carry):
+        peer = (me + step) % count
+        pltpu.make_async_remote_copy(
+            src_ref=x_ref.at[pl.ds(peer * chunk, chunk)],
+            dst_ref=landed.at[mine],
+            send_sem=send_sem,
+            recv_sem=recv_sem,
+            device_id={"lon": peer // n_lat, "lat": peer % n_lat},
+            device_id_type=pl.DeviceIdType.MESH,
+        ).start()
+        return carry
+
+    lax.fori_loop(1, count, body, 0)
+    others = pl.ds(0, (count - 1) * chunk)
+    pltpu.make_async_remote_copy(
+        src_ref=x_ref.at[others],
+        dst_ref=landed.at[others],
+        send_sem=send_sem,
+        recv_sem=recv_sem,
+        device_id={"lon": 0, "lat": 0},
+        device_id_type=pl.DeviceIdType.MESH,
+    ).wait()
+    local.wait()
+    out_ref[...] = landed[...]
+
+
+def exchange(x):
+    return pl.pallas_call(
+        exchange_kernel,
+        in_specs=[VMEM],
+        out_specs=VMEM,
+        out_shape=jax.ShapeDtypeStruct(x.shape, jnp.float32),
+        scratch_shapes=[
+            pltpu.VMEM(x.shape, jnp.float32),
+            pltpu.SemaphoreType.DMA(()),
+            pltpu.SemaphoreType.DMA(()),
+            pltpu.SemaphoreType.DMA(()),
+        ],
+        compiler_params=pltpu.CompilerParams(has_side_effects=True),
+    )(x)
 
 
 def on_device(state, diffusivity, sea_mask, send_cols, obs_slots, obs_weights, obs_precision):
@@ -301,10 +344,10 @@
     rows_of = smooth.reshape(vals, cell_count).T
     send_index = send_cols[0]
     outgoing = select_rows(send_index, rows_of, send_index.shape[0])
-    received = to_owners(outgoing)
+    received = exchange(outgoing)
     equivalent_rows, returned = interpolate(obs_slots, obs_weights, received, obs_precision.T)
     equivalents = equivalent_rows.T
-    incoming = to_sources(returned)
+    incoming = exchange(returned)
     adjoint_rows = place_rows(send_index, incoming, cell_count)
     adjoint_field = adjoint_rows.T.reshape(state.shape)
     product = state + diffuse(adjoint_field, conduct_blocks)

time: 305 us -> 329 us (1.079)
  Pallas kernels: 186 us -> 302 us
  waiting for transfers between devices: 76.7 us -> 0 us
  starting transfers between devices: 11.5 us -> 0 us
  local copies, waits for them, and re-layouts: 20.8 us -> 15.3 us
    pallas_call x0 -> x2, Pallas kernels: none -> 112 us  [exchange(): pl.pallas_call(exchange_kernel, in_specs=[VMEM], out_specs=VMEM, out_shap...]
    all_to_all x2 -> x0, waiting for transfers between devices: 76.7 us -> none  [the longest x1 38.4 us: to_sources(): lax.all_to_all(returned, ('lon', 'lat'), split_axis=0, concat_axis=0, til...]
    all_to_all x2 -> x0, starting transfers between devices: 11.5 us -> none  [the longest x1 6.59 us: to_owners(): lax.all_to_all(outgoing, ('lon', 'lat'), split_axis=0, concat_axis=0, til...]
    unnamed x10, local copies, waits for them, and re-layouts: 9.31 us -> 3.94 us
    pallas_call x2, Pallas kernels: 113 us -> 118 us  [diffuse(): pl.pallas_call(functools.partial(diffuse_kernel, rows), in_specs=[VMEM, V...]
  transfers between devices with their start and end apart: 2 -> 0, of which waited for: 2 -> 0; matrix products, arithmetic and copies ran while one was open for 2% -> 0% of each run, Pallas kernels for 0% -> 0%
where the time goes in v3:
time: 329 us; the launch traced here: 325 us
  Pallas kernels  302 us (92%)
  local copies, waits for them, and re-layouts  15.3 us (5%)
  other arithmetic  7.13 us (2%)
    pallas_call x2, Pallas kernels, diffuse(): pl.pallas_call(functools.partial(diffuse_kernel, rows), in_specs=[VMEM, V...  118 us
    pallas_call x2, Pallas kernels, exchange(): pl.pallas_call(exchange_kernel, in_specs=[VMEM], out_specs=VMEM, out_shap...  112 us
    pallas_call x1, Pallas kernels, interpolate(): pl.pallas_call(interp_kernel, in_specs=[SMEM, SMEM, VMEM, VMEM], out_spec...  36.4 us
    pallas_call x1, Pallas kernels, place_rows(): pl.pallas_call(place_kernel, in_specs=[SMEM, VMEM], out_specs=VMEM, out_s...  21.4 us
    pallas_call x1, Pallas kernels, select_rows(): pl.pallas_call(select_kernel, in_specs=[SMEM, VMEM], out_specs=VMEM, out_...  15.2 us

profile of v3, /device:TPU:8, one launch (start us, length us, event | category | flops | bytes accessed | tf_op | source)
XLA Modules:
  0.0 325.5 jit_solution(427952067659748872)
XLA Ops:
  0.6 0.0 copy-start.1
  0.6 1.6 convert_element_type.3
  2.2 0.5 copy-done.1
  2.7 0.0 copy-start.3
  2.7 1.9 maximum_multiply_fusion
  4.6 0.0 copy-done.3
  4.6 1.8 copy.13
  6.4 58.6 %shard_map.86 = f32[5,960,128]{2,1,0:T(8,128)} custom-call(f32[5,960,128]{2,1,0:T(8,128)} %bitcast.12, f32[5,960,128]{2,1,0:T(8,128)} %bitcast.8), custom_call_target="tpu_custom_call" | custom-call | flops 30720000 | bytes 7372800 | tf_op jit(solution)/shard_map/pallas_call | solution.py:150
  65.0 2.5 reshape_reshape.6
  67.6 3.3 %copy.12 = f32[150,4096]{0,1:T(8,128)} copy(f32[150,4096]{1,0:T(8,128)S(1)} %reshape_reshape.6) | data formatting | bytes 4915200 | tf_op jit(solution)/shard_map/reshape;reshape | solution.py:344
  70.9 15.2 %shard_map.87.x_ref = f32[3072,150]{1,0:T(8,128)} custom-call(s32[3072]{0:T(1024)} %bitcast.16, f32[4096,150]{1,0:T(8,128)} %bitcast.10), custom_call_target="tpu_custom_call" | custom-call | tf_op jit(solution)/shard_map/pallas_call | solution.py:249
  86.1 53.3 %shard_map.88.received_ref = f32[3072,150]{1,0:T(8,128)} custom-call(f32[3072,150]{1,0:T(8,128)} %shard_map.87.x_ref), custom_call_target="tpu_custom_call" | custom-call | tf_op jit(solution)/shard_map/pallas_call | solution.py:321
  139.4 36.4 %shard_map.89 = (f32[2048,150]{1,0:T(8,128)}, f32[3072,150]{1,0:T(8,128)}) custom-call(s32[4,2048]{1,0:T(4,128)} %slot_ref.1, f32[4,2048]{1,0:T(4,128)} %weight_ref.1, f32[3072,150]{1,0:T(8,128)} %shard_map.88.received_ref, f32[2048,150]{1,0:T(8,128)} %bitcast.14), custom_call_target="tpu_custom_call" | custom-call | tf_op jit(solution)/shard_map/pallas_call | solution.py:270
  175.8 0.0 copy-start.2
  175.8 58.5 %shard_map.90.rows_ref = f32[3072,150]{1,0:T(8,128)} custom-call(f32[3072,150]{1,0:T(8,128)} %get-tuple-element.4.x_ref), custom_call_target="tpu_custom_call" | custom-call | tf_op jit(solution)/shard_map/pallas_call | solution.py:321
  234.4 0.0 copy-done.2
  234.4 1.6 copy.15
  236.0 21.4 %shard_map.91 = f32[4096,150]{1,0:T(8,128)} custom-call(s32[3072]{0:T(1024)} %bitcast.17, f32[3072,150]{1,0:T(8,128)} %shard_map.90.rows_ref), custom_call_target="tpu_custom_call" | custom-call | tf_op jit(solution)/shard_map/pallas_call | solution.py:258
  257.4 3.7 %copy.14 = f32[150,4096]{1,0:T(8,128)S(1)} copy(f32[150,4096]{0,1:T(8,128)} %bitcast.11) | data formatting | bytes 4915200 | tf_op jit(solution)/shard_map/transpose | solution.py:352
  261.1 1.8 reshape_reshape.7.v_ref
  262.9 0.0 copy-start
  262.9 58.9 %shard_map.92 = f32[5,960,128]{2,1,0:T(8,128)} custom-call(f32[5,960,128]{2,1,0:T(8,128)} %reshape_reshape.7.v_ref, f32[5,960,128]{2,1,0:T(8,128)} %bitcast.9), custom_call_target="tpu_custom_call" | custom-call | flops 30720000 | bytes 7372800 | tf_op jit(solution)/shard_map/pallas_call | solution.py:150
  321.8 0.0 copy-done
  321.8 3.7 %add.3 = f32[150,32,128]{2,1,0:T(8,128)} add(f32[150,32,128]{2,1,0:T(8,128)S(1)} %copy-done, f32[150,32,128]{2,1,0:T(8,128)} %bitcast.13) | non-fusion elementwise | flops 614400 | bytes 7372800 | tf_op jit(solution)/shard_map/add | solution.py:353
Async XLA Ops:
  0.6 2.1 copy-start.1
  2.7 1.9 copy-start.3
  175.8 58.5 %copy-start.2 = (f32[2048,150]{1,0:T(8,128)S(1)}, f32[2048,150]{1,0:T(8,128)}, u32[]{:S(2)}) copy-start(f32[2048,150]{1,0:T(8,128)} %get-tuple-element.5) | copy-start | bytes 3686404
  262.9 58.9 %copy-start = (f32[150,32,128]{2,1,0:T(8,128)S(1)}, f32[150,32,128]{2,1,0:T(8,128)}, u32[]{:S(2)}) copy-start(f32[150,32,128]{2,1,0:T(8,128)} %param.7) | copy-start | bytes 7372804

commit v4 on v2

--- a/solution.py
+++ b/solution.py
@@ -14,8 +14,7 @@
 
 
 def slab_pass(rows, src_ref, conduct_ref, field_halo, coef_halo, scales, dst_ref, edges):
-    groups, span, lanes = src_ref.shape
-    group = span // rows
+    groups, rows, group, lanes = src_ref.shape
     north_ok, south_ok = scales
     row_halo, col_halo = field_halo
     coef_rows, coef_cols = coef_halo
@@ -25,7 +24,7 @@
         col = lax.broadcasted_iota(jnp.int32, (group, rows), 1)
 
         def slab(ref, r):
-            return ref[g, pl.ds(r, group, stride=rows), :]
+            return ref[g, r]
 
         vw = col_halo[0, g]
         ve = col_halo[1, g]
@@ -51,7 +50,7 @@
             total = total + jnp.minimum(c_mid, c_w) * (x_w - x_mid)
             total = total + jnp.minimum(c_mid, c_e) * (x_e - x_mid)
             out = x_mid + total
-            dst_ref[g, pl.ds(r, group, stride=rows), :] = out
+            dst_ref[g, r] = out
             if edges is not None:
                 if r == 0:
                     edges[0][0, g] = out
@@ -70,15 +69,14 @@
 
 
 def edge_pass(rows, src_ref, row_out, col_out):
-    groups, span, lanes = src_ref.shape
-    group = span // rows
+    groups, rows, group, lanes = src_ref.shape
 
     def body(g, carry):
         col = lax.broadcasted_iota(jnp.int32, (group, rows), 1)
         left = jnp.zeros((group, rows), jnp.float32)
         right = jnp.zeros((group, rows), jnp.float32)
         for r in range(rows):
-            x = src_ref[g, pl.ds(r, group, stride=rows), :]
+            x = src_ref[g, r]
             if r == 0:
                 row_out[0, g] = x
             if r == rows - 1:
@@ -142,12 +140,31 @@
     slab_pass(rows, mid_ref, c_ref, (row_halo.at[2], col_halo.at[2]), coef_halo, scales, out_ref, None)
 
 
-def diffuse(field, conduct_blocks):
+def to_slabs(field):
     vals, rows, lanes = field.shape
     groups = vals // GROUP
-    blocks = field.reshape(groups, GROUP * rows, lanes)
+    return field.reshape(groups, GROUP, rows, lanes).transpose(0, 2, 1, 3)
+
+
+def from_slabs(slabs):
+    groups, rows, group, lanes = slabs.shape
+    return slabs.transpose(0, 2, 1, 3).reshape(groups * group, rows, lanes)
+
+
+def slabs_to_rows(slabs):
+    groups, rows, group, lanes = slabs.shape
+    return slabs.transpose(1, 3, 0, 2).reshape(rows * lanes, groups * group)
+
+
+def rows_to_slabs(cell_rows, rows, lanes):
+    vals = cell_rows.shape[1]
+    return cell_rows.reshape(rows, lanes, vals // GROUP, GROUP).transpose(2, 0, 3, 1)
+
+
+def diffuse(blocks, conduct_blocks):
+    groups, rows, group, lanes = blocks.shape
     rounds = SWEEPS + 1
-    out = pl.pallas_call(
+    return pl.pallas_call(
         functools.partial(diffuse_kernel, rows),
         in_specs=[VMEM, VMEM],
         out_specs=VMEM,
@@ -163,10 +180,9 @@
         ],
         compiler_params=pltpu.CompilerParams(collective_id=0, has_side_effects=True),
         cost_estimate=pl.CostEstimate(
-            flops=50 * field.size, bytes_accessed=12 * field.size, transcendentals=0
+            flops=50 * blocks.size, bytes_accessed=12 * blocks.size, transcendentals=0
         ),
     )(blocks, conduct_blocks)
-    return out.reshape(vals, rows, lanes)
 
 
 def load_row(ref, index):
@@ -293,12 +309,11 @@
 def on_device(state, diffusivity, sea_mask, send_cols, obs_slots, obs_weights, obs_precision):
     vals, rows, lanes = state.shape
     cell_count = rows * lanes
-    steps = vals // GROUP
     sea_float = sea_mask.astype(jnp.float32)
     conduct = diffusivity * jnp.concatenate([sea_float, sea_float], axis=0)
-    conduct_blocks = conduct.reshape(steps, GROUP * rows, lanes)
-    smooth = diffuse(state, conduct_blocks)
-    rows_of = smooth.reshape(vals, cell_count).T
+    conduct_blocks = to_slabs(conduct)
+    smooth = diffuse(to_slabs(state), conduct_blocks)
+    rows_of = slabs_to_rows(smooth)
     send_index = send_cols[0]
     outgoing = select_rows(send_index, rows_of, send_index.shape[0])
     received = to_owners(outgoing)
@@ -306,8 +321,8 @@
     equivalents = equivalent_rows.T
     incoming = to_sources(returned)
     adjoint_rows = place_rows(send_index, incoming, cell_count)
-    adjoint_field = adjoint_rows.T.reshape(state.shape)
-    product = state + diffuse(adjoint_field, conduct_blocks)
+    adjoint_field = rows_to_slabs(adjoint_rows, rows, lanes)
+    product = state + from_slabs(diffuse(adjoint_field, conduct_blocks))
     return (product, equivalents)
 
 

time: 305 us -> 313 us (1.026)
  local copies, waits for them, and re-layouts: 20.8 us -> 35 us
  Pallas kernels: 186 us -> 182 us
    transpose x1 -> x3, local copies, waits for them, and re-layouts: 3.66 us -> 11.7 us  [the longest x1 5.3 us: to_slabs(): return field.reshape(groups, GROUP, rows, lanes).transpose(0, 2, 1, 3)]
    another operation x3 -> x0, local copies, waits for them, and re-layouts: 7.8 us -> none  [the longest x2 5.96 us: on_device(): rows_of = smooth.reshape(vals, cell_count).T]
    reshape x0 -> x2, local copies, waits for them, and re-layouts: none -> 6.2 us  [the longest x1 3.28 us: slabs_to_rows(): return slabs.transpose(1, 3, 0, 2).reshape(rows * lanes, groups * group)]
    pallas_call x2, Pallas kernels: 113 us -> 109 us  [diffuse(): pl.pallas_call(functools.partial(diffuse_kernel, rows), in_specs=[VMEM, V...]
    unnamed x10 -> x16, local copies, waits for them, and re-layouts: 9.31 us -> 13.5 us
    pallas_call x0 -> x1, local copies, waits for them, and re-layouts: none -> 3.66 us  [place_rows(): pl.pallas_call(place_kernel, in_specs=[SMEM, VMEM], out_specs=VMEM, out_s...]
where the time goes in v4:
time: 313 us; the launch traced here: 310 us
  Pallas kernels  182 us (58%)
  waiting for transfers between devices  76.7 us (25%)
  local copies, waits for them, and re-layouts  35 us (11%)
  starting transfers between devices  11.5 us (4%)
  other arithmetic  4.03 us (1%)
    pallas_call x2, Pallas kernels, diffuse(): pl.pallas_call(functools.partial(diffuse_kernel, rows), in_specs=[VMEM, V...  109 us
    all_to_all x1, waiting for transfers between devices, to_sources(): lax.all_to_all(returned, ('lon', 'lat'), split_axis=0, concat_axis=0, til...  38.4 us
    all_to_all x1, waiting for transfers between devices, to_owners(): lax.all_to_all(outgoing, ('lon', 'lat'), split_axis=0, concat_axis=0, til...  38.3 us
    pallas_call x1, Pallas kernels, interpolate(): pl.pallas_call(interp_kernel, in_specs=[SMEM, SMEM, VMEM, VMEM], out_spec...  36.5 us
    pallas_call x1, Pallas kernels, place_rows(): pl.pallas_call(place_kernel, in_specs=[SMEM, VMEM], out_specs=VMEM, out_s...  21.5 us
    pallas_call x1, Pallas kernels, select_rows(): pl.pallas_call(select_kernel, in_specs=[SMEM, VMEM], out_specs=VMEM, out_...  15.2 us
    unnamed x16, local copies, waits for them, and re-layouts  13.5 us
    all_to_all x1, starting transfers between devices, to_owners(): lax.all_to_all(outgoing, ('lon', 'lat'), split_axis=0, concat_axis=0, til...  6.59 us
  transfers between devices with their start and end apart: 2, of which 2 were waited for; matrix products, arithmetic and copies ran while one was open for 2% of the time, Pallas kernels for 0%

profile of v4, /device:TPU:8, one launch (start us, length us, event | category | flops | bytes accessed | tf_op | source)
XLA Modules:
  0.0 310.1 jit_solution(6988550888617015273)
XLA Ops:
  0.6 1.6 convert_element_type.3
  2.2 0.5 copy-done.4
  3.2 1.2 copy-done.2
  4.4 5.3 %copy_bitcast_fusion.1 = (f32[5,32,30,128]{3,2,1,0:T(8,128)}, f32[5,32,30,128]{3,2,1,0:T(8,128)}) fusion(f32[5,30,32,128]{3,2,1,0:T(8,128)S(1)} %bitcast.43, f32[5,30,32,128]{3,2,1,0:T(8,128)S(1)} %bitcast.42), kind=kLoop, calls=%fused_computation.1 | loop fusion | bytes 9830400 | tf_op jit(solution)/shard_map/transpose | solution.py:146
  9.7 56.6 %shard_map.86 = f32[5,32,30,128]{3,2,1,0:T(8,128)} custom-call(f32[5,32,30,128]{3,2,1,0:T(8,128)} %get-tuple-element.11.v_ref, f32[5,32,30,128]{3,2,1,0:T(8,128)} %get-tuple-element.10.c_ref), custom_call_target="tpu_custom_call" | custom-call | flops 30720000 | bytes 7372800 | tf_op jit(solution)/shard_map/pallas_call | solution.py:167
  66.3 3.1 %copy.14 = f32[32,128,5,30]{1,0,3,2:T(8,128)S(1)} copy(f32[32,128,5,30]{1,3,0,2:T(8,128)} %bitcast.37) | data formatting | bytes 4915200 | tf_op jit(solution)/shard_map/transpose | solution.py:156
  69.7 2.0 copy.21
  71.8 3.3 %copy.15.rows_ref = f32[4096,150]{1,0:T(8,128)} copy(f32[4096,150]{0,1:T(8,128)S(1)} %bitcast.39) | data formatting | bytes 4915200 | tf_op jit(solution)/shard_map/reshape | solution.py:156
  75.0 15.2 %shard_map.87 = f32[3072,150]{1,0:T(8,128)} custom-call(s32[3072]{0:T(1024)} %bitcast.49, f32[4096,150]{1,0:T(8,128)} %copy.15.rows_ref), custom_call_target="tpu_custom_call" | custom-call | tf_op jit(solution)/shard_map/pallas_call | solution.py:265
  90.2 6.6 %all-to-all-start = ((f32[128,24,150]{2,1,0:T(8,128)}), f32[128,24,150]{2,1,0:T(8,128)S(1)}, u32[]{:S(2)}, u32[]{:S(2)}) async-start(f32[128,24,150]{2,1,0:T(8,128)} %bitcast.34), calls=%async_computation | async-start | bytes 6291456 | tf_op jit(solution)/shard_map/all_to_all | solution.py:302
  96.8 2.7 copy.16
  99.6 38.3 %all-to-all-done = f32[128,24,150]{2,1,0:T(8,128)S(1)} async-done(((f32[128,24,150]{2,1,0:T(8,128)}), f32[128,24,150]{2,1,0:T(8,128)S(1)}, u32[]{:S(2)}, u32[]{:S(2)}) %all-to-all-start) | async-done | bytes 1843232 | tf_op jit(solution)/shard_map/all_to_all | solution.py:302
  137.9 1.7 copy-done
  139.6 36.5 %shard_map.88 = (f32[2048,150]{1,0:T(8,128)}, f32[3072,150]{1,0:T(8,128)}) custom-call(s32[4,2048]{1,0:T(4,128)} %slot_ref.1, f32[4,2048]{1,0:T(4,128)} %weight_ref.1, f32[3072,150]{1,0:T(8,128)} %bitcast.32, f32[2048,150]{1,0:T(8,128)} %bitcast.46), custom_call_target="tpu_custom_call" | custom-call | tf_op jit(solution)/shard_map/pallas_call | solution.py:286
  176.1 4.9 %all-to-all-start.1 = ((f32[128,24,150]{2,1,0:T(8,128)}), f32[128,24,150]{2,1,0:T(8,128)S(1)}, u32[]{:S(2)}, u32[]{:S(2)}) async-start(f32[128,24,150]{2,1,0:T(8,128)} %bitcast.47), calls=%async_computation.1 | async-start | bytes 6291456 | tf_op jit(solution)/shard_map/all_to_all | solution.py:306
  181.0 2.7 copy.20
  183.7 38.4 %all-to-all-done.1 = f32[128,24,150]{2,1,0:T(8,128)S(1)} async-done(((f32[128,24,150]{2,1,0:T(8,128)}), f32[128,24,150]{2,1,0:T(8,128)S(1)}, u32[]{:S(2)}, u32[]{:S(2)}) %all-to-all-start.1) | async-done | bytes 1843232 | tf_op jit(solution)/shard_map/all_to_all | solution.py:306
  222.1 1.7 copy-done.1
  223.8 21.5 %shard_map.89 = f32[4096,150]{1,0:T(8,128)} custom-call(s32[3072]{0:T(1024)} %bitcast.50, f32[3072,150]{1,0:T(8,128)} %bitcast.33), custom_call_target="tpu_custom_call" | custom-call | tf_op jit(solution)/shard_map/pallas_call | solution.py:274
  245.3 3.7 %copy.17 = f32[4096,150]{0,1:T(8,128)S(1)} copy(f32[4096,150]{1,0:T(8,128)} %shard_map.89) | data formatting | bytes 4915200 | tf_op jit(solution)/shard_map/pallas_call | solution.py:274
  249.6 2.9 copy.26
  252.5 52.2 %shard_map.90 = f32[5,32,30,128]{3,2,1,0:T(8,128)} custom-call(f32[5,32,30,128]{3,2,1,0:T(8,128)} %bitcast.35, f32[5,32,30,128]{3,2,1,0:T(8,128)} %get-tuple-element.10.c_ref), custom_call_target="tpu_custom_call" | custom-call | flops 30720000 | bytes 7372800 | tf_op jit(solution)/shard_map/pallas_call | solution.py:167
  304.7 3.3 %copy.19 = f32[5,30,32,128]{3,2,1,0:T(8,128)S(1)} copy(f32[5,30,32,128]{3,1,2,0:T(8,128)} %bitcast.36) | data formatting | bytes 4915200 | tf_op jit(solution)/shard_map/transpose | solution.py:151
  308.0 2.0 bitcast_add_fusion
  (10 shorter events, 1.4 us)
Async XLA Ops:
  0.6 2.1 copy-start.4
  2.7 1.7 copy-start.2
  90.2 47.6 %all-to-all-start = ((f32[128,24,150]{2,1,0:T(8,128)}), f32[128,24,150]{2,1,0:T(8,128)S(1)}, u32[]{:S(2)}, u32[]{:S(2)}) async-start(f32[128,24,150]{2,1,0:T(8,128)} %bitcast.34), calls=%async_computation | async-start | bytes 6291456 | tf_op jit(solution)/shard_map/all_to_all | solution.py:302
  137.9 1.7 copy-start
  176.1 46.0 %all-to-all-start.1 = ((f32[128,24,150]{2,1,0:T(8,128)}), f32[128,24,150]{2,1,0:T(8,128)S(1)}, u32[]{:S(2)}, u32[]{:S(2)}) async-start(f32[128,24,150]{2,1,0:T(8,128)} %bitcast.47), calls=%async_computation.1 | async-start | bytes 6291456 | tf_op jit(solution)/shard_map/all_to_all | solution.py:306
  222.1 1.7 copy-start.1
  304.7 3.3 %copy-start.3 = (f32[150,32,128]{2,1,0:T(8,128)S(1)}, f32[150,32,128]{2,1,0:T(8,128)}, u32[]{:S(2)}) copy-start(f32[150,32,128]{2,1,0:T(8,128)} %param.7) | copy-start | bytes 7372804

commit v5 on v2

--- a/solution.py
+++ b/solution.py
@@ -13,43 +13,131 @@
 VMEM = pl.BlockSpec(memory_space=pltpu.VMEM)
 
 
-def slab_pass(rows, src_ref, conduct_ref, field_halo, coef_halo, scales, dst_ref, edges):
+def slab(ref, g, r, rows, group):
+    return ref[g, pl.ds(r, group, stride=rows), :]
+
+
+def edge_pass(rows, src_ref, row_out, col_out):
+    groups, span, lanes = src_ref.shape
+    group = span // rows
+
+    def body(g, carry):
+        col = lax.broadcasted_iota(jnp.int32, (group, rows), 1)
+        left = jnp.zeros((group, rows), jnp.float32)
+        right = jnp.zeros((group, rows), jnp.float32)
+        for r in range(rows):
+            x = slab(src_ref, g, r, rows, group)
+            if r == 0:
+                row_out[0, g] = x
+            if r == rows - 1:
+                row_out[1, g] = x
+            left = jnp.where(col == r, x[:, 0:1], left)
+            right = jnp.where(col == r, x[:, lanes - 1 : lanes], right)
+        col_out[0, g] = left
+        col_out[1, g] = right
+        return carry
+
+    lax.fori_loop(0, groups, body, 0)
+
+
+def neighbours():
+    lon = lax.axis_index("lon")
+    lat = lax.axis_index("lat")
+    n_lon = lax.axis_size("lon")
+    n_lat = lax.axis_size("lat")
+    north = {"lat": (lat + n_lat - 1) % n_lat}
+    south = {"lat": (lat + 1) % n_lat}
+    west = {"lon": (lon + n_lon - 1) % n_lon}
+    east = {"lon": (lon + 1) % n_lon}
+    north_ok = jnp.minimum(lat, 1).astype(jnp.float32)
+    south_ok = jnp.minimum(n_lat - 1 - lat, 1).astype(jnp.float32)
+    return (north, south, west, east), (north_ok, south_ok)
+
+
+def enter(peers):
+    barrier = pltpu.get_barrier_semaphore()
+    for peer in peers:
+        pl.semaphore_signal(barrier, inc=1, device_id=peer, device_id_type=pl.DeviceIdType.MESH)
+    pl.semaphore_wait(barrier, len(peers))
+
+
+def swap(peers, row_edge, col_edge, row_halo, col_halo, send_sem, recv_sem, rd):
+    north, south, west, east = peers
+    plan = [
+        (row_edge.at[rd, 0], row_halo.at[rd, 1], north, 0),
+        (row_edge.at[rd, 1], row_halo.at[rd, 0], south, 1),
+        (col_edge.at[rd, 0], col_halo.at[rd, 1], west, 2),
+        (col_edge.at[rd, 1], col_halo.at[rd, 0], east, 3),
+    ]
+    copies = []
+    for src, dst, peer, k in plan:
+        copy = pltpu.make_async_remote_copy(
+            src_ref=src, dst_ref=dst, send_sem=send_sem.at[rd, k], recv_sem=recv_sem.at[rd, k],
+            device_id=peer, device_id_type=pl.DeviceIdType.MESH,
+        )
+        copy.start()
+        copies.append(copy)
+    for copy in copies:
+        copy.wait()
+
+
+def coef_kernel(rows, c_ref, k_ref, row_edge, col_edge, row_halo, col_halo, send_sem, recv_sem):
+    peers, (north_ok, south_ok) = neighbours()
+    enter(peers)
+    edge_pass(rows, c_ref, row_edge.at[0], col_edge.at[0])
+    swap(peers, row_edge, col_edge, row_halo, col_halo, send_sem, recv_sem, 0)
+    groups, span, lanes = c_ref.shape
+    group = span // rows
+
+    def body(g, carry):
+        lane = lax.broadcasted_iota(jnp.int32, (group, lanes), 1)
+        cw = col_halo[0, 0, g]
+        ce = col_halo[0, 1, g]
+        c_up = row_halo[0, 0, g] * north_ok
+        c_mid = slab(c_ref, g, 0, rows, group)
+        for r in range(rows):
+            if r + 1 < rows:
+                c_dn = slab(c_ref, g, r + 1, rows, group)
+            else:
+                c_dn = row_halo[0, 1, g] * south_ok
+            c_w = jnp.where(lane == 0, cw[:, r : r + 1], pltpu.roll(c_mid, 1, 1))
+            c_e = jnp.where(lane == lanes - 1, ce[:, r : r + 1], pltpu.roll(c_mid, lanes - 1, 1))
+            spot = pl.ds(r, group, stride=rows)
+            k_ref[0, g, spot, :] = jnp.minimum(c_mid, c_up)
+            k_ref[1, g, spot, :] = jnp.minimum(c_mid, c_dn)
+            k_ref[2, g, spot, :] = jnp.minimum(c_mid, c_w)
+            k_ref[3, g, spot, :] = jnp.minimum(c_mid, c_e)
+            c_up, c_mid = c_mid, c_dn
+        return carry
+
+    lax.fori_loop(0, groups, body, 0)
+
+
+def sweep_pass(rows, src_ref, k_ref, row_halo, col_halo, scales, dst_ref, edges):
     groups, span, lanes = src_ref.shape
     group = span // rows
     north_ok, south_ok = scales
-    row_halo, col_halo = field_halo
-    coef_rows, coef_cols = coef_halo
 
     def body(g, carry):
         lane = lax.broadcasted_iota(jnp.int32, (group, lanes), 1)
         col = lax.broadcasted_iota(jnp.int32, (group, rows), 1)
-
-        def slab(ref, r):
-            return ref[g, pl.ds(r, group, stride=rows), :]
-
         vw = col_halo[0, g]
         ve = col_halo[1, g]
-        cw = coef_cols[0, g]
-        ce = coef_cols[1, g]
         left = jnp.zeros((group, rows), jnp.float32)
         right = jnp.zeros((group, rows), jnp.float32)
         x_up = row_halo[0, g] * north_ok
-        c_up = coef_rows[0, g] * north_ok
-        x_mid, c_mid = slab(src_ref, 0), slab(conduct_ref, 0)
+        x_mid = slab(src_ref, g, 0, rows, group)
         for r in range(rows):
             if r + 1 < rows:
-                x_dn, c_dn = slab(src_ref, r + 1), slab(conduct_ref, r + 1)
+                x_dn = slab(src_ref, g, r + 1, rows, group)
             else:
                 x_dn = row_halo[1, g] * south_ok
-                c_dn = coef_rows[1, g] * south_ok
             x_w = jnp.where(lane == 0, vw[:, r : r + 1], pltpu.roll(x_mid, 1, 1))
             x_e = jnp.where(lane == lanes - 1, ve[:, r : r + 1], pltpu.roll(x_mid, lanes - 1, 1))
-            c_w = jnp.where(lane == 0, cw[:, r : r + 1], pltpu.roll(c_mid, 1, 1))
-            c_e = jnp.where(lane == lanes - 1, ce[:, r : r + 1], pltpu.roll(c_mid, lanes - 1, 1))
-            total = jnp.minimum(c_mid, c_up) * (x_up - x_mid)
-            total = total + jnp.minimum(c_mid, c_dn) * (x_dn - x_mid)
-            total = total + jnp.minimum(c_mid, c_w) * (x_w - x_mid)
-            total = total + jnp.minimum(c_mid, c_e) * (x_e - x_mid)
+            total = slab(k_ref.at[0], g, r, rows, group) * (x_up - x_mid)
+            total = total + slab(k_ref.at[1], g, r, rows, group) * (x_dn - x_mid)
+            total = total + slab(k_ref.at[2], g, r, rows, group) * (x_w - x_mid)
+            total = total + slab(k_ref.at[3], g, r, rows, group) * (x_e - x_mid)
             out = x_mid + total
             dst_ref[g, pl.ds(r, group, stride=rows), :] = out
             if edges is not None:
@@ -59,8 +147,7 @@
                     edges[0][1, g] = out
                 left = jnp.where(col == r, out[:, 0:1], left)
                 right = jnp.where(col == r, out[:, lanes - 1 : lanes], right)
-            x_up, c_up = x_mid, c_mid
-            x_mid, c_mid = x_dn, c_dn
+            x_up, x_mid = x_mid, x_dn
         if edges is not None:
             edges[1][0, g] = left
             edges[1][1, g] = right
@@ -69,103 +156,56 @@
     lax.fori_loop(0, groups, body, 0)
 
 
-def edge_pass(rows, src_ref, row_out, col_out):
-    groups, span, lanes = src_ref.shape
-    group = span // rows
-
-    def body(g, carry):
-        col = lax.broadcasted_iota(jnp.int32, (group, rows), 1)
-        left = jnp.zeros((group, rows), jnp.float32)
-        right = jnp.zeros((group, rows), jnp.float32)
-        for r in range(rows):
-            x = src_ref[g, pl.ds(r, group, stride=rows), :]
-            if r == 0:
-                row_out[0, g] = x
-            if r == rows - 1:
-                row_out[1, g] = x
-            left = jnp.where(col == r, x[:, 0:1], left)
-            right = jnp.where(col == r, x[:, lanes - 1 : lanes], right)
-        col_out[0, g] = left
-        col_out[1, g] = right
-        return carry
-
-    lax.fori_loop(0, groups, body, 0)
-
-
-def diffuse_kernel(rows, v_ref, c_ref, out_ref, mid_ref, row_edge, col_edge, row_halo, col_halo,
+def diffuse_kernel(rows, v_ref, k_ref, out_ref, mid_ref, row_edge, col_edge, row_halo, col_halo,
                    send_sem, recv_sem):
-    lon = lax.axis_index("lon")
-    lat = lax.axis_index("lat")
-    n_lon = lax.axis_size("lon")
-    n_lat = lax.axis_size("lat")
-    north = {"lat": (lat + n_lat - 1) % n_lat}
-    south = {"lat": (lat + 1) % n_lat}
-    west = {"lon": (lon + n_lon - 1) % n_lon}
-    east = {"lon": (lon + 1) % n_lon}
-    mesh_id = pl.DeviceIdType.MESH
-
-    barrier = pltpu.get_barrier_semaphore()
-    for peer in (north, south, west, east):
-        pl.semaphore_signal(barrier, inc=1, device_id=peer, device_id_type=mesh_id)
-    pl.semaphore_wait(barrier, 4)
-
-    def exchange(rd):
-        plan = [
-            (row_edge.at[rd, 0], row_halo.at[rd, 1], north, 0),
-            (row_edge.at[rd, 1], row_halo.at[rd, 0], south, 1),
-            (col_edge.at[rd, 0], col_halo.at[rd, 1], west, 2),
-            (col_edge.at[rd, 1], col_halo.at[rd, 0], east, 3),
-        ]
-        copies = []
-        for src, dst, peer, k in plan:
-            copy = pltpu.make_async_remote_copy(
-                src_ref=src, dst_ref=dst, send_sem=send_sem.at[rd, k], recv_sem=recv_sem.at[rd, k],
-                device_id=peer, device_id_type=mesh_id,
-            )
-            copy.start()
-            copies.append(copy)
-        return copies
-
-    edge_pass(rows, c_ref, row_edge.at[0], col_edge.at[0])
-    edge_pass(rows, v_ref, row_edge.at[1], col_edge.at[1])
-    first = exchange(0) + exchange(1)
-    for copy in first:
-        copy.wait()
-    north_ok = jnp.minimum(lat, 1).astype(jnp.float32)
-    south_ok = jnp.minimum(n_lat - 1 - lat, 1).astype(jnp.float32)
-    scales = (north_ok, south_ok)
-    coef_halo = (row_halo.at[0], col_halo.at[0])
-    slab_pass(rows, v_ref, c_ref, (row_halo.at[1], col_halo.at[1]), coef_halo, scales, mid_ref,
-              (row_edge.at[2], col_edge.at[2]))
-    for copy in exchange(2):
-        copy.wait()
-    slab_pass(rows, mid_ref, c_ref, (row_halo.at[2], col_halo.at[2]), coef_halo, scales, out_ref, None)
-
-
-def diffuse(field, conduct_blocks):
+    peers, scales = neighbours()
+    enter(peers)
+    edge_pass(rows, v_ref, row_edge.at[0], col_edge.at[0])
+    swap(peers, row_edge, col_edge, row_halo, col_halo, send_sem, recv_sem, 0)
+    sweep_pass(rows, v_ref, k_ref, row_halo.at[0], col_halo.at[0], scales, mid_ref,
+               (row_edge.at[1], col_edge.at[1]))
+    swap(peers, row_edge, col_edge, row_halo, col_halo, send_sem, recv_sem, 1)
+    sweep_pass(rows, mid_ref, k_ref, row_halo.at[1], col_halo.at[1], scales, out_ref, None)
+
+
+def edge_scratch(rounds, groups, rows, lanes):
+    return [
+        pltpu.VMEM((rounds, 2, groups, GROUP, lanes), jnp.float32),
+        pltpu.VMEM((rounds, 2, groups, GROUP, rows), jnp.float32),
+        pltpu.VMEM((rounds, 2, groups, GROUP, lanes), jnp.float32),
+        pltpu.VMEM((rounds, 2, groups, GROUP, rows), jnp.float32),
+        pltpu.SemaphoreType.DMA((rounds, 4)),
+        pltpu.SemaphoreType.DMA((rounds, 4)),
+    ]
+
+
+def coefficients(conduct_blocks, rows):
+    groups, span, lanes = conduct_blocks.shape
+    return pl.pallas_call(
+        functools.partial(coef_kernel, rows),
+        in_specs=[VMEM],
+        out_specs=VMEM,
+        out_shape=jax.ShapeDtypeStruct((4,) + conduct_blocks.shape, jnp.float32),
+        scratch_shapes=edge_scratch(1, groups, rows, lanes),
+        compiler_params=pltpu.CompilerParams(collective_id=1, has_side_effects=True),
+    )(conduct_blocks)
+
+
+def diffuse(field, coef):
     vals, rows, lanes = field.shape
     groups = vals // GROUP
     blocks = field.reshape(groups, GROUP * rows, lanes)
-    rounds = SWEEPS + 1
     out = pl.pallas_call(
         functools.partial(diffuse_kernel, rows),
         in_specs=[VMEM, VMEM],
         out_specs=VMEM,
         out_shape=jax.ShapeDtypeStruct(blocks.shape, jnp.float32),
-        scratch_shapes=[
-            pltpu.VMEM(blocks.shape, jnp.float32),
-            pltpu.VMEM((rounds, 2, groups, GROUP, lanes), jnp.float32),
-            pltpu.VMEM((rounds, 2, groups, GROUP, rows), jnp.float32),
-            pltpu.VMEM((rounds, 2, groups, GROUP, lanes), jnp.float32),
-            pltpu.VMEM((rounds, 2, groups, GROUP, rows), jnp.float32),
-            pltpu.SemaphoreType.DMA((rounds, 4)),
-            pltpu.SemaphoreType.DMA((rounds, 4)),
-        ],
+        scratch_shapes=[pltpu.VMEM(blocks.shape, jnp.float32)] + edge_scratch(SWEEPS, groups, rows, lanes),
         compiler_params=pltpu.CompilerParams(collective_id=0, has_side_effects=True),
         cost_estimate=pl.CostEstimate(
-            flops=50 * field.size, bytes_accessed=12 * field.size, transcendentals=0
+            flops=30 * field.size, bytes_accessed=28 * field.size, transcendentals=0
         ),
-    )(blocks, conduct_blocks)
+    )(blocks, coef)
     return out.reshape(vals, rows, lanes)
 
 
@@ -296,8 +336,8 @@
     steps = vals // GROUP
     sea_float = sea_mask.astype(jnp.float32)
     conduct = diffusivity * jnp.concatenate([sea_float, sea_float], axis=0)
-    conduct_blocks = conduct.reshape(steps, GROUP * rows, lanes)
-    smooth = diffuse(state, conduct_blocks)
+    coef = coefficients(conduct.reshape(steps, GROUP * rows, lanes), rows)
+    smooth = diffuse(state, coef)
     rows_of = smooth.reshape(vals, cell_count).T
     send_index = send_cols[0]
     outgoing = select_rows(send_index, rows_of, send_index.shape[0])
@@ -307,7 +347,7 @@
     incoming = to_sources(returned)
     adjoint_rows = place_rows(send_index, incoming, cell_count)
     adjoint_field = adjoint_rows.T.reshape(state.shape)
-    product = state + diffuse(adjoint_field, conduct_blocks)
+    product = state + diffuse(adjoint_field, coef)
     return (product, equivalents)
 
 

time: 305 us -> 325 us (1.066)
  Pallas kernels: 186 us -> 206 us
    pallas_call x0 -> x1, Pallas kernels: none -> 27.9 us  [coefficients(): pl.pallas_call(functools.partial(coef_kernel, rows), in_specs=[VMEM], out...]
    pallas_call x2, Pallas kernels: 113 us -> 105 us  [diffuse(): pl.pallas_call(functools.partial(diffuse_kernel, rows), in_specs=[VMEM, V...]
where the time goes in v5:
time: 325 us; the launch traced here: 322 us
  Pallas kernels  206 us (63%)
  waiting for transfers between devices  76.7 us (24%)
  local copies, waits for them, and re-layouts  20.6 us (6%)
  starting transfers between devices  11.5 us (4%)
  other arithmetic  7.13 us (2%)
    pallas_call x2, Pallas kernels, diffuse(): pl.pallas_call(functools.partial(diffuse_kernel, rows), in_specs=[VMEM, V...  105 us
    all_to_all x1, waiting for transfers between devices, to_sources(): lax.all_to_all(returned, ('lon', 'lat'), split_axis=0, concat_axis=0, til...  38.4 us
    all_to_all x1, waiting for transfers between devices, to_owners(): lax.all_to_all(outgoing, ('lon', 'lat'), split_axis=0, concat_axis=0, til...  38.3 us
    pallas_call x1, Pallas kernels, interpolate(): pl.pallas_call(interp_kernel, in_specs=[SMEM, SMEM, VMEM, VMEM], out_spec...  36.4 us
    pallas_call x1, Pallas kernels, coefficients(): pl.pallas_call(functools.partial(coef_kernel, rows), in_specs=[VMEM], out...  27.9 us
    pallas_call x1, Pallas kernels, place_rows(): pl.pallas_call(place_kernel, in_specs=[SMEM, VMEM], out_specs=VMEM, out_s...  21.6 us
    pallas_call x1, Pallas kernels, select_rows(): pl.pallas_call(select_kernel, in_specs=[SMEM, VMEM], out_specs=VMEM, out_...  15.1 us
    unnamed x10, local copies, waits for them, and re-layouts  9.25 us
  transfers between devices with their start and end apart: 2, of which 2 were waited for; matrix products, arithmetic and copies ran while one was open for 2% of the time, Pallas kernels for 0%

profile of v5, /device:TPU:8, one launch (start us, length us, event | category | flops | bytes accessed | tf_op | source)
XLA Modules:
  0.0 322.2 jit_solution(12371832663338967172)
XLA Ops:
  0.6 0.0 copy-start.3
  0.6 1.6 convert_element_type.3
  2.2 0.5 copy-done.3
  2.7 1.9 maximum_multiply_fusion
  4.6 27.9 %shard_map.86.k_ref = f32[4,5,960,128]{3,2,1,0:T(8,128)} custom-call(f32[5,960,128]{2,1,0:T(8,128)} %bitcast.19), custom_call_target="tpu_custom_call" | custom-call | tf_op jit(solution)/shard_map/pallas_call | solution.py:184
  32.5 53.1 %shard_map.87 = f32[5,960,128]{2,1,0:T(8,128)} custom-call(f32[5,960,128]{2,1,0:T(8,128)} %bitcast.17, f32[4,5,960,128]{3,2,1,0:T(8,128)} %shard_map.86.k_ref), custom_call_target="tpu_custom_call" | custom-call | flops 18432000 | bytes 17203200 | tf_op jit(solution)/shard_map/pallas_call | solution.py:198
  85.6 2.5 reshape_reshape.6
  88.1 3.3 %copy.12 = f32[150,4096]{0,1:T(8,128)} copy(f32[150,4096]{1,0:T(8,128)S(1)} %reshape_reshape.6) | data formatting | bytes 4915200 | tf_op jit(solution)/shard_map/reshape;reshape | solution.py:341
  91.4 15.1 %shard_map.88 = f32[3072,150]{1,0:T(8,128)} custom-call(s32[3072]{0:T(1024)} %bitcast.23, f32[4096,150]{1,0:T(8,128)} %bitcast.12), custom_call_target="tpu_custom_call" | custom-call | tf_op jit(solution)/shard_map/pallas_call | solution.py:289
  106.6 6.5 %all-to-all-start = ((f32[128,24,150]{2,1,0:T(8,128)}), f32[128,24,150]{2,1,0:T(8,128)S(1)}, u32[]{:S(2)}, u32[]{:S(2)}) async-start(f32[128,24,150]{2,1,0:T(8,128)} %bitcast.16), calls=%async_computation | async-start | bytes 6291456 | tf_op jit(solution)/shard_map/all_to_all | solution.py:326
  113.1 2.7 copy.13
  115.9 38.3 %all-to-all-done = f32[128,24,150]{2,1,0:T(8,128)S(1)} async-done(((f32[128,24,150]{2,1,0:T(8,128)}), f32[128,24,150]{2,1,0:T(8,128)S(1)}, u32[]{:S(2)}, u32[]{:S(2)}) %all-to-all-start) | async-done | bytes 1843232 | tf_op jit(solution)/shard_map/all_to_all | solution.py:326
  154.1 1.7 copy-done
  155.8 36.4 %shard_map.89 = (f32[2048,150]{1,0:T(8,128)}, f32[3072,150]{1,0:T(8,128)}) custom-call(s32[4,2048]{1,0:T(4,128)} %slot_ref.1, f32[4,2048]{1,0:T(4,128)} %weight_ref.1, f32[3072,150]{1,0:T(8,128)} %bitcast.14, f32[2048,150]{1,0:T(8,128)} %bitcast.20), custom_call_target="tpu_custom_call" | custom-call | tf_op jit(solution)/shard_map/pallas_call | solution.py:310
  192.2 4.9 %all-to-all-start.1 = ((f32[128,24,150]{2,1,0:T(8,128)}), f32[128,24,150]{2,1,0:T(8,128)S(1)}, u32[]{:S(2)}, u32[]{:S(2)}) async-start(f32[128,24,150]{2,1,0:T(8,128)} %bitcast.21), calls=%async_computation.1 | async-start | bytes 6291456 | tf_op jit(solution)/shard_map/all_to_all | solution.py:330
  197.2 2.7 copy.15
  199.9 38.4 %all-to-all-done.1 = f32[128,24,150]{2,1,0:T(8,128)S(1)} async-done(((f32[128,24,150]{2,1,0:T(8,128)}), f32[128,24,150]{2,1,0:T(8,128)S(1)}, u32[]{:S(2)}, u32[]{:S(2)}) %all-to-all-start.1) | async-done | bytes 1843232 | tf_op jit(solution)/shard_map/all_to_all | solution.py:330
  238.3 1.6 copy-done.1
  239.9 21.6 %shard_map.90 = f32[4096,150]{1,0:T(8,128)} custom-call(s32[3072]{0:T(1024)} %bitcast.24, f32[3072,150]{1,0:T(8,128)} %bitcast.15), custom_call_target="tpu_custom_call" | custom-call | tf_op jit(solution)/shard_map/pallas_call | solution.py:298
  261.5 3.7 %copy.14 = f32[150,4096]{1,0:T(8,128)S(1)} copy(f32[150,4096]{0,1:T(8,128)} %bitcast.13) | data formatting | bytes 4915200 | tf_op jit(solution)/shard_map/transpose | solution.py:349
  265.1 1.8 reshape_reshape.7.v_ref
  267.0 51.5 %shard_map.91 = f32[5,960,128]{2,1,0:T(8,128)} custom-call(f32[5,960,128]{2,1,0:T(8,128)} %reshape_reshape.7.v_ref, f32[4,5,960,128]{3,2,1,0:T(8,128)} %shard_map.86.k_ref), custom_call_target="tpu_custom_call" | custom-call | flops 18432000 | bytes 17203200 | tf_op jit(solution)/shard_map/pallas_call | solution.py:198
  318.5 0.0 copy-done.2
  318.5 3.7 %add.3 = f32[150,32,128]{2,1,0:T(8,128)} add(f32[150,32,128]{2,1,0:T(8,128)S(1)} %copy-done.2, f32[150,32,128]{2,1,0:T(8,128)} %bitcast.18) | non-fusion elementwise | flops 614400 | bytes 7372800 | tf_op jit(solution)/shard_map/add | solution.py:350
  (3 shorter events, 0.0 us)
Async XLA Ops:
  0.6 2.1 copy-start.3
  106.6 47.6 %all-to-all-start = ((f32[128,24,150]{2,1,0:T(8,128)}), f32[128,24,150]{2,1,0:T(8,128)S(1)}, u32[]{:S(2)}, u32[]{:S(2)}) async-start(f32[128,24,150]{2,1,0:T(8,128)} %bitcast.16), calls=%async_computation | async-start | bytes 6291456 | tf_op jit(solution)/shard_map/all_to_all | solution.py:326
  154.1 1.7 copy-start
  192.2 46.0 %all-to-all-start.1 = ((f32[128,24,150]{2,1,0:T(8,128)}), f32[128,24,150]{2,1,0:T(8,128)S(1)}, u32[]{:S(2)}, u32[]{:S(2)}) async-start(f32[128,24,150]{2,1,0:T(8,128)} %bitcast.21), calls=%async_computation.1 | async-start | bytes 6291456 | tf_op jit(solution)/shard_map/all_to_all | solution.py:330
  238.3 1.6 copy-start.1
  267.0 51.5 %copy-start.2 = (f32[150,32,128]{2,1,0:T(8,128)S(1)}, f32[150,32,128]{2,1,0:T(8,128)}, u32[]{:S(2)}) copy-start(f32[150,32,128]{2,1,0:T(8,128)} %param.7) | copy-start | bytes 7372804

commit v6 on v2

--- a/solution.py
+++ b/solution.py
@@ -282,12 +282,23 @@
     )(obs_slots, obs_weights, received, precision_rows)
 
 
+def regroup(rows):
+    n_lon = lax.axis_size("lon")
+    n_lat = lax.axis_size("lat")
+    slots, vals = rows.shape
+    chunk = slots // (n_lon * n_lat)
+    blocks = rows.reshape(n_lon, n_lat, chunk, vals)
+    blocks = lax.all_to_all(blocks, "lat", split_axis=1, concat_axis=1, tiled=True)
+    blocks = lax.all_to_all(blocks, "lon", split_axis=0, concat_axis=0, tiled=True)
+    return blocks.reshape(slots, vals)
+
+
 def to_owners(outgoing):
-    return lax.all_to_all(outgoing, ("lon", "lat"), split_axis=0, concat_axis=0, tiled=True)
+    return regroup(outgoing)
 
 
 def to_sources(returned):
-    return lax.all_to_all(returned, ("lon", "lat"), split_axis=0, concat_axis=0, tiled=True)
+    return regroup(returned)
 
 
 def on_device(state, diffusivity, sea_mask, send_cols, obs_slots, obs_weights, obs_precision):

time: 305 us -> 406 us (1.33)
  blocking collectives: 0 us -> 78.3 us
  local copies, waits for them, and re-layouts: 20.8 us -> 29 us
  Pallas kernels: 186 us -> 193 us
  starting transfers between devices: 11.5 us -> 17.1 us
    all_to_all x0 -> x2, blocking collectives: none -> 78.3 us  [regroup(): lax.all_to_all(blocks, 'lat', split_axis=1, concat_axis=1, tiled=True)]
    pallas_call x2, Pallas kernels: 113 us -> 120 us  [diffuse(): pl.pallas_call(functools.partial(diffuse_kernel, rows), in_specs=[VMEM, V...]
    all_to_all x2, starting transfers between devices: 11.5 us -> 17.1 us  [regroup(): lax.all_to_all(blocks, 'lon', split_axis=0, concat_axis=0, tiled=True)]
    reshape x0 -> x2, local copies, waits for them, and re-layouts: none -> 4.38 us  [regroup(): blocks = rows.reshape(n_lon, n_lat, chunk, vals)]
  transfers between devices with their start and end apart: 2 -> 2, of which waited for: 2 -> 2; matrix products, arithmetic and copies ran while one was open for 2% -> 1% of each run, Pallas kernels for 0% -> 0%
where the time goes in v6:
time: 406 us; the launch traced here: 403 us
  Pallas kernels  193 us (48%)
  blocking collectives  78.3 us (19%)
  waiting for transfers between devices  77.7 us (19%)
  local copies, waits for them, and re-layouts  29 us (7%)
  starting transfers between devices  17.1 us (4%)
  other arithmetic  7.13 us (2%)
    pallas_call x2, Pallas kernels, diffuse(): pl.pallas_call(functools.partial(diffuse_kernel, rows), in_specs=[VMEM, V...  120 us
    all_to_all x2, blocking collectives, regroup(): lax.all_to_all(blocks, 'lat', split_axis=1, concat_axis=1, tiled=True)  78.3 us
    all_to_all x2, waiting for transfers between devices, regroup(): lax.all_to_all(blocks, 'lon', split_axis=0, concat_axis=0, tiled=True)  77.7 us
    pallas_call x1, Pallas kernels, interpolate(): pl.pallas_call(interp_kernel, in_specs=[SMEM, SMEM, VMEM, VMEM], out_spec...  36.5 us
    pallas_call x1, Pallas kernels, place_rows(): pl.pallas_call(place_kernel, in_specs=[SMEM, VMEM], out_specs=VMEM, out_s...  21.4 us
    all_to_all x2, starting transfers between devices, regroup(): lax.all_to_all(blocks, 'lon', split_axis=0, concat_axis=0, tiled=True)  17.1 us
    pallas_call x1, Pallas kernels, select_rows(): pl.pallas_call(select_kernel, in_specs=[SMEM, VMEM], out_specs=VMEM, out_...  15.2 us
    unnamed x10, local copies, waits for them, and re-layouts  9.28 us
  transfers between devices with their start and end apart: 2, of which 2 were waited for; matrix products, arithmetic and copies ran while one was open for 1% of the time, Pallas kernels for 0%

profile of v6, /device:TPU:8, one launch (start us, length us, event | category | flops | bytes accessed | tf_op | source)
XLA Modules:
  0.0 402.9 jit_solution(13319984781142834301)
XLA Ops:
  2.7 1.9 maximum_multiply_fusion
  4.6 58.7 %shard_map.86 = f32[5,960,128]{2,1,0:T(8,128)} custom-call(f32[5,960,128]{2,1,0:T(8,128)} %bitcast.19, f32[5,960,128]{2,1,0:T(8,128)} %bitcast.12), custom_call_target="tpu_custom_call" | custom-call | flops 30720000 | bytes 7372800 | tf_op jit(solution)/shard_map/pallas_call | solution.py:150
  63.2 2.5 reshape_reshape.6
  65.8 3.3 copy.24
  69.0 15.2 %shard_map.87 = f32[3072,150]{1,0:T(8,128)} custom-call(s32[3072]{0:T(1024)} %bitcast.24, f32[4096,150]{1,0:T(8,128)} %bitcast.14), custom_call_target="tpu_custom_call" | custom-call | tf_op jit(solution)/shard_map/pallas_call | solution.py:249
  84.2 2.2 copy.25
  86.4 37.2 %all_to_all.20 = f32[16,8,24,150]{3,2,0,1:T(8,128)S(1)} all-to-all(f32[16,8,24,150]{3,2,0,1:T(8,128)S(1)} %copy.25), channel_id=1, replica_groups=mesh['lon'=16,'lat'=8] {'lat'}, dimensions={1} | all-to-all | bytes 3686400 | tf_op jit(solution)/shard_map/all_to_all | solution.py:291
  123.7 2.0 copy.26
  125.7 7.0 %all-to-all-start.1 = ((f32[16,8,24,150]{3,2,1,0:T(8,128)}), f32[16,8,24,150]{3,2,1,0:T(8,128)S(1)}, u32[]{:S(2)}, u32[]{:S(2)}) async-start(f32[16,8,24,150]{3,2,1,0:T(8,128)} %copy.26), calls=%async_computation.1 | async-start | bytes 6291456 | tf_op jit(solution)/shard_map/all_to_all | solution.py:292
  132.7 2.8 copy.27
  135.5 38.8 %all-to-all-done.1 = f32[16,8,24,150]{3,2,1,0:T(8,128)S(1)} async-done(((f32[16,8,24,150]{3,2,1,0:T(8,128)}), f32[16,8,24,150]{3,2,1,0:T(8,128)S(1)}, u32[]{:S(2)}, u32[]{:S(2)}) %all-to-all-start.1) | async-done | bytes 1843232 | tf_op jit(solution)/shard_map/all_to_all | solution.py:292
  175.9 36.5 %shard_map.88 = (f32[2048,150]{1,0:T(8,128)}, f32[3072,150]{1,0:T(8,128)}) custom-call(s32[4,2048]{1,0:T(4,128)} %slot_ref.1, f32[4,2048]{1,0:T(4,128)} %weight_ref.1, f32[3072,150]{1,0:T(8,128)} %bitcast.16, f32[2048,150]{1,0:T(8,128)} %bitcast.21), custom_call_target="tpu_custom_call" | custom-call | tf_op jit(solution)/shard_map/pallas_call | solution.py:270
  212.4 2.2 copy.28
  214.6 41.1 %all_to_all.21 = f32[16,8,24,150]{3,2,0,1:T(8,128)S(1)} all-to-all(f32[16,8,24,150]{3,2,0,1:T(8,128)S(1)} %copy.28), channel_id=1, replica_groups=mesh['lon'=16,'lat'=8] {'lat'}, dimensions={1} | all-to-all | bytes 3686400 | tf_op jit(solution)/shard_map/all_to_all | solution.py:291
  255.6 2.0 copy.29
  257.6 10.1 %all-to-all-start.3 = ((f32[16,8,24,150]{3,2,1,0:T(8,128)}), f32[16,8,24,150]{3,2,1,0:T(8,128)S(1)}, u32[]{:S(2)}, u32[]{:S(2)}) async-start(f32[16,8,24,150]{3,2,1,0:T(8,128)} %copy.29), calls=%async_computation.3 | async-start | bytes 6291456 | tf_op jit(solution)/shard_map/all_to_all | solution.py:292
  267.7 2.7 copy.31
  270.4 38.9 %all-to-all-done.3 = f32[16,8,24,150]{3,2,1,0:T(8,128)S(1)} async-done(((f32[16,8,24,150]{3,2,1,0:T(8,128)}), f32[16,8,24,150]{3,2,1,0:T(8,128)S(1)}, u32[]{:S(2)}, u32[]{:S(2)}) %all-to-all-start.3) | async-done | bytes 1843232 | tf_op jit(solution)/shard_map/all_to_all | solution.py:292
  309.3 1.7 copy-done.1
  311.0 21.4 %shard_map.89 = f32[4096,150]{1,0:T(8,128)} custom-call(s32[3072]{0:T(1024)} %bitcast.25, f32[3072,150]{1,0:T(8,128)} %bitcast.17), custom_call_target="tpu_custom_call" | custom-call | tf_op jit(solution)/shard_map/pallas_call | solution.py:258
  332.4 3.7 copy.30
  336.1 1.8 reshape_reshape.7.v_ref
  337.9 61.3 %shard_map.90 = f32[5,960,128]{2,1,0:T(8,128)} custom-call(f32[5,960,128]{2,1,0:T(8,128)} %reshape_reshape.7.v_ref, f32[5,960,128]{2,1,0:T(8,128)} %bitcast.13), custom_call_target="tpu_custom_call" | custom-call | flops 30720000 | bytes 7372800 | tf_op jit(solution)/shard_map/pallas_call | solution.py:150
  399.2 3.7 add.3
  (8 shorter events, 3.7 us)
Async XLA Ops:
  0.6 2.1 copy-start.3
  125.7 48.6 %all-to-all-start.1 = ((f32[16,8,24,150]{3,2,1,0:T(8,128)}), f32[16,8,24,150]{3,2,1,0:T(8,128)S(1)}, u32[]{:S(2)}, u32[]{:S(2)}) async-start(f32[16,8,24,150]{3,2,1,0:T(8,128)} %copy.26), calls=%async_computation.1 | async-start | bytes 6291456 | tf_op jit(solution)/shard_map/all_to_all | solution.py:292
  174.3 1.6 copy-start
  257.6 51.7 %all-to-all-start.3 = ((f32[16,8,24,150]{3,2,1,0:T(8,128)}), f32[16,8,24,150]{3,2,1,0:T(8,128)S(1)}, u32[]{:S(2)}, u32[]{:S(2)}) async-start(f32[16,8,24,150]{3,2,1,0:T(8,128)} %copy.29), calls=%async_computation.3 | async-start | bytes 6291456 | tf_op jit(solution)/shard_map/all_to_all | solution.py:292
  309.3 1.7 copy-start.1
  337.9 61.3 %copy-start.2 = (f32[150,32,128]{2,1,0:T(8,128)S(1)}, f32[150,32,128]{2,1,0:T(8,128)}, u32[]{:S(2)}) copy-start(f32[150,32,128]{2,1,0:T(8,128)} %param.7) | copy-start | bytes 7372804

commit v7 on v2

--- a/solution.py
+++ b/solution.py
@@ -13,12 +13,40 @@
 VMEM = pl.BlockSpec(memory_space=pltpu.VMEM)
 
 
-def slab_pass(rows, src_ref, conduct_ref, field_halo, coef_halo, scales, dst_ref, edges):
+def coef_pass(rows, c_ref, coef_halo, scales, k_ref):
+    groups, span, lanes = c_ref.shape
+    group = span // rows
+    north_ok, south_ok = scales
+    coef_rows, coef_cols = coef_halo
+
+    def body(g, carry):
+        lane = lax.broadcasted_iota(jnp.int32, (group, lanes), 1)
+        cw = coef_cols[0, g]
+        ce = coef_cols[1, g]
+        c_up = coef_rows[0, g] * north_ok
+        c_mid = c_ref[g, pl.ds(0, group, stride=rows), :]
+        for r in range(rows):
+            if r + 1 < rows:
+                c_dn = c_ref[g, pl.ds(r + 1, group, stride=rows), :]
+            else:
+                c_dn = coef_rows[1, g] * south_ok
+            c_w = jnp.where(lane == 0, cw[:, r : r + 1], pltpu.roll(c_mid, 1, 1))
+            c_e = jnp.where(lane == lanes - 1, ce[:, r : r + 1], pltpu.roll(c_mid, lanes - 1, 1))
+            k_ref[0, g, r] = jnp.minimum(c_mid, c_up)
+            k_ref[1, g, r] = jnp.minimum(c_mid, c_dn)
+            k_ref[2, g, r] = jnp.minimum(c_mid, c_w)
+            k_ref[3, g, r] = jnp.minimum(c_mid, c_e)
+            c_up, c_mid = c_mid, c_dn
+        return carry
+
+    lax.fori_loop(0, groups, body, 0)
+
+
+def slab_pass(rows, src_ref, k_ref, field_halo, scales, dst_ref, edges):
     groups, span, lanes = src_ref.shape
     group = span // rows
     north_ok, south_ok = scales
     row_halo, col_halo = field_halo
-    coef_rows, coef_cols = coef_halo
 
     def body(g, carry):
         lane = lax.broadcasted_iota(jnp.int32, (group, lanes), 1)
@@ -29,27 +57,21 @@
 
         vw = col_halo[0, g]
         ve = col_halo[1, g]
-        cw = coef_cols[0, g]
-        ce = coef_cols[1, g]
         left = jnp.zeros((group, rows), jnp.float32)
         right = jnp.zeros((group, rows), jnp.float32)
         x_up = row_halo[0, g] * north_ok
-        c_up = coef_rows[0, g] * north_ok
-        x_mid, c_mid = slab(src_ref, 0), slab(conduct_ref, 0)
+        x_mid = slab(src_ref, 0)
         for r in range(rows):
             if r + 1 < rows:
-                x_dn, c_dn = slab(src_ref, r + 1), slab(conduct_ref, r + 1)
+                x_dn = slab(src_ref, r + 1)
             else:
                 x_dn = row_halo[1, g] * south_ok
-                c_dn = coef_rows[1, g] * south_ok
             x_w = jnp.where(lane == 0, vw[:, r : r + 1], pltpu.roll(x_mid, 1, 1))
             x_e = jnp.where(lane == lanes - 1, ve[:, r : r + 1], pltpu.roll(x_mid, lanes - 1, 1))
-            c_w = jnp.where(lane == 0, cw[:, r : r + 1], pltpu.roll(c_mid, 1, 1))
-            c_e = jnp.where(lane == lanes - 1, ce[:, r : r + 1], pltpu.roll(c_mid, lanes - 1, 1))
-            total = jnp.minimum(c_mid, c_up) * (x_up - x_mid)
-            total = total + jnp.minimum(c_mid, c_dn) * (x_dn - x_mid)
-            total = total + jnp.minimum(c_mid, c_w) * (x_w - x_mid)
-            total = total + jnp.minimum(c_mid, c_e) * (x_e - x_mid)
+            total = k_ref[0, g, r] * (x_up - x_mid)
+            total = total + k_ref[1, g, r] * (x_dn - x_mid)
+            total = total + k_ref[2, g, r] * (x_w - x_mid)
+            total = total + k_ref[3, g, r] * (x_e - x_mid)
             out = x_mid + total
             dst_ref[g, pl.ds(r, group, stride=rows), :] = out
             if edges is not None:
@@ -59,8 +81,7 @@
                     edges[0][1, g] = out
                 left = jnp.where(col == r, out[:, 0:1], left)
                 right = jnp.where(col == r, out[:, lanes - 1 : lanes], right)
-            x_up, c_up = x_mid, c_mid
-            x_mid, c_mid = x_dn, c_dn
+            x_up, x_mid = x_mid, x_dn
         if edges is not None:
             edges[1][0, g] = left
             edges[1][1, g] = right
@@ -92,8 +113,8 @@
     lax.fori_loop(0, groups, body, 0)
 
 
-def diffuse_kernel(rows, v_ref, c_ref, out_ref, mid_ref, row_edge, col_edge, row_halo, col_halo,
-                   send_sem, recv_sem):
+def diffuse_kernel(rows, v_ref, c_ref, out_ref, mid_ref, k_ref, row_edge, col_edge, row_halo,
+                   col_halo, send_sem, recv_sem):
     lon = lax.axis_index("lon")
     lat = lax.axis_index("lat")
     n_lon = lax.axis_size("lon")
@@ -134,12 +155,12 @@
     north_ok = jnp.minimum(lat, 1).astype(jnp.float32)
     south_ok = jnp.minimum(n_lat - 1 - lat, 1).astype(jnp.float32)
     scales = (north_ok, south_ok)
-    coef_halo = (row_halo.at[0], col_halo.at[0])
-    slab_pass(rows, v_ref, c_ref, (row_halo.at[1], col_halo.at[1]), coef_halo, scales, mid_ref,
+    coef_pass(rows, c_ref, (row_halo.at[0], col_halo.at[0]), scales, k_ref)
+    slab_pass(rows, v_ref, k_ref, (row_halo.at[1], col_halo.at[1]), scales, mid_ref,
               (row_edge.at[2], col_edge.at[2]))
     for copy in exchange(2):
         copy.wait()
-    slab_pass(rows, mid_ref, c_ref, (row_halo.at[2], col_halo.at[2]), coef_halo, scales, out_ref, None)
+    slab_pass(rows, mid_ref, k_ref, (row_halo.at[2], col_halo.at[2]), scales, out_ref, None)
 
 
 def diffuse(field, conduct_blocks):
@@ -154,6 +175,7 @@
         out_shape=jax.ShapeDtypeStruct(blocks.shape, jnp.float32),
         scratch_shapes=[
             pltpu.VMEM(blocks.shape, jnp.float32),
+            pltpu.VMEM((4, groups, rows, GROUP, lanes), jnp.float32),
             pltpu.VMEM((rounds, 2, groups, GROUP, lanes), jnp.float32),
             pltpu.VMEM((rounds, 2, groups, GROUP, rows), jnp.float32),
             pltpu.VMEM((rounds, 2, groups, GROUP, lanes), jnp.float32),

time: 305 us -> 301 us (0.987)
  Pallas kernels: 186 us -> 182 us
    pallas_call x2, Pallas kernels: 113 us -> 109 us  [diffuse(): pl.pallas_call(functools.partial(diffuse_kernel, rows), in_specs=[VMEM, V...]
where the time goes in v7:
time: 301 us; the launch traced here: 298 us
  Pallas kernels  182 us (60%)
  waiting for transfers between devices  76.7 us (25%)
  local copies, waits for them, and re-layouts  20.8 us (7%)
  starting transfers between devices  11.5 us (4%)
  other arithmetic  7.13 us (2%)
    pallas_call x2, Pallas kernels, diffuse(): pl.pallas_call(functools.partial(diffuse_kernel, rows), in_specs=[VMEM, V...  109 us
    all_to_all x1, waiting for transfers between devices, to_sources(): lax.all_to_all(returned, ('lon', 'lat'), split_axis=0, concat_axis=0, til...  38.4 us
    all_to_all x1, waiting for transfers between devices, to_owners(): lax.all_to_all(outgoing, ('lon', 'lat'), split_axis=0, concat_axis=0, til...  38.2 us
    pallas_call x1, Pallas kernels, interpolate(): pl.pallas_call(interp_kernel, in_specs=[SMEM, SMEM, VMEM, VMEM], out_spec...  36.4 us
    pallas_call x1, Pallas kernels, place_rows(): pl.pallas_call(place_kernel, in_specs=[SMEM, VMEM], out_specs=VMEM, out_s...  21.4 us
    pallas_call x1, Pallas kernels, select_rows(): pl.pallas_call(select_kernel, in_specs=[SMEM, VMEM], out_specs=VMEM, out_...  15.2 us
    unnamed x10, local copies, waits for them, and re-layouts  9.31 us
    all_to_all x1, starting transfers between devices, to_owners(): lax.all_to_all(outgoing, ('lon', 'lat'), split_axis=0, concat_axis=0, til...  6.59 us
  transfers between devices with their start and end apart: 2, of which 2 were waited for; matrix products, arithmetic and copies ran while one was open for 2% of the time, Pallas kernels for 0%

profile of v7, /device:TPU:8, one launch (start us, length us, event | category | flops | bytes accessed | tf_op | source)
XLA Modules:
  0.0 298.5 jit_solution(11117207430343875724)
XLA Ops:
  0.6 0.0 copy-start.3
  0.6 1.6 convert_element_type.3
  2.2 0.5 copy-done.3
  2.7 1.9 maximum_multiply_fusion
  4.6 56.5 %shard_map.86 = f32[5,960,128]{2,1,0:T(8,128)} custom-call(f32[5,960,128]{2,1,0:T(8,128)} %bitcast.19, f32[5,960,128]{2,1,0:T(8,128)} %bitcast.12), custom_call_target="tpu_custom_call" | custom-call | flops 30720000 | bytes 7372800 | tf_op jit(solution)/shard_map/pallas_call | solution.py:171
  61.1 2.5 reshape_reshape.6
  63.6 3.4 %copy.12 = f32[150,4096]{0,1:T(8,128)} copy(f32[150,4096]{1,0:T(8,128)S(1)} %reshape_reshape.6) | data formatting | bytes 4915200 | tf_op jit(solution)/shard_map/reshape;reshape | solution.py:323
  67.0 15.2 %shard_map.87 = f32[3072,150]{1,0:T(8,128)} custom-call(s32[3072]{0:T(1024)} %bitcast.24, f32[4096,150]{1,0:T(8,128)} %bitcast.14), custom_call_target="tpu_custom_call" | custom-call | tf_op jit(solution)/shard_map/pallas_call | solution.py:271
  82.2 6.6 %all-to-all-start = ((f32[128,24,150]{2,1,0:T(8,128)}), f32[128,24,150]{2,1,0:T(8,128)S(1)}, u32[]{:S(2)}, u32[]{:S(2)}) async-start(f32[128,24,150]{2,1,0:T(8,128)} %bitcast.18), calls=%async_computation | async-start | bytes 6291456 | tf_op jit(solution)/shard_map/all_to_all | solution.py:308
  88.8 2.8 copy.13
  91.6 38.2 %all-to-all-done = f32[128,24,150]{2,1,0:T(8,128)S(1)} async-done(((f32[128,24,150]{2,1,0:T(8,128)}), f32[128,24,150]{2,1,0:T(8,128)S(1)}, u32[]{:S(2)}, u32[]{:S(2)}) %all-to-all-start) | async-done | bytes 1843232 | tf_op jit(solution)/shard_map/all_to_all | solution.py:308
  129.9 0.0 copy-start
  129.9 1.7 copy-done
  131.5 36.4 %shard_map.88 = (f32[2048,150]{1,0:T(8,128)}, f32[3072,150]{1,0:T(8,128)}) custom-call(s32[4,2048]{1,0:T(4,128)} %slot_ref.1, f32[4,2048]{1,0:T(4,128)} %weight_ref.1, f32[3072,150]{1,0:T(8,128)} %bitcast.16, f32[2048,150]{1,0:T(8,128)} %bitcast.21), custom_call_target="tpu_custom_call" | custom-call | tf_op jit(solution)/shard_map/pallas_call | solution.py:292
  167.9 4.9 %all-to-all-start.1 = ((f32[128,24,150]{2,1,0:T(8,128)}), f32[128,24,150]{2,1,0:T(8,128)S(1)}, u32[]{:S(2)}, u32[]{:S(2)}) async-start(f32[128,24,150]{2,1,0:T(8,128)} %bitcast.22), calls=%async_computation.1 | async-start | bytes 6291456 | tf_op jit(solution)/shard_map/all_to_all | solution.py:312
  172.9 2.7 copy.15
  175.6 38.4 %all-to-all-done.1 = f32[128,24,150]{2,1,0:T(8,128)S(1)} async-done(((f32[128,24,150]{2,1,0:T(8,128)}), f32[128,24,150]{2,1,0:T(8,128)S(1)}, u32[]{:S(2)}, u32[]{:S(2)}) %all-to-all-start.1) | async-done | bytes 1843232 | tf_op jit(solution)/shard_map/all_to_all | solution.py:312
  214.0 1.7 copy-done.1
  215.7 21.4 %shard_map.89 = f32[4096,150]{1,0:T(8,128)} custom-call(s32[3072]{0:T(1024)} %bitcast.25, f32[3072,150]{1,0:T(8,128)} %bitcast.17), custom_call_target="tpu_custom_call" | custom-call | tf_op jit(solution)/shard_map/pallas_call | solution.py:280
  237.1 3.7 %copy.14 = f32[150,4096]{1,0:T(8,128)S(1)} copy(f32[150,4096]{0,1:T(8,128)} %bitcast.15) | data formatting | bytes 4915200 | tf_op jit(solution)/shard_map/transpose | solution.py:331
  240.7 1.8 reshape_reshape.7.v_ref
  242.6 52.2 %shard_map.90 = f32[5,960,128]{2,1,0:T(8,128)} custom-call(f32[5,960,128]{2,1,0:T(8,128)} %reshape_reshape.7.v_ref, f32[5,960,128]{2,1,0:T(8,128)} %bitcast.13), custom_call_target="tpu_custom_call" | custom-call | flops 30720000 | bytes 7372800 | tf_op jit(solution)/shard_map/pallas_call | solution.py:171
  294.8 0.0 copy-done.2
  294.8 3.7 %add.3 = f32[150,32,128]{2,1,0:T(8,128)} add(f32[150,32,128]{2,1,0:T(8,128)S(1)} %copy-done.2, f32[150,32,128]{2,1,0:T(8,128)} %bitcast.20) | non-fusion elementwise | flops 614400 | bytes 7372800 | tf_op jit(solution)/shard_map/add | solution.py:332
  (2 shorter events, 0.0 us)
Async XLA Ops:
  0.6 2.1 copy-start.3
  82.2 47.6 %all-to-all-start = ((f32[128,24,150]{2,1,0:T(8,128)}), f32[128,24,150]{2,1,0:T(8,128)S(1)}, u32[]{:S(2)}, u32[]{:S(2)}) async-start(f32[128,24,150]{2,1,0:T(8,128)} %bitcast.18), calls=%async_computation | async-start | bytes 6291456 | tf_op jit(solution)/shard_map/all_to_all | solution.py:308
  129.9 1.7 copy-start
  167.9 46.0 %all-to-all-start.1 = ((f32[128,24,150]{2,1,0:T(8,128)}), f32[128,24,150]{2,1,0:T(8,128)S(1)}, u32[]{:S(2)}, u32[]{:S(2)}) async-start(f32[128,24,150]{2,1,0:T(8,128)} %bitcast.22), calls=%async_computation.1 | async-start | bytes 6291456 | tf_op jit(solution)/shard_map/all_to_all | solution.py:312
  214.0 1.7 copy-start.1
  242.6 52.2 %copy-start.2 = (f32[150,32,128]{2,1,0:T(8,128)S(1)}, f32[150,32,128]{2,1,0:T(8,128)}, u32[]{:S(2)}) copy-start(f32[150,32,128]{2,1,0:T(8,128)} %param.7) | copy-start | bytes 7372804

commit v8 on v7

--- a/solution.py
+++ b/solution.py
@@ -223,14 +223,18 @@
         part[...] = jnp.zeros_like(part)
 
     def body(t, carry):
-        for i, part in enumerate(parts):
+        spots, rows = [], []
+        for i in range(len(parts)):
             q = t * len(parts) + i
             target = index_ref[q]
-            row = load_row(rows_ref, q)
-            add_row(part, jnp.minimum(target, cells - 1), jnp.where(target < cells, row, 0.0))
-        return carry
-
-    lax.fori_loop(0, rows_ref.shape[0] // len(parts), body, 0, unroll=2)
+            spots.append(pl.ds(jnp.minimum(target, cells - 1), 1))
+            rows.append(jnp.where(target < cells, load_row(rows_ref, q), 0.0))
+        sums = [part[spot, :] + row for part, spot, row in zip(parts, spots, rows)]
+        for part, spot, value in zip(parts, spots, sums):
+            part[spot, :] = value
+        return carry
+
+    lax.fori_loop(0, rows_ref.shape[0] // len(parts), body, 0)
     total = parts[0][...]
     for part in parts[1:]:
         total = total + part[...]
@@ -241,23 +245,34 @@
     taps, obs_count = slot_ref.shape
     width = equiv_ref.shape[1]
     sub = lax.broadcasted_iota(jnp.int32, (8, width), 0)
+    pair = len(parts) // taps
     for part in parts:
         part[...] = jnp.zeros_like(part)
 
     def body(t, carry):
+        slots = [[slot_ref[k, t * 8 + i] for k in range(taps)] for i in range(8)]
+        weights = [[weight_ref[k, t * 8 + i] for k in range(taps)] for i in range(8)]
+        picked = [[load_row(received_ref, slots[i][k]) for k in range(taps)] for i in range(8)]
+        precision = [load_row(precision_ref, t * 8 + i) for i in range(8)]
         tile = jnp.zeros((8, width), jnp.float32)
+        weighted = []
         for i in range(8):
-            j = t * 8 + i
-            slots = [slot_ref[k, j] for k in range(taps)]
-            weights = [weight_ref[k, j] for k in range(taps)]
-            total = load_row(received_ref, slots[0]) * weights[0]
+            total = picked[i][0] * weights[i][0]
             for k in range(1, taps):
-                total = total + load_row(received_ref, slots[k]) * weights[k]
+                total = total + picked[i][k] * weights[i][k]
             tile = jnp.where(sub == i, jnp.broadcast_to(total, (8, width)), tile)
-            weighted = load_row(precision_ref, j) * total
-            for k in range(taps):
-                add_row(parts[(i % 2) * taps + k], slots[k], weighted * weights[k])
+            weighted.append(precision[i] * total)
         equiv_ref[pl.ds(pl.multiple_of(t * 8, 8), 8), :] = tile
+        for first in range(0, 8, pair):
+            batch = [(i, k) for i in range(first, first + pair) for k in range(taps)]
+            spots = [pl.ds(slots[i][k], 1) for i, k in batch]
+            owners = [parts[(i - first) * taps + k] for i, k in batch]
+            sums = [
+                owner[spot, :] + weighted[i] * weights[i][k]
+                for owner, spot, (i, k) in zip(owners, spots, batch)
+            ]
+            for owner, spot, value in zip(owners, spots, sums):
+                owner[spot, :] = value
         return carry
 
     lax.fori_loop(0, obs_count // 8, body, 0)
@@ -282,7 +297,7 @@
         in_specs=[SMEM, VMEM],
         out_specs=VMEM,
         out_shape=jax.ShapeDtypeStruct((cells, rows.shape[1]), jnp.float32),
-        scratch_shapes=[pltpu.VMEM((cells, rows.shape[1]), jnp.float32) for _ in range(4)],
+        scratch_shapes=[pltpu.VMEM((cells, rows.shape[1]), jnp.float32) for _ in range(8)],
         compiler_params=pltpu.CompilerParams(vmem_limit_bytes=60 * 1024 * 1024),
     )(index, rows)
 

time: 301 us -> 321 us (1.066)
  Pallas kernels: 182 us -> 202 us
    pallas_call x1, Pallas kernels: 36.4 us -> 55.7 us  [interpolate(): pl.pallas_call(interp_kernel, in_specs=[SMEM, SMEM, VMEM, VMEM], out_spec...]
where the time goes in v8:
time: 321 us; the launch traced here: 319 us
  Pallas kernels  202 us (63%)
  waiting for transfers between devices  76.7 us (24%)
  local copies, waits for them, and re-layouts  20.8 us (6%)
  starting transfers between devices  11.5 us (4%)
  other arithmetic  7.13 us (2%)
    pallas_call x2, Pallas kernels, diffuse(): pl.pallas_call(functools.partial(diffuse_kernel, rows), in_specs=[VMEM, V...  109 us
    pallas_call x1, Pallas kernels, interpolate(): pl.pallas_call(interp_kernel, in_specs=[SMEM, SMEM, VMEM, VMEM], out_spec...  55.7 us
    all_to_all x1, waiting for transfers between devices, to_sources(): lax.all_to_all(returned, ('lon', 'lat'), split_axis=0, concat_axis=0, til...  38.4 us
    all_to_all x1, waiting for transfers between devices, to_owners(): lax.all_to_all(outgoing, ('lon', 'lat'), split_axis=0, concat_axis=0, til...  38.2 us
    pallas_call x1, Pallas kernels, place_rows(): pl.pallas_call(place_kernel, in_specs=[SMEM, VMEM], out_specs=VMEM, out_s...  22.4 us
    pallas_call x1, Pallas kernels, select_rows(): pl.pallas_call(select_kernel, in_specs=[SMEM, VMEM], out_specs=VMEM, out_...  15.2 us
    unnamed x10, local copies, waits for them, and re-layouts  9.31 us
    all_to_all x1, starting transfers between devices, to_owners(): lax.all_to_all(outgoing, ('lon', 'lat'), split_axis=0, concat_axis=0, til...  6.59 us
  transfers between devices with their start and end apart: 2, of which 2 were waited for; matrix products, arithmetic and copies ran while one was open for 2% of the time, Pallas kernels for 0%

profile of v8, /device:TPU:8, one launch (start us, length us, event | category | flops | bytes accessed | tf_op | source)
XLA Modules:
  0.0 318.7 jit_solution(12267458561918469450)
XLA Ops:
  0.6 0.0 copy-start.3
  0.6 1.6 convert_element_type.3
  2.2 0.5 copy-done.3
  2.7 1.9 maximum_multiply_fusion
  4.6 56.5 %shard_map.86 = f32[5,960,128]{2,1,0:T(8,128)} custom-call(f32[5,960,128]{2,1,0:T(8,128)} %bitcast.19, f32[5,960,128]{2,1,0:T(8,128)} %bitcast.12), custom_call_target="tpu_custom_call" | custom-call | flops 30720000 | bytes 7372800 | tf_op jit(solution)/shard_map/pallas_call | solution.py:171
  61.1 2.5 reshape_reshape.6
  63.6 3.4 %copy.12 = f32[150,4096]{0,1:T(8,128)} copy(f32[150,4096]{1,0:T(8,128)S(1)} %reshape_reshape.6) | data formatting | bytes 4915200 | tf_op jit(solution)/shard_map/reshape;reshape | solution.py:338
  67.0 15.2 %shard_map.87 = f32[3072,150]{1,0:T(8,128)} custom-call(s32[3072]{0:T(1024)} %bitcast.24, f32[4096,150]{1,0:T(8,128)} %bitcast.14), custom_call_target="tpu_custom_call" | custom-call | tf_op jit(solution)/shard_map/pallas_call | solution.py:286
  82.2 6.6 %all-to-all-start = ((f32[128,24,150]{2,1,0:T(8,128)}), f32[128,24,150]{2,1,0:T(8,128)S(1)}, u32[]{:S(2)}, u32[]{:S(2)}) async-start(f32[128,24,150]{2,1,0:T(8,128)} %bitcast.18), calls=%async_computation | async-start | bytes 6291456 | tf_op jit(solution)/shard_map/all_to_all | solution.py:323
  88.8 2.8 copy.13
  91.6 38.2 %all-to-all-done = f32[128,24,150]{2,1,0:T(8,128)S(1)} async-done(((f32[128,24,150]{2,1,0:T(8,128)}), f32[128,24,150]{2,1,0:T(8,128)S(1)}, u32[]{:S(2)}, u32[]{:S(2)}) %all-to-all-start) | async-done | bytes 1843232 | tf_op jit(solution)/shard_map/all_to_all | solution.py:323
  129.9 0.0 copy-start
  129.9 1.7 copy-done
  131.5 55.7 %shard_map.88 = (f32[2048,150]{1,0:T(8,128)}, f32[3072,150]{1,0:T(8,128)}) custom-call(s32[4,2048]{1,0:T(4,128)} %slot_ref.1, f32[4,2048]{1,0:T(4,128)} %weight_ref.1, f32[3072,150]{1,0:T(8,128)} %bitcast.16, f32[2048,150]{1,0:T(8,128)} %bitcast.21), custom_call_target="tpu_custom_call" | custom-call | tf_op jit(solution)/shard_map/pallas_call | solution.py:307
  187.2 4.9 %all-to-all-start.1 = ((f32[128,24,150]{2,1,0:T(8,128)}), f32[128,24,150]{2,1,0:T(8,128)S(1)}, u32[]{:S(2)}, u32[]{:S(2)}) async-start(f32[128,24,150]{2,1,0:T(8,128)} %bitcast.22), calls=%async_computation.1 | async-start | bytes 6291456 | tf_op jit(solution)/shard_map/all_to_all | solution.py:327
  192.2 2.7 copy.15
  194.8 38.4 %all-to-all-done.1 = f32[128,24,150]{2,1,0:T(8,128)S(1)} async-done(((f32[128,24,150]{2,1,0:T(8,128)}), f32[128,24,150]{2,1,0:T(8,128)S(1)}, u32[]{:S(2)}, u32[]{:S(2)}) %all-to-all-start.1) | async-done | bytes 1843232 | tf_op jit(solution)/shard_map/all_to_all | solution.py:327
  233.3 1.7 copy-done.1
  234.9 22.4 %shard_map.89 = f32[4096,150]{1,0:T(8,128)} custom-call(s32[3072]{0:T(1024)} %bitcast.25, f32[3072,150]{1,0:T(8,128)} %bitcast.17), custom_call_target="tpu_custom_call" | custom-call | tf_op jit(solution)/shard_map/pallas_call | solution.py:295
  257.3 3.7 %copy.14 = f32[150,4096]{1,0:T(8,128)S(1)} copy(f32[150,4096]{0,1:T(8,128)} %bitcast.15) | data formatting | bytes 4915200 | tf_op jit(solution)/shard_map/transpose | solution.py:346
  261.0 1.8 reshape_reshape.7.v_ref
  262.8 52.2 %shard_map.90 = f32[5,960,128]{2,1,0:T(8,128)} custom-call(f32[5,960,128]{2,1,0:T(8,128)} %reshape_reshape.7.v_ref, f32[5,960,128]{2,1,0:T(8,128)} %bitcast.13), custom_call_target="tpu_custom_call" | custom-call | flops 30720000 | bytes 7372800 | tf_op jit(solution)/shard_map/pallas_call | solution.py:171
  315.0 0.0 copy-done.2
  315.0 3.7 %add.3 = f32[150,32,128]{2,1,0:T(8,128)} add(f32[150,32,128]{2,1,0:T(8,128)S(1)} %copy-done.2, f32[150,32,128]{2,1,0:T(8,128)} %bitcast.20) | non-fusion elementwise | flops 614400 | bytes 7372800 | tf_op jit(solution)/shard_map/add | solution.py:347
  (2 shorter events, 0.0 us)
Async XLA Ops:
  0.6 2.1 copy-start.3
  82.2 47.6 %all-to-all-start = ((f32[128,24,150]{2,1,0:T(8,128)}), f32[128,24,150]{2,1,0:T(8,128)S(1)}, u32[]{:S(2)}, u32[]{:S(2)}) async-start(f32[128,24,150]{2,1,0:T(8,128)} %bitcast.18), calls=%async_computation | async-start | bytes 6291456 | tf_op jit(solution)/shard_map/all_to_all | solution.py:323
  129.9 1.7 copy-start
  187.2 46.1 %all-to-all-start.1 = ((f32[128,24,150]{2,1,0:T(8,128)}), f32[128,24,150]{2,1,0:T(8,128)S(1)}, u32[]{:S(2)}, u32[]{:S(2)}) async-start(f32[128,24,150]{2,1,0:T(8,128)} %bitcast.22), calls=%async_computation.1 | async-start | bytes 6291456 | tf_op jit(solution)/shard_map/all_to_all | solution.py:327
  233.3 1.7 copy-start.1
  262.8 52.2 %copy-start.2 = (f32[150,32,128]{2,1,0:T(8,128)S(1)}, f32[150,32,128]{2,1,0:T(8,128)}, u32[]{:S(2)}) copy-start(f32[150,32,128]{2,1,0:T(8,128)} %param.7) | copy-start | bytes 7372804

commit v9 on v7

--- a/solution.py
+++ b/solution.py
@@ -320,7 +320,7 @@
     conduct = diffusivity * jnp.concatenate([sea_float, sea_float], axis=0)
     conduct_blocks = conduct.reshape(steps, GROUP * rows, lanes)
     smooth = diffuse(state, conduct_blocks)
-    rows_of = smooth.reshape(vals, cell_count).T
+    rows_of = smooth.transpose(1, 2, 0).reshape(cell_count, vals)
     send_index = send_cols[0]
     outgoing = select_rows(send_index, rows_of, send_index.shape[0])
     received = to_owners(outgoing)
@@ -328,7 +328,7 @@
     equivalents = equivalent_rows.T
     incoming = to_sources(returned)
     adjoint_rows = place_rows(send_index, incoming, cell_count)
-    adjoint_field = adjoint_rows.T.reshape(state.shape)
+    adjoint_field = adjoint_rows.reshape(rows, lanes, vals).transpose(2, 0, 1)
     product = state + diffuse(adjoint_field, conduct_blocks)
     return (product, equivalents)
 

time: 301 us -> 300 us (level)
    reshape x0 -> x2, local copies, waits for them, and re-layouts: none -> 9.84 us  [the longest x1 4.99 us: on_device(): adjoint_field = adjoint_rows.reshape(rows, lanes, vals).transpose(2, 0, 1)]
    another operation x3 -> x0, local copies, waits for them, and re-layouts: 7.8 us -> none  [the longest x2 5.96 us: on_device(): rows_of = smooth.reshape(vals, cell_count).T]
    transpose x1 -> x0, local copies, waits for them, and re-layouts: 3.66 us -> none  [on_device(): adjoint_field = adjoint_rows.T.reshape(state.shape)]
where the time goes in v9:
time: 300 us; the launch traced here: 297 us
  Pallas kernels  182 us (61%)
  waiting for transfers between devices  76.7 us (26%)
  local copies, waits for them, and re-layouts  19.1 us (6%)
  starting transfers between devices  11.5 us (4%)
  other arithmetic  7.13 us (2%)
    pallas_call x2, Pallas kernels, diffuse(): pl.pallas_call(functools.partial(diffuse_kernel, rows), in_specs=[VMEM, V...  109 us
    all_to_all x1, waiting for transfers between devices, to_sources(): lax.all_to_all(returned, ('lon', 'lat'), split_axis=0, concat_axis=0, til...  38.4 us
    all_to_all x1, waiting for transfers between devices, to_owners(): lax.all_to_all(outgoing, ('lon', 'lat'), split_axis=0, concat_axis=0, til...  38.2 us
    pallas_call x1, Pallas kernels, interpolate(): pl.pallas_call(interp_kernel, in_specs=[SMEM, SMEM, VMEM, VMEM], out_spec...  36.4 us
    pallas_call x1, Pallas kernels, place_rows(): pl.pallas_call(place_kernel, in_specs=[SMEM, VMEM], out_specs=VMEM, out_s...  21.4 us
    pallas_call x1, Pallas kernels, select_rows(): pl.pallas_call(select_kernel, in_specs=[SMEM, VMEM], out_specs=VMEM, out_...  15.2 us
    unnamed x10, local copies, waits for them, and re-layouts  9.31 us
    all_to_all x1, starting transfers between devices, to_owners(): lax.all_to_all(outgoing, ('lon', 'lat'), split_axis=0, concat_axis=0, til...  6.59 us
  transfers between devices with their start and end apart: 2, of which 2 were waited for; matrix products, arithmetic and copies ran while one was open for 2% of the time, Pallas kernels for 0%

profile of v9, /device:TPU:8, one launch (start us, length us, event | category | flops | bytes accessed | tf_op | source)
XLA Modules:
  0.0 296.8 jit_solution(7379915103609869628)
XLA Ops:
  0.6 0.0 copy-start.3
  0.6 1.6 convert_element_type.3
  2.2 0.5 copy-done.3
  2.7 1.9 maximum_multiply_fusion
  4.6 56.5 %shard_map.86 = f32[5,960,128]{2,1,0:T(8,128)} custom-call(f32[5,960,128]{2,1,0:T(8,128)} %bitcast.25, f32[5,960,128]{2,1,0:T(8,128)} %bitcast.18), custom_call_target="tpu_custom_call" | custom-call | flops 30720000 | bytes 7372800 | tf_op jit(solution)/shard_map/pallas_call | solution.py:171
  61.1 4.8 %copy.9 = f32[150,32,128]{0,2,1:T(8,128)} copy(f32[150,32,128]{2,1,0:T(8,128)} %bitcast.28) | data formatting | bytes 4915200 | tf_op jit(solution)/shard_map/reshape | solution.py:191
  65.9 15.2 %shard_map.87 = f32[3072,150]{1,0:T(8,128)} custom-call(s32[3072]{0:T(1024)} %bitcast.32, f32[4096,150]{1,0:T(8,128)} %bitcast.20), custom_call_target="tpu_custom_call" | custom-call | tf_op jit(solution)/shard_map/pallas_call | solution.py:271
  81.1 6.6 %all-to-all-start = ((f32[128,24,150]{2,1,0:T(8,128)}), f32[128,24,150]{2,1,0:T(8,128)S(1)}, u32[]{:S(2)}, u32[]{:S(2)}) async-start(f32[128,24,150]{2,1,0:T(8,128)} %bitcast.24), calls=%async_computation | async-start | bytes 6291456 | tf_op jit(solution)/shard_map/all_to_all | solution.py:308
  87.7 2.8 copy.10
  90.5 38.2 %all-to-all-done = f32[128,24,150]{2,1,0:T(8,128)S(1)} async-done(((f32[128,24,150]{2,1,0:T(8,128)}), f32[128,24,150]{2,1,0:T(8,128)S(1)}, u32[]{:S(2)}, u32[]{:S(2)}) %all-to-all-start) | async-done | bytes 1843232 | tf_op jit(solution)/shard_map/all_to_all | solution.py:308
  128.8 0.0 copy-start
  128.8 1.7 copy-done
  130.4 36.4 %shard_map.88 = (f32[2048,150]{1,0:T(8,128)}, f32[3072,150]{1,0:T(8,128)}) custom-call(s32[4,2048]{1,0:T(4,128)} %slot_ref.1, f32[4,2048]{1,0:T(4,128)} %weight_ref.1, f32[3072,150]{1,0:T(8,128)} %bitcast.22, f32[2048,150]{1,0:T(8,128)} %bitcast.29), custom_call_target="tpu_custom_call" | custom-call | tf_op jit(solution)/shard_map/pallas_call | solution.py:292
  166.8 4.9 %all-to-all-start.1 = ((f32[128,24,150]{2,1,0:T(8,128)}), f32[128,24,150]{2,1,0:T(8,128)S(1)}, u32[]{:S(2)}, u32[]{:S(2)}) async-start(f32[128,24,150]{2,1,0:T(8,128)} %bitcast.30), calls=%async_computation.1 | async-start | bytes 6291456 | tf_op jit(solution)/shard_map/all_to_all | solution.py:312
  171.8 2.7 copy.12
  174.5 38.4 %all-to-all-done.1 = f32[128,24,150]{2,1,0:T(8,128)S(1)} async-done(((f32[128,24,150]{2,1,0:T(8,128)}), f32[128,24,150]{2,1,0:T(8,128)S(1)}, u32[]{:S(2)}, u32[]{:S(2)}) %all-to-all-start.1) | async-done | bytes 1843232 | tf_op jit(solution)/shard_map/all_to_all | solution.py:312
  212.9 0.0 copy-start.1
  212.9 1.7 copy-done.1
  214.6 21.4 %shard_map.89 = f32[4096,150]{1,0:T(8,128)} custom-call(s32[3072]{0:T(1024)} %bitcast.33, f32[3072,150]{1,0:T(8,128)} %bitcast.23), custom_call_target="tpu_custom_call" | custom-call | tf_op jit(solution)/shard_map/pallas_call | solution.py:280
  236.0 5.0 %copy.11 = f32[32,128,150]{1,0,2:T(8,128)} copy(f32[32,128,150]{2,1,0:T(8,128)} %bitcast.21) | data formatting | bytes 4915200 | tf_op jit(solution)/shard_map/reshape | solution.py:331
  241.0 0.0 copy-start.2
  241.0 52.2 %shard_map.90 = f32[5,960,128]{2,1,0:T(8,128)} custom-call(f32[5,960,128]{2,1,0:T(8,128)} %bitcast.26, f32[5,960,128]{2,1,0:T(8,128)} %bitcast.19), custom_call_target="tpu_custom_call" | custom-call | flops 30720000 | bytes 7372800 | tf_op jit(solution)/shard_map/pallas_call | solution.py:171
  293.1 0.0 copy-done.2
  293.1 3.7 %add.3 = f32[150,32,128]{2,1,0:T(8,128)} add(f32[150,32,128]{2,1,0:T(8,128)S(1)} %copy-done.2, f32[150,32,128]{2,1,0:T(8,128)} %bitcast.27) | non-fusion elementwise | flops 614400 | bytes 7372800 | tf_op jit(solution)/shard_map/add | solution.py:332
Async XLA Ops:
  0.6 2.1 copy-start.3
  81.1 47.6 %all-to-all-start = ((f32[128,24,150]{2,1,0:T(8,128)}), f32[128,24,150]{2,1,0:T(8,128)S(1)}, u32[]{:S(2)}, u32[]{:S(2)}) async-start(f32[128,24,150]{2,1,0:T(8,128)} %bitcast.24), calls=%async_computation | async-start | bytes 6291456 | tf_op jit(solution)/shard_map/all_to_all | solution.py:308
  128.8 1.7 copy-start
  166.8 46.1 %all-to-all-start.1 = ((f32[128,24,150]{2,1,0:T(8,128)}), f32[128,24,150]{2,1,0:T(8,128)S(1)}, u32[]{:S(2)}, u32[]{:S(2)}) async-start(f32[128,24,150]{2,1,0:T(8,128)} %bitcast.30), calls=%async_computation.1 | async-start | bytes 6291456 | tf_op jit(solution)/shard_map/all_to_all | solution.py:312
  212.9 1.7 copy-start.1
  241.0 52.2 %copy-start.2 = (f32[150,32,128]{2,1,0:T(8,128)S(1)}, f32[150,32,128]{2,1,0:T(8,128)}, u32[]{:S(2)}) copy-start(f32[150,32,128]{2,1,0:T(8,128)} %param.7) | copy-start | bytes 7372804

commit v10 on v9

--- a/solution.py
+++ b/solution.py
@@ -113,8 +113,7 @@
     lax.fori_loop(0, groups, body, 0)
 
 
-def diffuse_kernel(rows, v_ref, c_ref, out_ref, mid_ref, k_ref, row_edge, col_edge, row_halo,
-                   col_halo, send_sem, recv_sem):
+def exchanger(row_edge, col_edge, row_halo, col_halo, send_sem, recv_sem):
     lon = lax.axis_index("lon")
     lat = lax.axis_index("lat")
     n_lon = lax.axis_size("lon")
@@ -147,15 +146,25 @@
             copies.append(copy)
         return copies
 
+    north_ok = jnp.minimum(lat, 1).astype(jnp.float32)
+    south_ok = jnp.minimum(n_lat - 1 - lat, 1).astype(jnp.float32)
+    return exchange, (north_ok, south_ok)
+
+
+def diffuse_kernel(rows, v_ref, c_ref, out_ref, mid_ref, k_ref, row_edge, col_edge, row_halo,
+                   col_halo, send_sem, recv_sem):
+    exchange, scales = exchanger(row_edge, col_edge, row_halo, col_halo, send_sem, recv_sem)
     edge_pass(rows, c_ref, row_edge.at[0], col_edge.at[0])
     edge_pass(rows, v_ref, row_edge.at[1], col_edge.at[1])
-    first = exchange(0) + exchange(1)
-    for copy in first:
+    for copy in exchange(0) + exchange(1):
         copy.wait()
-    north_ok = jnp.minimum(lat, 1).astype(jnp.float32)
-    south_ok = jnp.minimum(n_lat - 1 - lat, 1).astype(jnp.float32)
-    scales = (north_ok, south_ok)
     coef_pass(rows, c_ref, (row_halo.at[0], col_halo.at[0]), scales, k_ref)
+    sweeps(rows, v_ref, k_ref, out_ref, mid_ref, row_edge, col_edge, row_halo, col_halo, exchange,
+           scales)
+
+
+def sweeps(rows, v_ref, k_ref, out_ref, mid_ref, row_edge, col_edge, row_halo, col_halo, exchange,
+           scales):
     slab_pass(rows, v_ref, k_ref, (row_halo.at[1], col_halo.at[1]), scales, mid_ref,
               (row_edge.at[2], col_edge.at[2]))
     for copy in exchange(2):
@@ -163,11 +172,42 @@
     slab_pass(rows, mid_ref, k_ref, (row_halo.at[2], col_halo.at[2]), scales, out_ref, None)
 
 
+def sweep_kernel(rows, v_ref, k_ref, out_ref, mid_ref, row_edge, col_edge, row_halo, col_halo,
+                 send_sem, recv_sem):
+    exchange, scales = exchanger(row_edge, col_edge, row_halo, col_halo, send_sem, recv_sem)
+    edge_pass(rows, v_ref, row_edge.at[1], col_edge.at[1])
+    for copy in exchange(1):
+        copy.wait()
+    sweeps(rows, v_ref, k_ref, out_ref, mid_ref, row_edge, col_edge, row_halo, col_halo, exchange,
+           scales)
+
+
+def coef_kernel(rows, c_ref, anchor_ref, k_ref, row_edge, col_edge, row_halo, col_halo, send_sem,
+                recv_sem):
+    del anchor_ref
+    exchange, scales = exchanger(row_edge, col_edge, row_halo, col_halo, send_sem, recv_sem)
+    edge_pass(rows, c_ref, row_edge.at[0], col_edge.at[0])
+    for copy in exchange(0):
+        copy.wait()
+    coef_pass(rows, c_ref, (row_halo.at[0], col_halo.at[0]), scales, k_ref)
+
+
+def halo_scratch(groups, rows, lanes):
+    rounds = SWEEPS + 1
+    return [
+        pltpu.VMEM((rounds, 2, groups, GROUP, lanes), jnp.float32),
+        pltpu.VMEM((rounds, 2, groups, GROUP, rows), jnp.float32),
+        pltpu.VMEM((rounds, 2, groups, GROUP, lanes), jnp.float32),
+        pltpu.VMEM((rounds, 2, groups, GROUP, rows), jnp.float32),
+        pltpu.SemaphoreType.DMA((rounds, 4)),
+        pltpu.SemaphoreType.DMA((rounds, 4)),
+    ]
+
+
 def diffuse(field, conduct_blocks):
     vals, rows, lanes = field.shape
     groups = vals // GROUP
     blocks = field.reshape(groups, GROUP * rows, lanes)
-    rounds = SWEEPS + 1
     out = pl.pallas_call(
         functools.partial(diffuse_kernel, rows),
         in_specs=[VMEM, VMEM],
@@ -176,18 +216,47 @@
         scratch_shapes=[
             pltpu.VMEM(blocks.shape, jnp.float32),
             pltpu.VMEM((4, groups, rows, GROUP, lanes), jnp.float32),
-            pltpu.VMEM((rounds, 2, groups, GROUP, lanes), jnp.float32),
-            pltpu.VMEM((rounds, 2, groups, GROUP, rows), jnp.float32),
-            pltpu.VMEM((rounds, 2, groups, GROUP, lanes), jnp.float32),
-            pltpu.VMEM((rounds, 2, groups, GROUP, rows), jnp.float32),
-            pltpu.SemaphoreType.DMA((rounds, 4)),
-            pltpu.SemaphoreType.DMA((rounds, 4)),
-        ],
+        ]
+        + halo_scratch(groups, rows, lanes),
         compiler_params=pltpu.CompilerParams(collective_id=0, has_side_effects=True),
         cost_estimate=pl.CostEstimate(
             flops=50 * field.size, bytes_accessed=12 * field.size, transcendentals=0
         ),
     )(blocks, conduct_blocks)
+    return out.reshape(vals, rows, lanes)
+
+
+def coefficients(conduct_blocks, anchor, rows):
+    groups, span, lanes = conduct_blocks.shape
+    return pl.pallas_call(
+        functools.partial(coef_kernel, rows),
+        in_specs=[VMEM, VMEM],
+        out_specs=VMEM,
+        out_shape=jax.ShapeDtypeStruct((4, groups, rows, GROUP, lanes), jnp.float32),
+        scratch_shapes=halo_scratch(groups, rows, lanes),
+        compiler_params=pltpu.CompilerParams(collective_id=1, has_side_effects=True),
+        cost_estimate=pl.CostEstimate(
+            flops=10 * conduct_blocks.size, bytes_accessed=20 * conduct_blocks.size,
+            transcendentals=0,
+        ),
+    )(conduct_blocks, anchor)
+
+
+def diffuse_with(field, coef):
+    vals, rows, lanes = field.shape
+    groups = vals // GROUP
+    blocks = field.reshape(groups, GROUP * rows, lanes)
+    out = pl.pallas_call(
+        functools.partial(sweep_kernel, rows),
+        in_specs=[VMEM, VMEM],
+        out_specs=VMEM,
+        out_shape=jax.ShapeDtypeStruct(blocks.shape, jnp.float32),
+        scratch_shapes=[pltpu.VMEM(blocks.shape, jnp.float32)] + halo_scratch(groups, rows, lanes),
+        compiler_params=pltpu.CompilerParams(collective_id=2, has_side_effects=True),
+        cost_estimate=pl.CostEstimate(
+            flops=40 * field.size, bytes_accessed=24 * field.size, transcendentals=0
+        ),
+    )(blocks, coef)
     return out.reshape(vals, rows, lanes)
 
 
@@ -326,10 +395,11 @@
     received = to_owners(outgoing)
     equivalent_rows, returned = interpolate(obs_slots, obs_weights, received, obs_precision.T)
     equivalents = equivalent_rows.T
+    coef = coefficients(conduct_blocks, returned[:8, :], rows)
     incoming = to_sources(returned)
     adjoint_rows = place_rows(send_index, incoming, cell_count)
     adjoint_field = adjoint_rows.reshape(rows, lanes, vals).transpose(2, 0, 1)
-    product = state + diffuse(adjoint_field, conduct_blocks)
+    product = state + diffuse_with(adjoint_field, coef)
     return (product, equivalents)
 
 

time: 300 us -> 303 us (1.010)
  Pallas kernels: 182 us -> 222 us
  waiting for transfers between devices: 76.7 us -> 38.2 us
    pallas_call x0 -> x2, Pallas kernels: none -> 92.7 us  [the longest x1 48 us: coefficients(): pl.pallas_call(functools.partial(coef_kernel, rows), in_specs=[VMEM, VMEM...]
    pallas_call x2 -> x1, Pallas kernels: 109 us -> 56.5 us  [diffuse(): pl.pallas_call(functools.partial(diffuse_kernel, rows), in_specs=[VMEM, V...]
    all_to_all x1, waiting for transfers between devices: 38.4 us -> 0.01 us  [to_sources(): lax.all_to_all(returned, ('lon', 'lat'), split_axis=0, concat_axis=0, til...]
  transfers between devices with their start and end apart: 2 -> 2, of which waited for: 2 -> 1; matrix products, arithmetic and copies ran while one was open for 2% -> 2% of each run, Pallas kernels for 0% -> 16%
where the time goes in v10:
time: 303 us; the launch traced here: 300 us
  Pallas kernels  222 us (73%)
  waiting for transfers between devices  38.2 us (13%)
  local copies, waits for them, and re-layouts  20.3 us (7%)
  starting transfers between devices  11.5 us (4%)
  other arithmetic  7.13 us (2%)
    pallas_call x1, Pallas kernels, diffuse(): pl.pallas_call(functools.partial(diffuse_kernel, rows), in_specs=[VMEM, V...  56.5 us
    pallas_call x1, Pallas kernels, coefficients(): pl.pallas_call(functools.partial(coef_kernel, rows), in_specs=[VMEM, VMEM...  48 us
    pallas_call x1, Pallas kernels, diffuse_with(): pl.pallas_call(functools.partial(sweep_kernel, rows), in_specs=[VMEM, VME...  44.7 us
    all_to_all x1, waiting for transfers between devices, to_owners(): lax.all_to_all(outgoing, ('lon', 'lat'), split_axis=0, concat_axis=0, til...  38.2 us
    pallas_call x1, Pallas kernels, interpolate(): pl.pallas_call(interp_kernel, in_specs=[SMEM, SMEM, VMEM, VMEM], out_spec...  36.5 us
    pallas_call x1, Pallas kernels, place_rows(): pl.pallas_call(place_kernel, in_specs=[SMEM, VMEM], out_specs=VMEM, out_s...  21.5 us
    pallas_call x1, Pallas kernels, select_rows(): pl.pallas_call(select_kernel, in_specs=[SMEM, VMEM], out_specs=VMEM, out_...  15.2 us
    unnamed x10, local copies, waits for them, and re-layouts  9.26 us
  transfers between devices with their start and end apart: 2, of which 1 were waited for; matrix products, arithmetic and copies ran while one was open for 2% of the time, Pallas kernels for 16%

profile of v10, /device:TPU:8, one launch (start us, length us, event | category | flops | bytes accessed | tf_op | source)
XLA Modules:
  0.0 300.3 jit_solution(3561837557630954862)
XLA Ops:
  0.6 0.0 copy-start.3
  0.6 1.6 convert_element_type.3
  2.2 0.5 copy-done.3
  2.7 1.9 maximum_multiply_fusion
  4.6 56.5 %shard_map.86 = f32[5,960,128]{2,1,0:T(8,128)} custom-call(f32[5,960,128]{2,1,0:T(8,128)} %bitcast.25, f32[5,960,128]{2,1,0:T(8,128)} %bitcast.18), custom_call_target="tpu_custom_call" | custom-call | flops 30720000 | bytes 7372800 | tf_op jit(solution)/shard_map/pallas_call | solution.py:211
  61.1 4.8 %copy.9 = f32[150,32,128]{0,2,1:T(8,128)} copy(f32[150,32,128]{2,1,0:T(8,128)} %bitcast.26) | data formatting | bytes 4915200 | tf_op jit(solution)/shard_map/reshape | solution.py:226
  65.9 15.2 %shard_map.87 = f32[3072,150]{1,0:T(8,128)} custom-call(s32[3072]{0:T(1024)} %bitcast.32, f32[4096,150]{1,0:T(8,128)} %bitcast.20), custom_call_target="tpu_custom_call" | custom-call | tf_op jit(solution)/shard_map/pallas_call | solution.py:340
  81.1 6.6 %all-to-all-start = ((f32[128,24,150]{2,1,0:T(8,128)}), f32[128,24,150]{2,1,0:T(8,128)S(1)}, u32[]{:S(2)}, u32[]{:S(2)}) async-start(f32[128,24,150]{2,1,0:T(8,128)} %bitcast.24), calls=%async_computation | async-start | bytes 6291456 | tf_op jit(solution)/shard_map/all_to_all | solution.py:377
  87.7 2.8 copy.10
  90.5 38.2 %all-to-all-done = f32[128,24,150]{2,1,0:T(8,128)S(1)} async-done(((f32[128,24,150]{2,1,0:T(8,128)}), f32[128,24,150]{2,1,0:T(8,128)S(1)}, u32[]{:S(2)}, u32[]{:S(2)}) %all-to-all-start) | async-done | bytes 1843232 | tf_op jit(solution)/shard_map/all_to_all | solution.py:377
  128.8 1.6 copy-done.1
  130.4 36.5 %shard_map.88 = (f32[2048,150]{1,0:T(8,128)}, f32[3072,150]{1,0:T(8,128)}) custom-call(s32[4,2048]{1,0:T(4,128)} %slot_ref.1, f32[4,2048]{1,0:T(4,128)} %weight_ref.1, f32[3072,150]{1,0:T(8,128)} %bitcast.23, f32[2048,150]{1,0:T(8,128)} %bitcast.29), custom_call_target="tpu_custom_call" | custom-call | tf_op jit(solution)/shard_map/pallas_call | solution.py:361
  166.9 4.9 %all-to-all-start.1 = ((f32[128,24,150]{2,1,0:T(8,128)}), f32[128,24,150]{2,1,0:T(8,128)S(1)}, u32[]{:S(2)}, u32[]{:S(2)}) async-start(f32[128,24,150]{2,1,0:T(8,128)} %bitcast.30), calls=%async_computation.1 | async-start | bytes 6291456 | tf_op jit(solution)/shard_map/all_to_all | solution.py:381
  171.8 1.3 slice.3.anchor_ref
  173.1 2.7 copy.12
  175.8 48.0 %shard_map.90.k_ref = f32[4,5,32,30,128]{4,3,2,1,0:T(8,128)} custom-call(f32[5,960,128]{2,1,0:T(8,128)} %bitcast.19, f32[8,150]{1,0:T(8,128)} %slice.3.anchor_ref), custom_call_target="tpu_custom_call" | custom-call | flops 6144000 | bytes 12288000 | tf_op jit(solution)/shard_map/pallas_call | solution.py:231
  223.8 0.0 all-to-all-done.1
  223.9 0.0 copy-start
  223.9 1.6 copy-done
  225.5 21.5 %shard_map.89 = f32[4096,150]{1,0:T(8,128)} custom-call(s32[3072]{0:T(1024)} %bitcast.33, f32[3072,150]{1,0:T(8,128)} %bitcast.22), custom_call_target="tpu_custom_call" | custom-call | tf_op jit(solution)/shard_map/pallas_call | solution.py:349
  247.0 4.9 %copy.11 = f32[32,128,150]{1,0,2:T(8,128)} copy(f32[32,128,150]{2,1,0:T(8,128)} %bitcast.21) | data formatting | bytes 4915200 | tf_op jit(solution)/shard_map/reshape | solution.py:401
  251.9 44.7 %shard_map.91 = f32[5,960,128]{2,1,0:T(8,128)} custom-call(f32[5,960,128]{2,1,0:T(8,128)} %bitcast.27, f32[4,5,32,30,128]{4,3,2,1,0:T(8,128)} %shard_map.90.k_ref), custom_call_target="tpu_custom_call" | custom-call | flops 24576000 | bytes 14745600 | tf_op jit(solution)/shard_map/pallas_call | solution.py:249
  296.6 0.0 copy-done.2
  296.6 3.7 %add.3 = f32[150,32,128]{2,1,0:T(8,128)} add(f32[150,32,128]{2,1,0:T(8,128)S(1)} %copy-done.2, f32[150,32,128]{2,1,0:T(8,128)} %bitcast.28) | non-fusion elementwise | flops 614400 | bytes 7372800 | tf_op jit(solution)/shard_map/add | solution.py:402
  (2 shorter events, 0.0 us)
Async XLA Ops:
  0.6 2.1 copy-start.3
  81.1 47.6 %all-to-all-start = ((f32[128,24,150]{2,1,0:T(8,128)}), f32[128,24,150]{2,1,0:T(8,128)S(1)}, u32[]{:S(2)}, u32[]{:S(2)}) async-start(f32[128,24,150]{2,1,0:T(8,128)} %bitcast.24), calls=%async_computation | async-start | bytes 6291456 | tf_op jit(solution)/shard_map/all_to_all | solution.py:377
  128.8 1.6 copy-start.1
  166.9 57.0 %all-to-all-start.1 = ((f32[128,24,150]{2,1,0:T(8,128)}), f32[128,24,150]{2,1,0:T(8,128)S(1)}, u32[]{:S(2)}, u32[]{:S(2)}) async-start(f32[128,24,150]{2,1,0:T(8,128)} %bitcast.30), calls=%async_computation.1 | async-start | bytes 6291456 | tf_op jit(solution)/shard_map/all_to_all | solution.py:381
  223.9 1.6 copy-start
  251.9 44.7 %copy-start.2 = (f32[150,32,128]{2,1,0:T(8,128)S(1)}, f32[150,32,128]{2,1,0:T(8,128)}, u32[]{:S(2)}) copy-start(f32[150,32,128]{2,1,0:T(8,128)} %param.7) | copy-start | bytes 7372804

commit v11 on v9

--- a/solution.py
+++ b/solution.py
@@ -256,7 +256,7 @@
             tile = jnp.where(sub == i, jnp.broadcast_to(total, (8, width)), tile)
             weighted = load_row(precision_ref, j) * total
             for k in range(taps):
-                add_row(parts[(i % 2) * taps + k], slots[k], weighted * weights[k])
+                add_row(parts[k], slots[k], weighted * weights[k])
         equiv_ref[pl.ds(pl.multiple_of(t * 8, 8), 8), :] = tile
         return carry
 
@@ -282,7 +282,7 @@
         in_specs=[SMEM, VMEM],
         out_specs=VMEM,
         out_shape=jax.ShapeDtypeStruct((cells, rows.shape[1]), jnp.float32),
-        scratch_shapes=[pltpu.VMEM((cells, rows.shape[1]), jnp.float32) for _ in range(4)],
+        scratch_shapes=[pltpu.VMEM((cells, rows.shape[1]), jnp.float32) for _ in range(2)],
         compiler_params=pltpu.CompilerParams(vmem_limit_bytes=60 * 1024 * 1024),
     )(index, rows)
 
@@ -298,7 +298,7 @@
             jax.ShapeDtypeStruct(received.shape, jnp.float32),
         ],
         scratch_shapes=[
-            pltpu.VMEM(received.shape, jnp.float32) for _ in range(2 * obs_slots.shape[0])
+            pltpu.VMEM(received.shape, jnp.float32) for _ in range(obs_slots.shape[0])
         ],
         compiler_params=pltpu.CompilerParams(vmem_limit_bytes=60 * 1024 * 1024),
     )(obs_slots, obs_weights, received, precision_rows)

time: 300 us -> 300 us (level)
  no operation moved by 1% of the time
where the time goes in v11:
time: 300 us; the launch traced here: 297 us
  Pallas kernels  182 us (61%)
  waiting for transfers between devices  76.7 us (26%)
  local copies, waits for them, and re-layouts  19.1 us (6%)
  starting transfers between devices  11.5 us (4%)
  other arithmetic  7.13 us (2%)
    pallas_call x2, Pallas kernels, diffuse(): pl.pallas_call(functools.partial(diffuse_kernel, rows), in_specs=[VMEM, V...  109 us
    all_to_all x1, waiting for transfers between devices, to_sources(): lax.all_to_all(returned, ('lon', 'lat'), split_axis=0, concat_axis=0, til...  38.4 us
    all_to_all x1, waiting for transfers between devices, to_owners(): lax.all_to_all(outgoing, ('lon', 'lat'), split_axis=0, concat_axis=0, til...  38.2 us
    pallas_call x1, Pallas kernels, interpolate(): pl.pallas_call(interp_kernel, in_specs=[SMEM, SMEM, VMEM, VMEM], out_spec...  35.2 us
    pallas_call x1, Pallas kernels, place_rows(): pl.pallas_call(place_kernel, in_specs=[SMEM, VMEM], out_specs=VMEM, out_s...  22.6 us
    pallas_call x1, Pallas kernels, select_rows(): pl.pallas_call(select_kernel, in_specs=[SMEM, VMEM], out_specs=VMEM, out_...  15.2 us
    unnamed x10, local copies, waits for them, and re-layouts  9.31 us
    all_to_all x1, starting transfers between devices, to_owners(): lax.all_to_all(outgoing, ('lon', 'lat'), split_axis=0, concat_axis=0, til...  6.59 us
  transfers between devices with their start and end apart: 2, of which 2 were waited for; matrix products, arithmetic and copies ran while one was open for 2% of the time, Pallas kernels for 0%

profile of v11, /device:TPU:8, one launch (start us, length us, event | category | flops | bytes accessed | tf_op | source)
XLA Modules:
  0.0 296.8 jit_solution(16040700661185257353)
XLA Ops:
  0.6 0.0 copy-start.3
  0.6 1.6 convert_element_type.3
  2.2 0.5 copy-done.3
  2.7 1.9 maximum_multiply_fusion
  4.6 56.5 %shard_map.86 = f32[5,960,128]{2,1,0:T(8,128)} custom-call(f32[5,960,128]{2,1,0:T(8,128)} %bitcast.25, f32[5,960,128]{2,1,0:T(8,128)} %bitcast.18), custom_call_target="tpu_custom_call" | custom-call | flops 30720000 | bytes 7372800 | tf_op jit(solution)/shard_map/pallas_call | solution.py:171
  61.1 4.8 %copy.9 = f32[150,32,128]{0,2,1:T(8,128)} copy(f32[150,32,128]{2,1,0:T(8,128)} %bitcast.28) | data formatting | bytes 4915200 | tf_op jit(solution)/shard_map/reshape | solution.py:191
  65.9 15.2 %shard_map.87 = f32[3072,150]{1,0:T(8,128)} custom-call(s32[3072]{0:T(1024)} %bitcast.32, f32[4096,150]{1,0:T(8,128)} %bitcast.20), custom_call_target="tpu_custom_call" | custom-call | tf_op jit(solution)/shard_map/pallas_call | solution.py:271
  81.1 6.6 %all-to-all-start = ((f32[128,24,150]{2,1,0:T(8,128)}), f32[128,24,150]{2,1,0:T(8,128)S(1)}, u32[]{:S(2)}, u32[]{:S(2)}) async-start(f32[128,24,150]{2,1,0:T(8,128)} %bitcast.24), calls=%async_computation | async-start | bytes 6291456 | tf_op jit(solution)/shard_map/all_to_all | solution.py:308
  87.7 2.8 copy.10
  90.5 38.2 %all-to-all-done = f32[128,24,150]{2,1,0:T(8,128)S(1)} async-done(((f32[128,24,150]{2,1,0:T(8,128)}), f32[128,24,150]{2,1,0:T(8,128)S(1)}, u32[]{:S(2)}, u32[]{:S(2)}) %all-to-all-start) | async-done | bytes 1843232 | tf_op jit(solution)/shard_map/all_to_all | solution.py:308
  128.8 0.0 copy-start
  128.8 1.7 copy-done
  130.4 35.2 %shard_map.88 = (f32[2048,150]{1,0:T(8,128)}, f32[3072,150]{1,0:T(8,128)}) custom-call(s32[4,2048]{1,0:T(4,128)} %slot_ref.1, f32[4,2048]{1,0:T(4,128)} %weight_ref.1, f32[3072,150]{1,0:T(8,128)} %bitcast.22, f32[2048,150]{1,0:T(8,128)} %bitcast.29), custom_call_target="tpu_custom_call" | custom-call | tf_op jit(solution)/shard_map/pallas_call | solution.py:292
  165.6 4.9 %all-to-all-start.1 = ((f32[128,24,150]{2,1,0:T(8,128)}), f32[128,24,150]{2,1,0:T(8,128)S(1)}, u32[]{:S(2)}, u32[]{:S(2)}) async-start(f32[128,24,150]{2,1,0:T(8,128)} %bitcast.30), calls=%async_computation.1 | async-start | bytes 6291456 | tf_op jit(solution)/shard_map/all_to_all | solution.py:312
  170.5 2.7 copy.12
  173.2 38.4 %all-to-all-done.1 = f32[128,24,150]{2,1,0:T(8,128)S(1)} async-done(((f32[128,24,150]{2,1,0:T(8,128)}), f32[128,24,150]{2,1,0:T(8,128)S(1)}, u32[]{:S(2)}, u32[]{:S(2)}) %all-to-all-start.1) | async-done | bytes 1843232 | tf_op jit(solution)/shard_map/all_to_all | solution.py:312
  211.7 0.0 copy-start.1
  211.7 1.7 copy-done.1
  213.3 22.6 %shard_map.89 = f32[4096,150]{1,0:T(8,128)} custom-call(s32[3072]{0:T(1024)} %bitcast.33, f32[3072,150]{1,0:T(8,128)} %bitcast.23), custom_call_target="tpu_custom_call" | custom-call | tf_op jit(solution)/shard_map/pallas_call | solution.py:280
  235.9 5.0 %copy.11 = f32[32,128,150]{1,0,2:T(8,128)} copy(f32[32,128,150]{2,1,0:T(8,128)} %bitcast.21) | data formatting | bytes 4915200 | tf_op jit(solution)/shard_map/reshape | solution.py:331
  240.9 0.0 copy-start.2
  240.9 52.2 %shard_map.90 = f32[5,960,128]{2,1,0:T(8,128)} custom-call(f32[5,960,128]{2,1,0:T(8,128)} %bitcast.26, f32[5,960,128]{2,1,0:T(8,128)} %bitcast.19), custom_call_target="tpu_custom_call" | custom-call | flops 30720000 | bytes 7372800 | tf_op jit(solution)/shard_map/pallas_call | solution.py:171
  293.1 0.0 copy-done.2
  293.1 3.7 %add.3 = f32[150,32,128]{2,1,0:T(8,128)} add(f32[150,32,128]{2,1,0:T(8,128)S(1)} %copy-done.2, f32[150,32,128]{2,1,0:T(8,128)} %bitcast.27) | non-fusion elementwise | flops 614400 | bytes 7372800 | tf_op jit(solution)/shard_map/add | solution.py:332
Async XLA Ops:
  0.6 2.1 copy-start.3
  81.1 47.6 %all-to-all-start = ((f32[128,24,150]{2,1,0:T(8,128)}), f32[128,24,150]{2,1,0:T(8,128)S(1)}, u32[]{:S(2)}, u32[]{:S(2)}) async-start(f32[128,24,150]{2,1,0:T(8,128)} %bitcast.24), calls=%async_computation | async-start | bytes 6291456 | tf_op jit(solution)/shard_map/all_to_all | solution.py:308
  128.8 1.7 copy-start
  165.6 46.1 %all-to-all-start.1 = ((f32[128,24,150]{2,1,0:T(8,128)}), f32[128,24,150]{2,1,0:T(8,128)S(1)}, u32[]{:S(2)}, u32[]{:S(2)}) async-start(f32[128,24,150]{2,1,0:T(8,128)} %bitcast.30), calls=%async_computation.1 | async-start | bytes 6291456 | tf_op jit(solution)/shard_map/all_to_all | solution.py:312
  211.7 1.7 copy-start.1
  240.9 52.2 %copy-start.2 = (f32[150,32,128]{2,1,0:T(8,128)S(1)}, f32[150,32,128]{2,1,0:T(8,128)}, u32[]{:S(2)}) copy-start(f32[150,32,128]{2,1,0:T(8,128)} %param.7) | copy-start | bytes 7372804

commit v12 on v11

--- a/solution.py
+++ b/solution.py
@@ -282,7 +282,7 @@
         in_specs=[SMEM, VMEM],
         out_specs=VMEM,
         out_shape=jax.ShapeDtypeStruct((cells, rows.shape[1]), jnp.float32),
-        scratch_shapes=[pltpu.VMEM((cells, rows.shape[1]), jnp.float32) for _ in range(2)],
+        scratch_shapes=[pltpu.VMEM((cells, rows.shape[1]), jnp.float32) for _ in range(4)],
         compiler_params=pltpu.CompilerParams(vmem_limit_bytes=60 * 1024 * 1024),
     )(index, rows)
 

time: 300 us -> 298 us (level)
  no operation moved by 1% of the time
where the time goes in v12:
time: 298 us; the launch traced here: 296 us
  Pallas kernels  180 us (60%)
  waiting for transfers between devices  76.7 us (26%)
  local copies, waits for them, and re-layouts  19.1 us (6%)
  starting transfers between devices  11.5 us (4%)
  other arithmetic  7.13 us (2%)
    pallas_call x2, Pallas kernels, diffuse(): pl.pallas_call(functools.partial(diffuse_kernel, rows), in_specs=[VMEM, V...  109 us
    all_to_all x1, waiting for transfers between devices, to_sources(): lax.all_to_all(returned, ('lon', 'lat'), split_axis=0, concat_axis=0, til...  38.4 us
    all_to_all x1, waiting for transfers between devices, to_owners(): lax.all_to_all(outgoing, ('lon', 'lat'), split_axis=0, concat_axis=0, til...  38.2 us
    pallas_call x1, Pallas kernels, interpolate(): pl.pallas_call(interp_kernel, in_specs=[SMEM, SMEM, VMEM, VMEM], out_spec...  35.2 us
    pallas_call x1, Pallas kernels, place_rows(): pl.pallas_call(place_kernel, in_specs=[SMEM, VMEM], out_specs=VMEM, out_s...  21.4 us
    pallas_call x1, Pallas kernels, select_rows(): pl.pallas_call(select_kernel, in_specs=[SMEM, VMEM], out_specs=VMEM, out_...  15.2 us
    unnamed x10, local copies, waits for them, and re-layouts  9.31 us
    all_to_all x1, starting transfers between devices, to_owners(): lax.all_to_all(outgoing, ('lon', 'lat'), split_axis=0, concat_axis=0, til...  6.59 us
  transfers between devices with their start and end apart: 2, of which 2 were waited for; matrix products, arithmetic and copies ran while one was open for 2% of the time, Pallas kernels for 0%

profile of v12, /device:TPU:8, one launch (start us, length us, event | category | flops | bytes accessed | tf_op | source)
XLA Modules:
  0.0 295.6 jit_solution(3253271077866980138)
XLA Ops:
  0.6 0.0 copy-start.3
  0.6 1.6 convert_element_type.3
  2.2 0.5 copy-done.3
  2.7 1.9 maximum_multiply_fusion
  4.6 56.5 %shard_map.86 = f32[5,960,128]{2,1,0:T(8,128)} custom-call(f32[5,960,128]{2,1,0:T(8,128)} %bitcast.25, f32[5,960,128]{2,1,0:T(8,128)} %bitcast.18), custom_call_target="tpu_custom_call" | custom-call | flops 30720000 | bytes 7372800 | tf_op jit(solution)/shard_map/pallas_call | solution.py:171
  61.1 4.8 %copy.9 = f32[150,32,128]{0,2,1:T(8,128)} copy(f32[150,32,128]{2,1,0:T(8,128)} %bitcast.28) | data formatting | bytes 4915200 | tf_op jit(solution)/shard_map/reshape | solution.py:191
  65.9 15.2 %shard_map.87 = f32[3072,150]{1,0:T(8,128)} custom-call(s32[3072]{0:T(1024)} %bitcast.32, f32[4096,150]{1,0:T(8,128)} %bitcast.20), custom_call_target="tpu_custom_call" | custom-call | tf_op jit(solution)/shard_map/pallas_call | solution.py:271
  81.1 6.6 %all-to-all-start = ((f32[128,24,150]{2,1,0:T(8,128)}), f32[128,24,150]{2,1,0:T(8,128)S(1)}, u32[]{:S(2)}, u32[]{:S(2)}) async-start(f32[128,24,150]{2,1,0:T(8,128)} %bitcast.24), calls=%async_computation | async-start | bytes 6291456 | tf_op jit(solution)/shard_map/all_to_all | solution.py:308
  87.7 2.8 copy.10
  90.5 38.2 %all-to-all-done = f32[128,24,150]{2,1,0:T(8,128)S(1)} async-done(((f32[128,24,150]{2,1,0:T(8,128)}), f32[128,24,150]{2,1,0:T(8,128)S(1)}, u32[]{:S(2)}, u32[]{:S(2)}) %all-to-all-start) | async-done | bytes 1843232 | tf_op jit(solution)/shard_map/all_to_all | solution.py:308
  128.8 0.0 copy-start
  128.8 1.7 copy-done
  130.4 35.2 %shard_map.88 = (f32[2048,150]{1,0:T(8,128)}, f32[3072,150]{1,0:T(8,128)}) custom-call(s32[4,2048]{1,0:T(4,128)} %slot_ref.1, f32[4,2048]{1,0:T(4,128)} %weight_ref.1, f32[3072,150]{1,0:T(8,128)} %bitcast.22, f32[2048,150]{1,0:T(8,128)} %bitcast.29), custom_call_target="tpu_custom_call" | custom-call | tf_op jit(solution)/shard_map/pallas_call | solution.py:292
  165.6 4.9 %all-to-all-start.1 = ((f32[128,24,150]{2,1,0:T(8,128)}), f32[128,24,150]{2,1,0:T(8,128)S(1)}, u32[]{:S(2)}, u32[]{:S(2)}) async-start(f32[128,24,150]{2,1,0:T(8,128)} %bitcast.30), calls=%async_computation.1 | async-start | bytes 6291456 | tf_op jit(solution)/shard_map/all_to_all | solution.py:312
  170.5 2.7 copy.12
  173.2 38.4 %all-to-all-done.1 = f32[128,24,150]{2,1,0:T(8,128)S(1)} async-done(((f32[128,24,150]{2,1,0:T(8,128)}), f32[128,24,150]{2,1,0:T(8,128)S(1)}, u32[]{:S(2)}, u32[]{:S(2)}) %all-to-all-start.1) | async-done | bytes 1843232 | tf_op jit(solution)/shard_map/all_to_all | solution.py:312
  211.7 0.0 copy-start.1
  211.7 1.7 copy-done.1
  213.3 21.4 %shard_map.89 = f32[4096,150]{1,0:T(8,128)} custom-call(s32[3072]{0:T(1024)} %bitcast.33, f32[3072,150]{1,0:T(8,128)} %bitcast.23), custom_call_target="tpu_custom_call" | custom-call | tf_op jit(solution)/shard_map/pallas_call | solution.py:280
  234.7 5.0 %copy.11 = f32[32,128,150]{1,0,2:T(8,128)} copy(f32[32,128,150]{2,1,0:T(8,128)} %bitcast.21) | data formatting | bytes 4915200 | tf_op jit(solution)/shard_map/reshape | solution.py:331
  239.7 0.0 copy-start.2
  239.7 52.2 %shard_map.90 = f32[5,960,128]{2,1,0:T(8,128)} custom-call(f32[5,960,128]{2,1,0:T(8,128)} %bitcast.26, f32[5,960,128]{2,1,0:T(8,128)} %bitcast.19), custom_call_target="tpu_custom_call" | custom-call | flops 30720000 | bytes 7372800 | tf_op jit(solution)/shard_map/pallas_call | solution.py:171
  291.9 0.0 copy-done.2
  291.9 3.7 %add.3 = f32[150,32,128]{2,1,0:T(8,128)} add(f32[150,32,128]{2,1,0:T(8,128)S(1)} %copy-done.2, f32[150,32,128]{2,1,0:T(8,128)} %bitcast.27) | non-fusion elementwise | flops 614400 | bytes 7372800 | tf_op jit(solution)/shard_map/add | solution.py:332
Async XLA Ops:
  0.6 2.1 copy-start.3
  81.1 47.6 %all-to-all-start = ((f32[128,24,150]{2,1,0:T(8,128)}), f32[128,24,150]{2,1,0:T(8,128)S(1)}, u32[]{:S(2)}, u32[]{:S(2)}) async-start(f32[128,24,150]{2,1,0:T(8,128)} %bitcast.24), calls=%async_computation | async-start | bytes 6291456 | tf_op jit(solution)/shard_map/all_to_all | solution.py:308
  128.8 1.7 copy-start
  165.6 46.1 %all-to-all-start.1 = ((f32[128,24,150]{2,1,0:T(8,128)}), f32[128,24,150]{2,1,0:T(8,128)S(1)}, u32[]{:S(2)}, u32[]{:S(2)}) async-start(f32[128,24,150]{2,1,0:T(8,128)} %bitcast.30), calls=%async_computation.1 | async-start | bytes 6291456 | tf_op jit(solution)/shard_map/all_to_all | solution.py:312
  211.7 1.7 copy-start.1
  239.7 52.2 %copy-start.2 = (f32[150,32,128]{2,1,0:T(8,128)S(1)}, f32[150,32,128]{2,1,0:T(8,128)}, u32[]{:S(2)}) copy-start(f32[150,32,128]{2,1,0:T(8,128)} %param.7) | copy-start | bytes 7372804

commit v13 on v12

--- a/solution.py
+++ b/solution.py
@@ -260,7 +260,7 @@
         equiv_ref[pl.ds(pl.multiple_of(t * 8, 8), 8), :] = tile
         return carry
 
-    lax.fori_loop(0, obs_count // 8, body, 0)
+    lax.fori_loop(0, obs_count // 8, body, 0, unroll=2)
     total = parts[0][...]
     for part in parts[1:]:
         total = total + part[...]

time: 298 us -> 298 us (level)
  no operation moved by 1% of the time
where the time goes in v13:
time: 298 us; the launch traced here: 295 us
  Pallas kernels  180 us (60%)
  waiting for transfers between devices  76.7 us (26%)
  local copies, waits for them, and re-layouts  19.1 us (6%)
  starting transfers between devices  11.5 us (4%)
  other arithmetic  7.13 us (2%)
    pallas_call x2, Pallas kernels, diffuse(): pl.pallas_call(functools.partial(diffuse_kernel, rows), in_specs=[VMEM, V...  109 us
    all_to_all x1, waiting for transfers between devices, to_sources(): lax.all_to_all(returned, ('lon', 'lat'), split_axis=0, concat_axis=0, til...  38.4 us
    all_to_all x1, waiting for transfers between devices, to_owners(): lax.all_to_all(outgoing, ('lon', 'lat'), split_axis=0, concat_axis=0, til...  38.2 us
    pallas_call x1, Pallas kernels, interpolate(): pl.pallas_call(interp_kernel, in_specs=[SMEM, SMEM, VMEM, VMEM], out_spec...  34.5 us
    pallas_call x1, Pallas kernels, place_rows(): pl.pallas_call(place_kernel, in_specs=[SMEM, VMEM], out_specs=VMEM, out_s...  21.4 us
    pallas_call x1, Pallas kernels, select_rows(): pl.pallas_call(select_kernel, in_specs=[SMEM, VMEM], out_specs=VMEM, out_...  15.2 us
    unnamed x10, local copies, waits for them, and re-layouts  9.31 us
    all_to_all x1, starting transfers between devices, to_owners(): lax.all_to_all(outgoing, ('lon', 'lat'), split_axis=0, concat_axis=0, til...  6.59 us
  transfers between devices with their start and end apart: 2, of which 2 were waited for; matrix products, arithmetic and copies ran while one was open for 2% of the time, Pallas kernels for 0%

profile of v13, /device:TPU:8, one launch (start us, length us, event | category | flops | bytes accessed | tf_op | source)
XLA Modules:
  0.0 294.9 jit_solution(5751050223342721782)
XLA Ops:
  0.6 0.0 copy-start.3
  0.6 1.6 convert_element_type.3
  2.2 0.5 copy-done.3
  2.7 1.9 maximum_multiply_fusion
  4.6 56.5 %shard_map.86 = f32[5,960,128]{2,1,0:T(8,128)} custom-call(f32[5,960,128]{2,1,0:T(8,128)} %bitcast.25, f32[5,960,128]{2,1,0:T(8,128)} %bitcast.18), custom_call_target="tpu_custom_call" | custom-call | flops 30720000 | bytes 7372800 | tf_op jit(solution)/shard_map/pallas_call | solution.py:171
  61.1 4.8 %copy.9 = f32[150,32,128]{0,2,1:T(8,128)} copy(f32[150,32,128]{2,1,0:T(8,128)} %bitcast.28) | data formatting | bytes 4915200 | tf_op jit(solution)/shard_map/reshape | solution.py:191
  65.9 15.2 %shard_map.87 = f32[3072,150]{1,0:T(8,128)} custom-call(s32[3072]{0:T(1024)} %bitcast.32, f32[4096,150]{1,0:T(8,128)} %bitcast.20), custom_call_target="tpu_custom_call" | custom-call | tf_op jit(solution)/shard_map/pallas_call | solution.py:271
  81.1 6.6 %all-to-all-start = ((f32[128,24,150]{2,1,0:T(8,128)}), f32[128,24,150]{2,1,0:T(8,128)S(1)}, u32[]{:S(2)}, u32[]{:S(2)}) async-start(f32[128,24,150]{2,1,0:T(8,128)} %bitcast.24), calls=%async_computation | async-start | bytes 6291456 | tf_op jit(solution)/shard_map/all_to_all | solution.py:308
  87.7 2.8 copy.10
  90.5 38.2 %all-to-all-done = f32[128,24,150]{2,1,0:T(8,128)S(1)} async-done(((f32[128,24,150]{2,1,0:T(8,128)}), f32[128,24,150]{2,1,0:T(8,128)S(1)}, u32[]{:S(2)}, u32[]{:S(2)}) %all-to-all-start) | async-done | bytes 1843232 | tf_op jit(solution)/shard_map/all_to_all | solution.py:308
  128.8 0.0 copy-start
  128.8 1.7 copy-done
  130.4 34.5 %shard_map.88 = (f32[2048,150]{1,0:T(8,128)}, f32[3072,150]{1,0:T(8,128)}) custom-call(s32[4,2048]{1,0:T(4,128)} %slot_ref.1, f32[4,2048]{1,0:T(4,128)} %weight_ref.1, f32[3072,150]{1,0:T(8,128)} %bitcast.22, f32[2048,150]{1,0:T(8,128)} %bitcast.29), custom_call_target="tpu_custom_call" | custom-call | tf_op jit(solution)/shard_map/pallas_call | solution.py:292
  164.9 4.9 %all-to-all-start.1 = ((f32[128,24,150]{2,1,0:T(8,128)}), f32[128,24,150]{2,1,0:T(8,128)S(1)}, u32[]{:S(2)}, u32[]{:S(2)}) async-start(f32[128,24,150]{2,1,0:T(8,128)} %bitcast.30), calls=%async_computation.1 | async-start | bytes 6291456 | tf_op jit(solution)/shard_map/all_to_all | solution.py:312
  169.9 2.7 copy.12
  172.6 38.4 %all-to-all-done.1 = f32[128,24,150]{2,1,0:T(8,128)S(1)} async-done(((f32[128,24,150]{2,1,0:T(8,128)}), f32[128,24,150]{2,1,0:T(8,128)S(1)}, u32[]{:S(2)}, u32[]{:S(2)}) %all-to-all-start.1) | async-done | bytes 1843232 | tf_op jit(solution)/shard_map/all_to_all | solution.py:312
  211.0 0.0 copy-start.1
  211.0 1.7 copy-done.1
  212.7 21.4 %shard_map.89 = f32[4096,150]{1,0:T(8,128)} custom-call(s32[3072]{0:T(1024)} %bitcast.33, f32[3072,150]{1,0:T(8,128)} %bitcast.23), custom_call_target="tpu_custom_call" | custom-call | tf_op jit(solution)/shard_map/pallas_call | solution.py:280
  234.1 5.0 %copy.11 = f32[32,128,150]{1,0,2:T(8,128)} copy(f32[32,128,150]{2,1,0:T(8,128)} %bitcast.21) | data formatting | bytes 4915200 | tf_op jit(solution)/shard_map/reshape | solution.py:331
  239.0 0.0 copy-start.2
  239.0 52.2 %shard_map.90 = f32[5,960,128]{2,1,0:T(8,128)} custom-call(f32[5,960,128]{2,1,0:T(8,128)} %bitcast.26, f32[5,960,128]{2,1,0:T(8,128)} %bitcast.19), custom_call_target="tpu_custom_call" | custom-call | flops 30720000 | bytes 7372800 | tf_op jit(solution)/shard_map/pallas_call | solution.py:171
  291.2 0.0 copy-done.2
  291.2 3.7 %add.3 = f32[150,32,128]{2,1,0:T(8,128)} add(f32[150,32,128]{2,1,0:T(8,128)S(1)} %copy-done.2, f32[150,32,128]{2,1,0:T(8,128)} %bitcast.27) | non-fusion elementwise | flops 614400 | bytes 7372800 | tf_op jit(solution)/shard_map/add | solution.py:332
Async XLA Ops:
  0.6 2.1 copy-start.3
  81.1 47.6 %all-to-all-start = ((f32[128,24,150]{2,1,0:T(8,128)}), f32[128,24,150]{2,1,0:T(8,128)S(1)}, u32[]{:S(2)}, u32[]{:S(2)}) async-start(f32[128,24,150]{2,1,0:T(8,128)} %bitcast.24), calls=%async_computation | async-start | bytes 6291456 | tf_op jit(solution)/shard_map/all_to_all | solution.py:308
  128.8 1.7 copy-start
  164.9 46.1 %all-to-all-start.1 = ((f32[128,24,150]{2,1,0:T(8,128)}), f32[128,24,150]{2,1,0:T(8,128)S(1)}, u32[]{:S(2)}, u32[]{:S(2)}) async-start(f32[128,24,150]{2,1,0:T(8,128)} %bitcast.30), calls=%async_computation.1 | async-start | bytes 6291456 | tf_op jit(solution)/shard_map/all_to_all | solution.py:312
  211.0 1.7 copy-start.1
  239.0 52.2 %copy-start.2 = (f32[150,32,128]{2,1,0:T(8,128)S(1)}, f32[150,32,128]{2,1,0:T(8,128)}, u32[]{:S(2)}) copy-start(f32[150,32,128]{2,1,0:T(8,128)} %param.7) | copy-start | bytes 7372804

commit v14 on v13

--- a/solution.py
+++ b/solution.py
@@ -8,13 +8,25 @@
 from jax.sharding import PartitionSpec as P
 
 SWEEPS = 2
-GROUP = 30
+GROUP = 15
 SMEM = pl.BlockSpec(memory_space=pltpu.SMEM)
 VMEM = pl.BlockSpec(memory_space=pltpu.VMEM)
 
 
-def coef_pass(rows, c_ref, coef_halo, scales, k_ref):
-    groups, span, lanes = c_ref.shape
+def conduct_slabs(d_ref, m_ref, rows):
+    mask_groups = m_ref.shape[0]
+    group = d_ref.shape[1] // rows
+
+    def slab(g, r):
+        spot = pl.ds(r, group, stride=rows)
+        return d_ref[g, spot, :] * m_ref[g % mask_groups, spot, :].astype(jnp.float32)
+
+    return slab
+
+
+def coef_pass(rows, d_ref, m_ref, coef_halo, scales, k_ref):
+    c_slab = conduct_slabs(d_ref, m_ref, rows)
+    groups, span, lanes = d_ref.shape
     group = span // rows
     north_ok, south_ok = scales
     coef_rows, coef_cols = coef_halo
@@ -24,10 +36,10 @@
         cw = coef_cols[0, g]
         ce = coef_cols[1, g]
         c_up = coef_rows[0, g] * north_ok
-        c_mid = c_ref[g, pl.ds(0, group, stride=rows), :]
+        c_mid = c_slab(g, 0)
         for r in range(rows):
             if r + 1 < rows:
-                c_dn = c_ref[g, pl.ds(r + 1, group, stride=rows), :]
+                c_dn = c_slab(g, r + 1)
             else:
                 c_dn = coef_rows[1, g] * south_ok
             c_w = jnp.where(lane == 0, cw[:, r : r + 1], pltpu.roll(c_mid, 1, 1))
@@ -90,16 +102,18 @@
     lax.fori_loop(0, groups, body, 0)
 
 
-def edge_pass(rows, src_ref, row_out, col_out):
+def edge_pass(rows, src_ref, row_out, col_out, read=None):
     groups, span, lanes = src_ref.shape
     group = span // rows
+    if read is None:
+        read = lambda g, r: src_ref[g, pl.ds(r, group, stride=rows), :]
 
     def body(g, carry):
         col = lax.broadcasted_iota(jnp.int32, (group, rows), 1)
         left = jnp.zeros((group, rows), jnp.float32)
         right = jnp.zeros((group, rows), jnp.float32)
         for r in range(rows):
-            x = src_ref[g, pl.ds(r, group, stride=rows), :]
+            x = read(g, r)
             if r == 0:
                 row_out[0, g] = x
             if r == rows - 1:
@@ -113,7 +127,7 @@
     lax.fori_loop(0, groups, body, 0)
 
 
-def diffuse_kernel(rows, v_ref, c_ref, out_ref, mid_ref, k_ref, row_edge, col_edge, row_halo,
+def diffuse_kernel(rows, v_ref, d_ref, m_ref, out_ref, mid_ref, k_ref, row_edge, col_edge, row_halo,
                    col_halo, send_sem, recv_sem):
     lon = lax.axis_index("lon")
     lat = lax.axis_index("lat")
@@ -147,7 +161,7 @@
             copies.append(copy)
         return copies
 
-    edge_pass(rows, c_ref, row_edge.at[0], col_edge.at[0])
+    edge_pass(rows, d_ref, row_edge.at[0], col_edge.at[0], conduct_slabs(d_ref, m_ref, rows))
     edge_pass(rows, v_ref, row_edge.at[1], col_edge.at[1])
     first = exchange(0) + exchange(1)
     for copy in first:
@@ -155,7 +169,7 @@
     north_ok = jnp.minimum(lat, 1).astype(jnp.float32)
     south_ok = jnp.minimum(n_lat - 1 - lat, 1).astype(jnp.float32)
     scales = (north_ok, south_ok)
-    coef_pass(rows, c_ref, (row_halo.at[0], col_halo.at[0]), scales, k_ref)
+    coef_pass(rows, d_ref, m_ref, (row_halo.at[0], col_halo.at[0]), scales, k_ref)
     slab_pass(rows, v_ref, k_ref, (row_halo.at[1], col_halo.at[1]), scales, mid_ref,
               (row_edge.at[2], col_edge.at[2]))
     for copy in exchange(2):
@@ -163,14 +177,14 @@
     slab_pass(rows, mid_ref, k_ref, (row_halo.at[2], col_halo.at[2]), scales, out_ref, None)
 
 
-def diffuse(field, conduct_blocks):
+def diffuse(field, diffusivity_blocks, mask_blocks):
     vals, rows, lanes = field.shape
     groups = vals // GROUP
     blocks = field.reshape(groups, GROUP * rows, lanes)
     rounds = SWEEPS + 1
     out = pl.pallas_call(
         functools.partial(diffuse_kernel, rows),
-        in_specs=[VMEM, VMEM],
+        in_specs=[VMEM, VMEM, VMEM],
         out_specs=VMEM,
         out_shape=jax.ShapeDtypeStruct(blocks.shape, jnp.float32),
         scratch_shapes=[
@@ -187,7 +201,7 @@
         cost_estimate=pl.CostEstimate(
             flops=50 * field.size, bytes_accessed=12 * field.size, transcendentals=0
         ),
-    )(blocks, conduct_blocks)
+    )(blocks, diffusivity_blocks, mask_blocks)
     return out.reshape(vals, rows, lanes)
 
 
@@ -316,10 +330,9 @@
     vals, rows, lanes = state.shape
     cell_count = rows * lanes
     steps = vals // GROUP
-    sea_float = sea_mask.astype(jnp.float32)
-    conduct = diffusivity * jnp.concatenate([sea_float, sea_float], axis=0)
-    conduct_blocks = conduct.reshape(steps, GROUP * rows, lanes)
-    smooth = diffuse(state, conduct_blocks)
+    diffusivity_blocks = diffusivity.reshape(steps, GROUP * rows, lanes)
+    mask_blocks = sea_mask.reshape(sea_mask.shape[0] // GROUP, GROUP * rows, lanes)
+    smooth = diffuse(state, diffusivity_blocks, mask_blocks)
     rows_of = smooth.transpose(1, 2, 0).reshape(cell_count, vals)
     send_index = send_cols[0]
     outgoing = select_rows(send_index, rows_of, send_index.shape[0])
@@ -329,7 +342,7 @@
     incoming = to_sources(returned)
     adjoint_rows = place_rows(send_index, incoming, cell_count)
     adjoint_field = adjoint_rows.reshape(rows, lanes, vals).transpose(2, 0, 1)
-    product = state + diffuse(adjoint_field, conduct_blocks)
+    product = state + diffuse(adjoint_field, diffusivity_blocks, mask_blocks)
     return (product, equivalents)
 
 

time: 298 us -> 315 us (1.057)
  Pallas kernels: 180 us -> 201 us
  other arithmetic: 7.13 us -> 3.7 us
    pallas_call x2, Pallas kernels: 109 us -> 130 us  [diffuse(): pl.pallas_call(functools.partial(diffuse_kernel, rows), in_specs=[VMEM, V...]
    unnamed x10 -> x8, local copies, waits for them, and re-layouts: 9.31 us -> 8.74 us
where the time goes in v14:
time: 315 us; the launch traced here: 312 us
  Pallas kernels  201 us (64%)
  waiting for transfers between devices  76.7 us (24%)
  local copies, waits for them, and re-layouts  18.5 us (6%)
  starting transfers between devices  11.5 us (4%)
  other arithmetic  3.7 us (1%)
    pallas_call x2, Pallas kernels, diffuse(): pl.pallas_call(functools.partial(diffuse_kernel, rows), in_specs=[VMEM, V...  130 us
    all_to_all x1, waiting for transfers between devices, to_sources(): lax.all_to_all(returned, ('lon', 'lat'), split_axis=0, concat_axis=0, til...  38.4 us
    all_to_all x1, waiting for transfers between devices, to_owners(): lax.all_to_all(outgoing, ('lon', 'lat'), split_axis=0, concat_axis=0, til...  38.3 us
    pallas_call x1, Pallas kernels, interpolate(): pl.pallas_call(interp_kernel, in_specs=[SMEM, SMEM, VMEM, VMEM], out_spec...  34.5 us
    pallas_call x1, Pallas kernels, place_rows(): pl.pallas_call(place_kernel, in_specs=[SMEM, VMEM], out_specs=VMEM, out_s...  21.4 us
    pallas_call x1, Pallas kernels, select_rows(): pl.pallas_call(select_kernel, in_specs=[SMEM, VMEM], out_specs=VMEM, out_...  15.2 us
    unnamed x8, local copies, waits for them, and re-layouts  8.74 us
    all_to_all x1, starting transfers between devices, to_owners(): lax.all_to_all(outgoing, ('lon', 'lat'), split_axis=0, concat_axis=0, til...  6.59 us
  transfers between devices with their start and end apart: 2, of which 2 were waited for; matrix products, arithmetic and copies ran while one was open for 2% of the time, Pallas kernels for 0%

profile of v14, /device:TPU:8, one launch (start us, length us, event | category | flops | bytes accessed | tf_op | source)
XLA Modules:
  0.0 312.4 jit_solution(1878565674077733737)
XLA Ops:
  0.6 67.3 %shard_map.86 = f32[10,480,128]{2,1,0:T(8,128)} custom-call(f32[10,480,128]{2,1,0:T(8,128)} %bitcast.24, f32[10,480,128]{2,1,0:T(8,128)} %bitcast.28, s32[5,480,128]{2,1,0:T(8,128)} %bitcast.31), custom_call_target="tpu_custom_call" | custom-call | flops 30720000 | bytes 7372800 | tf_op jit(solution)/shard_map/pallas_call | solution.py:185
  68.0 4.8 %copy.9 = f32[150,32,128]{0,2,1:T(8,128)} copy(f32[150,32,128]{2,1,0:T(8,128)} %bitcast.27) | data formatting | bytes 4915200 | tf_op jit(solution)/shard_map/reshape | solution.py:205
  72.8 15.2 %shard_map.87 = f32[3072,150]{1,0:T(8,128)} custom-call(s32[3072]{0:T(1024)} %bitcast.35, f32[4096,150]{1,0:T(8,128)} %bitcast.19), custom_call_target="tpu_custom_call" | custom-call | tf_op jit(solution)/shard_map/pallas_call | solution.py:285
  88.0 6.6 %all-to-all-start = ((f32[128,24,150]{2,1,0:T(8,128)}), f32[128,24,150]{2,1,0:T(8,128)S(1)}, u32[]{:S(2)}, u32[]{:S(2)}) async-start(f32[128,24,150]{2,1,0:T(8,128)} %bitcast.23), calls=%async_computation | async-start | bytes 6291456 | tf_op jit(solution)/shard_map/all_to_all | solution.py:322
  94.6 2.7 copy.10
  97.3 38.3 %all-to-all-done = f32[128,24,150]{2,1,0:T(8,128)S(1)} async-done(((f32[128,24,150]{2,1,0:T(8,128)}), f32[128,24,150]{2,1,0:T(8,128)S(1)}, u32[]{:S(2)}, u32[]{:S(2)}) %all-to-all-start) | async-done | bytes 1843232 | tf_op jit(solution)/shard_map/all_to_all | solution.py:322
  135.6 0.0 copy-start
  135.6 1.6 copy-done
  137.3 34.5 %shard_map.88 = (f32[2048,150]{1,0:T(8,128)}, f32[3072,150]{1,0:T(8,128)}) custom-call(s32[4,2048]{1,0:T(4,128)} %slot_ref.1, f32[4,2048]{1,0:T(4,128)} %weight_ref.1, f32[3072,150]{1,0:T(8,128)} %bitcast.21, f32[2048,150]{1,0:T(8,128)} %bitcast.30), custom_call_target="tpu_custom_call" | custom-call | tf_op jit(solution)/shard_map/pallas_call | solution.py:306
  171.8 4.9 %all-to-all-start.1 = ((f32[128,24,150]{2,1,0:T(8,128)}), f32[128,24,150]{2,1,0:T(8,128)S(1)}, u32[]{:S(2)}, u32[]{:S(2)}) async-start(f32[128,24,150]{2,1,0:T(8,128)} %bitcast.33), calls=%async_computation.1 | async-start | bytes 6291456 | tf_op jit(solution)/shard_map/all_to_all | solution.py:326
  176.7 2.7 copy.12
  179.4 38.4 %all-to-all-done.1 = f32[128,24,150]{2,1,0:T(8,128)S(1)} async-done(((f32[128,24,150]{2,1,0:T(8,128)}), f32[128,24,150]{2,1,0:T(8,128)S(1)}, u32[]{:S(2)}, u32[]{:S(2)}) %all-to-all-start.1) | async-done | bytes 1843232 | tf_op jit(solution)/shard_map/all_to_all | solution.py:326
  217.9 0.0 copy-start.1
  217.9 1.7 copy-done.1
  219.5 21.4 %shard_map.89 = f32[4096,150]{1,0:T(8,128)} custom-call(s32[3072]{0:T(1024)} %bitcast.36, f32[3072,150]{1,0:T(8,128)} %bitcast.22), custom_call_target="tpu_custom_call" | custom-call | tf_op jit(solution)/shard_map/pallas_call | solution.py:294
  240.9 4.9 %copy.11 = f32[32,128,150]{1,0,2:T(8,128)} copy(f32[32,128,150]{2,1,0:T(8,128)} %bitcast.20) | data formatting | bytes 4915200 | tf_op jit(solution)/shard_map/reshape | solution.py:344
  245.8 0.0 copy-start.2
  245.8 62.9 %shard_map.90 = f32[10,480,128]{2,1,0:T(8,128)} custom-call(f32[10,480,128]{2,1,0:T(8,128)} %bitcast.25, f32[10,480,128]{2,1,0:T(8,128)} %bitcast.29, s32[5,480,128]{2,1,0:T(8,128)} %bitcast.32), custom_call_target="tpu_custom_call" | custom-call | flops 30720000 | bytes 7372800 | tf_op jit(solution)/shard_map/pallas_call | solution.py:185
  308.7 0.0 copy-done.2
  308.7 3.7 %add.3 = f32[150,32,128]{2,1,0:T(8,128)} add(f32[150,32,128]{2,1,0:T(8,128)S(1)} %copy-done.2, f32[150,32,128]{2,1,0:T(8,128)} %bitcast.26) | non-fusion elementwise | flops 614400 | bytes 7372800 | tf_op jit(solution)/shard_map/add | solution.py:345
Async XLA Ops:
  88.0 47.6 %all-to-all-start = ((f32[128,24,150]{2,1,0:T(8,128)}), f32[128,24,150]{2,1,0:T(8,128)S(1)}, u32[]{:S(2)}, u32[]{:S(2)}) async-start(f32[128,24,150]{2,1,0:T(8,128)} %bitcast.23), calls=%async_computation | async-start | bytes 6291456 | tf_op jit(solution)/shard_map/all_to_all | solution.py:322
  135.6 1.6 copy-start
  171.8 46.1 %all-to-all-start.1 = ((f32[128,24,150]{2,1,0:T(8,128)}), f32[128,24,150]{2,1,0:T(8,128)S(1)}, u32[]{:S(2)}, u32[]{:S(2)}) async-start(f32[128,24,150]{2,1,0:T(8,128)} %bitcast.33), calls=%async_computation.1 | async-start | bytes 6291456 | tf_op jit(solution)/shard_map/all_to_all | solution.py:326
  217.9 1.7 copy-start.1
  245.8 62.9 %copy-start.2 = (f32[150,32,128]{2,1,0:T(8,128)S(1)}, f32[150,32,128]{2,1,0:T(8,128)}, u32[]{:S(2)}) copy-start(f32[150,32,128]{2,1,0:T(8,128)} %param.7) | copy-start | bytes 7372804

commit v15 on v13

--- a/solution.py
+++ b/solution.py
@@ -42,7 +42,7 @@
     lax.fori_loop(0, groups, body, 0)
 
 
-def slab_pass(rows, src_ref, k_ref, field_halo, scales, dst_ref, edges):
+def slab_pass(rows, src_ref, k_ref, field_halo, scales, dst_ref, edges, base_ref=None):
     groups, span, lanes = src_ref.shape
     group = span // rows
     north_ok, south_ok = scales
@@ -73,7 +73,10 @@
             total = total + k_ref[2, g, r] * (x_w - x_mid)
             total = total + k_ref[3, g, r] * (x_e - x_mid)
             out = x_mid + total
-            dst_ref[g, pl.ds(r, group, stride=rows), :] = out
+            if base_ref is None:
+                dst_ref[g, pl.ds(r, group, stride=rows), :] = out
+            else:
+                dst_ref[g, pl.ds(r, group, stride=rows), :] = slab(base_ref, r) + out
             if edges is not None:
                 if r == 0:
                     edges[0][0, g] = out
@@ -113,8 +116,12 @@
     lax.fori_loop(0, groups, body, 0)
 
 
-def diffuse_kernel(rows, v_ref, c_ref, out_ref, mid_ref, k_ref, row_edge, col_edge, row_halo,
-                   col_halo, send_sem, recv_sem):
+def diffuse_kernel(rows, v_ref, c_ref, *refs):
+    if len(refs) == 10:
+        base_ref, refs = refs[0], refs[1:]
+    else:
+        base_ref = None
+    out_ref, mid_ref, k_ref, row_edge, col_edge, row_halo, col_halo, send_sem, recv_sem = refs
     lon = lax.axis_index("lon")
     lat = lax.axis_index("lat")
     n_lon = lax.axis_size("lon")
@@ -160,17 +167,20 @@
               (row_edge.at[2], col_edge.at[2]))
     for copy in exchange(2):
         copy.wait()
-    slab_pass(rows, mid_ref, k_ref, (row_halo.at[2], col_halo.at[2]), scales, out_ref, None)
-
-
-def diffuse(field, conduct_blocks):
+    slab_pass(rows, mid_ref, k_ref, (row_halo.at[2], col_halo.at[2]), scales, out_ref, None, base_ref)
+
+
+def diffuse(field, conduct_blocks, base=None):
     vals, rows, lanes = field.shape
     groups = vals // GROUP
     blocks = field.reshape(groups, GROUP * rows, lanes)
     rounds = SWEEPS + 1
+    operands = [blocks, conduct_blocks]
+    if base is not None:
+        operands.append(base.reshape(blocks.shape))
     out = pl.pallas_call(
         functools.partial(diffuse_kernel, rows),
-        in_specs=[VMEM, VMEM],
+        in_specs=[VMEM] * len(operands),
         out_specs=VMEM,
         out_shape=jax.ShapeDtypeStruct(blocks.shape, jnp.float32),
         scratch_shapes=[
@@ -183,11 +193,13 @@
             pltpu.SemaphoreType.DMA((rounds, 4)),
             pltpu.SemaphoreType.DMA((rounds, 4)),
         ],
-        compiler_params=pltpu.CompilerParams(collective_id=0, has_side_effects=True),
+        compiler_params=pltpu.CompilerParams(
+            collective_id=0 if base is None else 1, has_side_effects=True
+        ),
         cost_estimate=pl.CostEstimate(
             flops=50 * field.size, bytes_accessed=12 * field.size, transcendentals=0
         ),
-    )(blocks, conduct_blocks)
+    )(*operands)
     return out.reshape(vals, rows, lanes)
 
 
@@ -329,7 +341,7 @@
     incoming = to_sources(returned)
     adjoint_rows = place_rows(send_index, incoming, cell_count)
     adjoint_field = adjoint_rows.reshape(rows, lanes, vals).transpose(2, 0, 1)
-    product = state + diffuse(adjoint_field, conduct_blocks)
+    product = diffuse(adjoint_field, conduct_blocks, state)
     return (product, equivalents)
 
 

time: 298 us -> 299 us (level)
  other arithmetic: 7.13 us -> 3.43 us
  local copies, waits for them, and re-layouts: 19.1 us -> 22.5 us
    add x1 -> x0, other arithmetic: 3.7 us -> none  [on_device(): product = state + diffuse(adjoint_field, conduct_blocks)]
    unnamed x10 -> x9, local copies, waits for them, and re-layouts: 9.31 us -> 12.7 us
where the time goes in v15:
time: 299 us; the launch traced here: 296 us
  Pallas kernels  181 us (61%)
  waiting for transfers between devices  76.7 us (26%)
  local copies, waits for them, and re-layouts  22.5 us (8%)
  starting transfers between devices  11.5 us (4%)
  other arithmetic  3.43 us (1%)
    pallas_call x2, Pallas kernels, diffuse(): pl.pallas_call(functools.partial(diffuse_kernel, rows), in_specs=[VMEM] *...  110 us
    all_to_all x1, waiting for transfers between devices, to_sources(): lax.all_to_all(returned, ('lon', 'lat'), split_axis=0, concat_axis=0, til...  38.4 us
    all_to_all x1, waiting for transfers between devices, to_owners(): lax.all_to_all(outgoing, ('lon', 'lat'), split_axis=0, concat_axis=0, til...  38.2 us
    pallas_call x1, Pallas kernels, interpolate(): pl.pallas_call(interp_kernel, in_specs=[SMEM, SMEM, VMEM, VMEM], out_spec...  34.5 us
    pallas_call x1, Pallas kernels, place_rows(): pl.pallas_call(place_kernel, in_specs=[SMEM, VMEM], out_specs=VMEM, out_s...  21.4 us
    pallas_call x1, Pallas kernels, select_rows(): pl.pallas_call(select_kernel, in_specs=[SMEM, VMEM], out_specs=VMEM, out_...  15.2 us
    unnamed x9, local copies, waits for them, and re-layouts  12.7 us
    all_to_all x1, starting transfers between devices, to_owners(): lax.all_to_all(outgoing, ('lon', 'lat'), split_axis=0, concat_axis=0, til...  6.59 us
  transfers between devices with their start and end apart: 2, of which 2 were waited for; matrix products, arithmetic and copies ran while one was open for 2% of the time, Pallas kernels for 0%

profile of v15, /device:TPU:8, one launch (start us, length us, event | category | flops | bytes accessed | tf_op | source)
XLA Modules:
  0.0 295.9 jit_solution(3552901700699284343)
XLA Ops:
  0.6 0.0 copy-start.2
  0.6 1.6 convert_element_type.3
  2.2 0.5 copy-done.2
  2.7 1.9 maximum_multiply_fusion
  4.6 56.5 %shard_map.86 = f32[5,960,128]{2,1,0:T(8,128)} custom-call(f32[5,960,128]{2,1,0:T(8,128)} %bitcast.26, f32[5,960,128]{2,1,0:T(8,128)} %bitcast.18), custom_call_target="tpu_custom_call" | custom-call | flops 30720000 | bytes 7372800 | tf_op jit(solution)/shard_map/pallas_call | solution.py:181
  61.1 4.8 %copy.9 = f32[150,32,128]{0,2,1:T(8,128)} copy(f32[150,32,128]{2,1,0:T(8,128)} %bitcast.25) | data formatting | bytes 4915200 | tf_op jit(solution)/shard_map/reshape | solution.py:203
  65.9 15.2 %shard_map.87 = f32[3072,150]{1,0:T(8,128)} custom-call(s32[3072]{0:T(1024)} %bitcast.33, f32[4096,150]{1,0:T(8,128)} %bitcast.20), custom_call_target="tpu_custom_call" | custom-call | tf_op jit(solution)/shard_map/pallas_call | solution.py:283
  81.1 6.6 %all-to-all-start = ((f32[128,24,150]{2,1,0:T(8,128)}), f32[128,24,150]{2,1,0:T(8,128)S(1)}, u32[]{:S(2)}, u32[]{:S(2)}) async-start(f32[128,24,150]{2,1,0:T(8,128)} %bitcast.24), calls=%async_computation | async-start | bytes 6291456 | tf_op jit(solution)/shard_map/all_to_all | solution.py:320
  87.7 2.8 copy.10
  90.5 38.2 %all-to-all-done = f32[128,24,150]{2,1,0:T(8,128)S(1)} async-done(((f32[128,24,150]{2,1,0:T(8,128)}), f32[128,24,150]{2,1,0:T(8,128)S(1)}, u32[]{:S(2)}, u32[]{:S(2)}) %all-to-all-start) | async-done | bytes 1843232 | tf_op jit(solution)/shard_map/all_to_all | solution.py:320
  128.8 0.0 copy-start
  128.8 1.7 copy-done
  130.4 34.5 %shard_map.88 = (f32[2048,150]{1,0:T(8,128)}, f32[3072,150]{1,0:T(8,128)}) custom-call(s32[4,2048]{1,0:T(4,128)} %slot_ref.1, f32[4,2048]{1,0:T(4,128)} %weight_ref.1, f32[3072,150]{1,0:T(8,128)} %bitcast.22, f32[2048,150]{1,0:T(8,128)} %bitcast.30), custom_call_target="tpu_custom_call" | custom-call | tf_op jit(solution)/shard_map/pallas_call | solution.py:304
  165.0 4.9 %all-to-all-start.1 = ((f32[128,24,150]{2,1,0:T(8,128)}), f32[128,24,150]{2,1,0:T(8,128)S(1)}, u32[]{:S(2)}, u32[]{:S(2)}) async-start(f32[128,24,150]{2,1,0:T(8,128)} %bitcast.31), calls=%async_computation.1 | async-start | bytes 6291456 | tf_op jit(solution)/shard_map/all_to_all | solution.py:324
  169.9 2.7 copy.12
  172.6 38.4 %all-to-all-done.1 = f32[128,24,150]{2,1,0:T(8,128)S(1)} async-done(((f32[128,24,150]{2,1,0:T(8,128)}), f32[128,24,150]{2,1,0:T(8,128)S(1)}, u32[]{:S(2)}, u32[]{:S(2)}) %all-to-all-start.1) | async-done | bytes 1843232 | tf_op jit(solution)/shard_map/all_to_all | solution.py:324
  211.0 0.0 copy-start.1
  211.0 1.7 copy-done.1
  212.7 21.4 %shard_map.89 = f32[4096,150]{1,0:T(8,128)} custom-call(s32[3072]{0:T(1024)} %bitcast.34, f32[3072,150]{1,0:T(8,128)} %bitcast.23), custom_call_target="tpu_custom_call" | custom-call | tf_op jit(solution)/shard_map/pallas_call | solution.py:292
  234.1 5.0 %copy.11 = f32[32,128,150]{1,0,2:T(8,128)} copy(f32[32,128,150]{2,1,0:T(8,128)} %bitcast.21) | data formatting | bytes 4915200 | tf_op jit(solution)/shard_map/reshape | solution.py:343
  239.1 53.4 %shard_map.90 = f32[5,960,128]{2,1,0:T(8,128)} custom-call(f32[5,960,128]{2,1,0:T(8,128)} %bitcast.28, f32[5,960,128]{2,1,0:T(8,128)} %bitcast.19, f32[5,960,128]{2,1,0:T(8,128)} %bitcast.27), custom_call_target="tpu_custom_call" | custom-call | flops 30720000 | bytes 7372800 | tf_op jit(solution)/shard_map/pallas_call | solution.py:181
  292.5 3.3 %copy.14 = f32[150,32,128]{2,1,0:T(8,128)} copy(f32[150,32,128]{2,1,0:T(8,128)} %bitcast.29) | data formatting | bytes 4915200
Async XLA Ops:
  0.6 2.1 copy-start.2
  81.1 47.6 %all-to-all-start = ((f32[128,24,150]{2,1,0:T(8,128)}), f32[128,24,150]{2,1,0:T(8,128)S(1)}, u32[]{:S(2)}, u32[]{:S(2)}) async-start(f32[128,24,150]{2,1,0:T(8,128)} %bitcast.24), calls=%async_computation | async-start | bytes 6291456 | tf_op jit(solution)/shard_map/all_to_all | solution.py:320
  128.8 1.7 copy-start
  165.0 46.1 %all-to-all-start.1 = ((f32[128,24,150]{2,1,0:T(8,128)}), f32[128,24,150]{2,1,0:T(8,128)S(1)}, u32[]{:S(2)}, u32[]{:S(2)}) async-start(f32[128,24,150]{2,1,0:T(8,128)} %bitcast.31), calls=%async_computation.1 | async-start | bytes 6291456 | tf_op jit(solution)/shard_map/all_to_all | solution.py:324
  211.0 1.7 copy-start.1

commit v16 on v13

--- a/solution.py
+++ b/solution.py
@@ -214,7 +214,7 @@
         out_ref[pl.ds(pl.multiple_of(t * 8, 8), 8), :] = tile
         return carry
 
-    lax.fori_loop(0, out_ref.shape[0] // 8, body, 0, unroll=2)
+    lax.fori_loop(0, out_ref.shape[0] // 8, body, 0, unroll=4)
 
 
 def place_kernel(index_ref, rows_ref, out_ref, *parts):
@@ -230,7 +230,7 @@
             add_row(part, jnp.minimum(target, cells - 1), jnp.where(target < cells, row, 0.0))
         return carry
 
-    lax.fori_loop(0, rows_ref.shape[0] // len(parts), body, 0, unroll=2)
+    lax.fori_loop(0, rows_ref.shape[0] // len(parts), body, 0, unroll=4)
     total = parts[0][...]
     for part in parts[1:]:
         total = total + part[...]

time: 298 us -> 296 us (level)
  no operation moved by 1% of the time
where the time goes in v16:
time: 296 us; the launch traced here: 294 us
  Pallas kernels  178 us (60%)
  waiting for transfers between devices  76.7 us (26%)
  local copies, waits for them, and re-layouts  19.1 us (6%)
  starting transfers between devices  11.5 us (4%)
  other arithmetic  7.13 us (2%)
    pallas_call x2, Pallas kernels, diffuse(): pl.pallas_call(functools.partial(diffuse_kernel, rows), in_specs=[VMEM, V...  109 us
    all_to_all x1, waiting for transfers between devices, to_sources(): lax.all_to_all(returned, ('lon', 'lat'), split_axis=0, concat_axis=0, til...  38.4 us
    all_to_all x1, waiting for transfers between devices, to_owners(): lax.all_to_all(outgoing, ('lon', 'lat'), split_axis=0, concat_axis=0, til...  38.2 us
    pallas_call x1, Pallas kernels, interpolate(): pl.pallas_call(interp_kernel, in_specs=[SMEM, SMEM, VMEM, VMEM], out_spec...  34.5 us
    pallas_call x1, Pallas kernels, place_rows(): pl.pallas_call(place_kernel, in_specs=[SMEM, VMEM], out_specs=VMEM, out_s...  20.6 us
    pallas_call x1, Pallas kernels, select_rows(): pl.pallas_call(select_kernel, in_specs=[SMEM, VMEM], out_specs=VMEM, out_...  14.7 us
    unnamed x10, local copies, waits for them, and re-layouts  9.31 us
    all_to_all x1, starting transfers between devices, to_owners(): lax.all_to_all(outgoing, ('lon', 'lat'), split_axis=0, concat_axis=0, til...  6.59 us
  transfers between devices with their start and end apart: 2, of which 2 were waited for; matrix products, arithmetic and copies ran while one was open for 2% of the time, Pallas kernels for 0%

profile of v16, /device:TPU:8, one launch (start us, length us, event | category | flops | bytes accessed | tf_op | source)
XLA Modules:
  0.0 293.6 jit_solution(12401426349579231106)
XLA Ops:
  0.6 0.0 copy-start.3
  0.6 1.6 convert_element_type.3
  2.2 0.5 copy-done.3
  2.7 1.9 maximum_multiply_fusion
  4.6 56.5 %shard_map.86 = f32[5,960,128]{2,1,0:T(8,128)} custom-call(f32[5,960,128]{2,1,0:T(8,128)} %bitcast.25, f32[5,960,128]{2,1,0:T(8,128)} %bitcast.18), custom_call_target="tpu_custom_call" | custom-call | flops 30720000 | bytes 7372800 | tf_op jit(solution)/shard_map/pallas_call | solution.py:171
  61.1 4.8 %copy.9 = f32[150,32,128]{0,2,1:T(8,128)} copy(f32[150,32,128]{2,1,0:T(8,128)} %bitcast.28) | data formatting | bytes 4915200 | tf_op jit(solution)/shard_map/reshape | solution.py:191
  65.9 14.7 %shard_map.87 = f32[3072,150]{1,0:T(8,128)} custom-call(s32[3072]{0:T(1024)} %bitcast.32, f32[4096,150]{1,0:T(8,128)} %bitcast.20), custom_call_target="tpu_custom_call" | custom-call | tf_op jit(solution)/shard_map/pallas_call | solution.py:271
  80.6 6.6 %all-to-all-start = ((f32[128,24,150]{2,1,0:T(8,128)}), f32[128,24,150]{2,1,0:T(8,128)S(1)}, u32[]{:S(2)}, u32[]{:S(2)}) async-start(f32[128,24,150]{2,1,0:T(8,128)} %bitcast.24), calls=%async_computation | async-start | bytes 6291456 | tf_op jit(solution)/shard_map/all_to_all | solution.py:308
  87.2 2.8 copy.10
  90.0 38.2 %all-to-all-done = f32[128,24,150]{2,1,0:T(8,128)S(1)} async-done(((f32[128,24,150]{2,1,0:T(8,128)}), f32[128,24,150]{2,1,0:T(8,128)S(1)}, u32[]{:S(2)}, u32[]{:S(2)}) %all-to-all-start) | async-done | bytes 1843232 | tf_op jit(solution)/shard_map/all_to_all | solution.py:308
  128.2 0.0 copy-start
  128.2 1.7 copy-done
  129.9 34.5 %shard_map.88 = (f32[2048,150]{1,0:T(8,128)}, f32[3072,150]{1,0:T(8,128)}) custom-call(s32[4,2048]{1,0:T(4,128)} %slot_ref.1, f32[4,2048]{1,0:T(4,128)} %weight_ref.1, f32[3072,150]{1,0:T(8,128)} %bitcast.22, f32[2048,150]{1,0:T(8,128)} %bitcast.29), custom_call_target="tpu_custom_call" | custom-call | tf_op jit(solution)/shard_map/pallas_call | solution.py:292
  164.4 4.9 %all-to-all-start.1 = ((f32[128,24,150]{2,1,0:T(8,128)}), f32[128,24,150]{2,1,0:T(8,128)S(1)}, u32[]{:S(2)}, u32[]{:S(2)}) async-start(f32[128,24,150]{2,1,0:T(8,128)} %bitcast.30), calls=%async_computation.1 | async-start | bytes 6291456 | tf_op jit(solution)/shard_map/all_to_all | solution.py:312
  169.4 2.7 copy.12
  172.1 38.4 %all-to-all-done.1 = f32[128,24,150]{2,1,0:T(8,128)S(1)} async-done(((f32[128,24,150]{2,1,0:T(8,128)}), f32[128,24,150]{2,1,0:T(8,128)S(1)}, u32[]{:S(2)}, u32[]{:S(2)}) %all-to-all-start.1) | async-done | bytes 1843232 | tf_op jit(solution)/shard_map/all_to_all | solution.py:312
  210.5 0.0 copy-start.1
  210.5 1.7 copy-done.1
  212.2 20.6 %shard_map.89 = f32[4096,150]{1,0:T(8,128)} custom-call(s32[3072]{0:T(1024)} %bitcast.33, f32[3072,150]{1,0:T(8,128)} %bitcast.23), custom_call_target="tpu_custom_call" | custom-call | tf_op jit(solution)/shard_map/pallas_call | solution.py:280
  232.7 5.0 %copy.11 = f32[32,128,150]{1,0,2:T(8,128)} copy(f32[32,128,150]{2,1,0:T(8,128)} %bitcast.21) | data formatting | bytes 4915200 | tf_op jit(solution)/shard_map/reshape | solution.py:331
  237.7 0.0 copy-start.2
  237.7 52.2 %shard_map.90 = f32[5,960,128]{2,1,0:T(8,128)} custom-call(f32[5,960,128]{2,1,0:T(8,128)} %bitcast.26, f32[5,960,128]{2,1,0:T(8,128)} %bitcast.19), custom_call_target="tpu_custom_call" | custom-call | flops 30720000 | bytes 7372800 | tf_op jit(solution)/shard_map/pallas_call | solution.py:171
  289.9 0.0 copy-done.2
  289.9 3.7 %add.3 = f32[150,32,128]{2,1,0:T(8,128)} add(f32[150,32,128]{2,1,0:T(8,128)S(1)} %copy-done.2, f32[150,32,128]{2,1,0:T(8,128)} %bitcast.27) | non-fusion elementwise | flops 614400 | bytes 7372800 | tf_op jit(solution)/shard_map/add | solution.py:332
Async XLA Ops:
  0.6 2.1 copy-start.3
  80.6 47.6 %all-to-all-start = ((f32[128,24,150]{2,1,0:T(8,128)}), f32[128,24,150]{2,1,0:T(8,128)S(1)}, u32[]{:S(2)}, u32[]{:S(2)}) async-start(f32[128,24,150]{2,1,0:T(8,128)} %bitcast.24), calls=%async_computation | async-start | bytes 6291456 | tf_op jit(solution)/shard_map/all_to_all | solution.py:308
  128.2 1.7 copy-start
  164.4 46.1 %all-to-all-start.1 = ((f32[128,24,150]{2,1,0:T(8,128)}), f32[128,24,150]{2,1,0:T(8,128)S(1)}, u32[]{:S(2)}, u32[]{:S(2)}) async-start(f32[128,24,150]{2,1,0:T(8,128)} %bitcast.30), calls=%async_computation.1 | async-start | bytes 6291456 | tf_op jit(solution)/shard_map/all_to_all | solution.py:312
  210.5 1.7 copy-start.1
  237.7 52.2 %copy-start.2 = (f32[150,32,128]{2,1,0:T(8,128)S(1)}, f32[150,32,128]{2,1,0:T(8,128)}, u32[]{:S(2)}) copy-start(f32[150,32,128]{2,1,0:T(8,128)} %param.7) | copy-start | bytes 7372804

commit v17 on v16

--- a/solution.py
+++ b/solution.py
@@ -214,7 +214,7 @@
         out_ref[pl.ds(pl.multiple_of(t * 8, 8), 8), :] = tile
         return carry
 
-    lax.fori_loop(0, out_ref.shape[0] // 8, body, 0, unroll=4)
+    lax.fori_loop(0, out_ref.shape[0] // 8, body, 0, unroll=8)
 
 
 def place_kernel(index_ref, rows_ref, out_ref, *parts):
@@ -230,7 +230,7 @@
             add_row(part, jnp.minimum(target, cells - 1), jnp.where(target < cells, row, 0.0))
         return carry
 
-    lax.fori_loop(0, rows_ref.shape[0] // len(parts), body, 0, unroll=4)
+    lax.fori_loop(0, rows_ref.shape[0] // len(parts), body, 0, unroll=8)
     total = parts[0][...]
     for part in parts[1:]:
         total = total + part[...]

time: 296 us -> 296 us (level)
  no operation moved by 1% of the time
where the time goes in v17:
time: 296 us; the launch traced here: 293 us
  Pallas kernels  178 us (60%)
  waiting for transfers between devices  76.7 us (26%)
  local copies, waits for them, and re-layouts  19.1 us (6%)
  starting transfers between devices  11.5 us (4%)
  other arithmetic  7.13 us (2%)
    pallas_call x2, Pallas kernels, diffuse(): pl.pallas_call(functools.partial(diffuse_kernel, rows), in_specs=[VMEM, V...  109 us
    all_to_all x1, waiting for transfers between devices, to_sources(): lax.all_to_all(returned, ('lon', 'lat'), split_axis=0, concat_axis=0, til...  38.4 us
    all_to_all x1, waiting for transfers between devices, to_owners(): lax.all_to_all(outgoing, ('lon', 'lat'), split_axis=0, concat_axis=0, til...  38.2 us
    pallas_call x1, Pallas kernels, interpolate(): pl.pallas_call(interp_kernel, in_specs=[SMEM, SMEM, VMEM, VMEM], out_spec...  34.5 us
    pallas_call x1, Pallas kernels, place_rows(): pl.pallas_call(place_kernel, in_specs=[SMEM, VMEM], out_specs=VMEM, out_s...  20.1 us
    pallas_call x1, Pallas kernels, select_rows(): pl.pallas_call(select_kernel, in_specs=[SMEM, VMEM], out_specs=VMEM, out_...  14.8 us
    unnamed x10, local copies, waits for them, and re-layouts  9.31 us
    all_to_all x1, starting transfers between devices, to_owners(): lax.all_to_all(outgoing, ('lon', 'lat'), split_axis=0, concat_axis=0, til...  6.59 us
  transfers between devices with their start and end apart: 2, of which 2 were waited for; matrix products, arithmetic and copies ran while one was open for 2% of the time, Pallas kernels for 0%

profile of v17, /device:TPU:8, one launch (start us, length us, event | category | flops | bytes accessed | tf_op | source)
XLA Modules:
  0.0 293.3 jit_solution(4966592446389284460)
XLA Ops:
  0.6 0.0 copy-start.3
  0.6 1.6 convert_element_type.3
  2.2 0.5 copy-done.3
  2.7 1.9 maximum_multiply_fusion
  4.6 56.5 %shard_map.86 = f32[5,960,128]{2,1,0:T(8,128)} custom-call(f32[5,960,128]{2,1,0:T(8,128)} %bitcast.25, f32[5,960,128]{2,1,0:T(8,128)} %bitcast.18), custom_call_target="tpu_custom_call" | custom-call | flops 30720000 | bytes 7372800 | tf_op jit(solution)/shard_map/pallas_call | solution.py:171
  61.1 4.8 %copy.9 = f32[150,32,128]{0,2,1:T(8,128)} copy(f32[150,32,128]{2,1,0:T(8,128)} %bitcast.28) | data formatting | bytes 4915200 | tf_op jit(solution)/shard_map/reshape | solution.py:191
  65.9 14.8 %shard_map.87 = f32[3072,150]{1,0:T(8,128)} custom-call(s32[3072]{0:T(1024)} %bitcast.32, f32[4096,150]{1,0:T(8,128)} %bitcast.20), custom_call_target="tpu_custom_call" | custom-call | tf_op jit(solution)/shard_map/pallas_call | solution.py:271
  80.8 6.6 %all-to-all-start = ((f32[128,24,150]{2,1,0:T(8,128)}), f32[128,24,150]{2,1,0:T(8,128)S(1)}, u32[]{:S(2)}, u32[]{:S(2)}) async-start(f32[128,24,150]{2,1,0:T(8,128)} %bitcast.24), calls=%async_computation | async-start | bytes 6291456 | tf_op jit(solution)/shard_map/all_to_all | solution.py:308
  87.4 2.8 copy.10
  90.2 38.2 %all-to-all-done = f32[128,24,150]{2,1,0:T(8,128)S(1)} async-done(((f32[128,24,150]{2,1,0:T(8,128)}), f32[128,24,150]{2,1,0:T(8,128)S(1)}, u32[]{:S(2)}, u32[]{:S(2)}) %all-to-all-start) | async-done | bytes 1843232 | tf_op jit(solution)/shard_map/all_to_all | solution.py:308
  128.4 0.0 copy-start
  128.4 1.7 copy-done
  130.1 34.5 %shard_map.88 = (f32[2048,150]{1,0:T(8,128)}, f32[3072,150]{1,0:T(8,128)}) custom-call(s32[4,2048]{1,0:T(4,128)} %slot_ref.1, f32[4,2048]{1,0:T(4,128)} %weight_ref.1, f32[3072,150]{1,0:T(8,128)} %bitcast.22, f32[2048,150]{1,0:T(8,128)} %bitcast.29), custom_call_target="tpu_custom_call" | custom-call | tf_op jit(solution)/shard_map/pallas_call | solution.py:292
  164.6 4.9 %all-to-all-start.1 = ((f32[128,24,150]{2,1,0:T(8,128)}), f32[128,24,150]{2,1,0:T(8,128)S(1)}, u32[]{:S(2)}, u32[]{:S(2)}) async-start(f32[128,24,150]{2,1,0:T(8,128)} %bitcast.30), calls=%async_computation.1 | async-start | bytes 6291456 | tf_op jit(solution)/shard_map/all_to_all | solution.py:312
  169.5 2.7 copy.12
  172.2 38.4 %all-to-all-done.1 = f32[128,24,150]{2,1,0:T(8,128)S(1)} async-done(((f32[128,24,150]{2,1,0:T(8,128)}), f32[128,24,150]{2,1,0:T(8,128)S(1)}, u32[]{:S(2)}, u32[]{:S(2)}) %all-to-all-start.1) | async-done | bytes 1843232 | tf_op jit(solution)/shard_map/all_to_all | solution.py:312
  210.6 0.0 copy-start.1
  210.6 1.7 copy-done.1
  212.3 20.1 %shard_map.89 = f32[4096,150]{1,0:T(8,128)} custom-call(s32[3072]{0:T(1024)} %bitcast.33, f32[3072,150]{1,0:T(8,128)} %bitcast.23), custom_call_target="tpu_custom_call" | custom-call | tf_op jit(solution)/shard_map/pallas_call | solution.py:280
  232.4 5.0 %copy.11 = f32[32,128,150]{1,0,2:T(8,128)} copy(f32[32,128,150]{2,1,0:T(8,128)} %bitcast.21) | data formatting | bytes 4915200 | tf_op jit(solution)/shard_map/reshape | solution.py:331
  237.4 0.0 copy-start.2
  237.4 52.2 %shard_map.90 = f32[5,960,128]{2,1,0:T(8,128)} custom-call(f32[5,960,128]{2,1,0:T(8,128)} %bitcast.26, f32[5,960,128]{2,1,0:T(8,128)} %bitcast.19), custom_call_target="tpu_custom_call" | custom-call | flops 30720000 | bytes 7372800 | tf_op jit(solution)/shard_map/pallas_call | solution.py:171
  289.6 0.0 copy-done.2
  289.6 3.7 %add.3 = f32[150,32,128]{2,1,0:T(8,128)} add(f32[150,32,128]{2,1,0:T(8,128)S(1)} %copy-done.2, f32[150,32,128]{2,1,0:T(8,128)} %bitcast.27) | non-fusion elementwise | flops 614400 | bytes 7372800 | tf_op jit(solution)/shard_map/add | solution.py:332
Async XLA Ops:
  0.6 2.1 copy-start.3
  80.8 47.6 %all-to-all-start = ((f32[128,24,150]{2,1,0:T(8,128)}), f32[128,24,150]{2,1,0:T(8,128)S(1)}, u32[]{:S(2)}, u32[]{:S(2)}) async-start(f32[128,24,150]{2,1,0:T(8,128)} %bitcast.24), calls=%async_computation | async-start | bytes 6291456 | tf_op jit(solution)/shard_map/all_to_all | solution.py:308
  128.4 1.7 copy-start
  164.6 46.1 %all-to-all-start.1 = ((f32[128,24,150]{2,1,0:T(8,128)}), f32[128,24,150]{2,1,0:T(8,128)S(1)}, u32[]{:S(2)}, u32[]{:S(2)}) async-start(f32[128,24,150]{2,1,0:T(8,128)} %bitcast.30), calls=%async_computation.1 | async-start | bytes 6291456 | tf_op jit(solution)/shard_map/all_to_all | solution.py:312
  210.6 1.7 copy-start.1
  237.4 52.2 %copy-start.2 = (f32[150,32,128]{2,1,0:T(8,128)S(1)}, f32[150,32,128]{2,1,0:T(8,128)}, u32[]{:S(2)}) copy-start(f32[150,32,128]{2,1,0:T(8,128)} %param.7) | copy-start | bytes 7372804

commit v18 on v16

--- a/solution.py
+++ b/solution.py
@@ -260,7 +260,7 @@
         equiv_ref[pl.ds(pl.multiple_of(t * 8, 8), 8), :] = tile
         return carry
 
-    lax.fori_loop(0, obs_count // 8, body, 0, unroll=2)
+    lax.fori_loop(0, obs_count // 8, body, 0, unroll=4)
     total = parts[0][...]
     for part in parts[1:]:
         total = total + part[...]

time: 296 us -> 296 us (level)
  no operation moved by 1% of the time
where the time goes in v18:
time: 296 us; the launch traced here: 293 us
  Pallas kernels  178 us (60%)
  waiting for transfers between devices  76.7 us (26%)
  local copies, waits for them, and re-layouts  19.1 us (6%)
  starting transfers between devices  11.5 us (4%)
  other arithmetic  7.13 us (2%)
    pallas_call x2, Pallas kernels, diffuse(): pl.pallas_call(functools.partial(diffuse_kernel, rows), in_specs=[VMEM, V...  109 us
    all_to_all x1, waiting for transfers between devices, to_sources(): lax.all_to_all(returned, ('lon', 'lat'), split_axis=0, concat_axis=0, til...  38.4 us
    all_to_all x1, waiting for transfers between devices, to_owners(): lax.all_to_all(outgoing, ('lon', 'lat'), split_axis=0, concat_axis=0, til...  38.2 us
    pallas_call x1, Pallas kernels, interpolate(): pl.pallas_call(interp_kernel, in_specs=[SMEM, SMEM, VMEM, VMEM], out_spec...  34.2 us
    pallas_call x1, Pallas kernels, place_rows(): pl.pallas_call(place_kernel, in_specs=[SMEM, VMEM], out_specs=VMEM, out_s...  20.6 us
    pallas_call x1, Pallas kernels, select_rows(): pl.pallas_call(select_kernel, in_specs=[SMEM, VMEM], out_specs=VMEM, out_...  14.7 us
    unnamed x10, local copies, waits for them, and re-layouts  9.31 us
    all_to_all x1, starting transfers between devices, to_owners(): lax.all_to_all(outgoing, ('lon', 'lat'), split_axis=0, concat_axis=0, til...  6.59 us
  transfers between devices with their start and end apart: 2, of which 2 were waited for; matrix products, arithmetic and copies ran while one was open for 2% of the time, Pallas kernels for 0%

profile of v18, /device:TPU:8, one launch (start us, length us, event | category | flops | bytes accessed | tf_op | source)
XLA Modules:
  0.0 293.3 jit_solution(3295083064271537979)
XLA Ops:
  0.6 0.0 copy-start.3
  0.6 1.6 convert_element_type.3
  2.2 0.5 copy-done.3
  2.7 1.9 maximum_multiply_fusion
  4.6 56.5 %shard_map.86 = f32[5,960,128]{2,1,0:T(8,128)} custom-call(f32[5,960,128]{2,1,0:T(8,128)} %bitcast.25, f32[5,960,128]{2,1,0:T(8,128)} %bitcast.18), custom_call_target="tpu_custom_call" | custom-call | flops 30720000 | bytes 7372800 | tf_op jit(solution)/shard_map/pallas_call | solution.py:171
  61.1 4.8 %copy.9 = f32[150,32,128]{0,2,1:T(8,128)} copy(f32[150,32,128]{2,1,0:T(8,128)} %bitcast.28) | data formatting | bytes 4915200 | tf_op jit(solution)/shard_map/reshape | solution.py:191
  65.9 14.7 %shard_map.87 = f32[3072,150]{1,0:T(8,128)} custom-call(s32[3072]{0:T(1024)} %bitcast.32, f32[4096,150]{1,0:T(8,128)} %bitcast.20), custom_call_target="tpu_custom_call" | custom-call | tf_op jit(solution)/shard_map/pallas_call | solution.py:271
  80.6 6.6 %all-to-all-start = ((f32[128,24,150]{2,1,0:T(8,128)}), f32[128,24,150]{2,1,0:T(8,128)S(1)}, u32[]{:S(2)}, u32[]{:S(2)}) async-start(f32[128,24,150]{2,1,0:T(8,128)} %bitcast.24), calls=%async_computation | async-start | bytes 6291456 | tf_op jit(solution)/shard_map/all_to_all | solution.py:308
  87.2 2.8 copy.10
  90.0 38.2 %all-to-all-done = f32[128,24,150]{2,1,0:T(8,128)S(1)} async-done(((f32[128,24,150]{2,1,0:T(8,128)}), f32[128,24,150]{2,1,0:T(8,128)S(1)}, u32[]{:S(2)}, u32[]{:S(2)}) %all-to-all-start) | async-done | bytes 1843232 | tf_op jit(solution)/shard_map/all_to_all | solution.py:308
  128.2 0.0 copy-start
  128.2 1.7 copy-done
  129.9 34.2 %shard_map.88 = (f32[2048,150]{1,0:T(8,128)}, f32[3072,150]{1,0:T(8,128)}) custom-call(s32[4,2048]{1,0:T(4,128)} %slot_ref.1, f32[4,2048]{1,0:T(4,128)} %weight_ref.1, f32[3072,150]{1,0:T(8,128)} %bitcast.22, f32[2048,150]{1,0:T(8,128)} %bitcast.29), custom_call_target="tpu_custom_call" | custom-call | tf_op jit(solution)/shard_map/pallas_call | solution.py:292
  164.1 4.9 %all-to-all-start.1 = ((f32[128,24,150]{2,1,0:T(8,128)}), f32[128,24,150]{2,1,0:T(8,128)S(1)}, u32[]{:S(2)}, u32[]{:S(2)}) async-start(f32[128,24,150]{2,1,0:T(8,128)} %bitcast.30), calls=%async_computation.1 | async-start | bytes 6291456 | tf_op jit(solution)/shard_map/all_to_all | solution.py:312
  169.0 2.7 copy.12
  171.7 38.4 %all-to-all-done.1 = f32[128,24,150]{2,1,0:T(8,128)S(1)} async-done(((f32[128,24,150]{2,1,0:T(8,128)}), f32[128,24,150]{2,1,0:T(8,128)S(1)}, u32[]{:S(2)}, u32[]{:S(2)}) %all-to-all-start.1) | async-done | bytes 1843232 | tf_op jit(solution)/shard_map/all_to_all | solution.py:312
  210.1 0.0 copy-start.1
  210.1 1.7 copy-done.1
  211.8 20.6 %shard_map.89 = f32[4096,150]{1,0:T(8,128)} custom-call(s32[3072]{0:T(1024)} %bitcast.33, f32[3072,150]{1,0:T(8,128)} %bitcast.23), custom_call_target="tpu_custom_call" | custom-call | tf_op jit(solution)/shard_map/pallas_call | solution.py:280
  232.4 5.0 %copy.11 = f32[32,128,150]{1,0,2:T(8,128)} copy(f32[32,128,150]{2,1,0:T(8,128)} %bitcast.21) | data formatting | bytes 4915200 | tf_op jit(solution)/shard_map/reshape | solution.py:331
  237.4 0.0 copy-start.2
  237.4 52.2 %shard_map.90 = f32[5,960,128]{2,1,0:T(8,128)} custom-call(f32[5,960,128]{2,1,0:T(8,128)} %bitcast.26, f32[5,960,128]{2,1,0:T(8,128)} %bitcast.19), custom_call_target="tpu_custom_call" | custom-call | flops 30720000 | bytes 7372800 | tf_op jit(solution)/shard_map/pallas_call | solution.py:171
  289.6 0.0 copy-done.2
  289.6 3.7 %add.3 = f32[150,32,128]{2,1,0:T(8,128)} add(f32[150,32,128]{2,1,0:T(8,128)S(1)} %copy-done.2, f32[150,32,128]{2,1,0:T(8,128)} %bitcast.27) | non-fusion elementwise | flops 614400 | bytes 7372800 | tf_op jit(solution)/shard_map/add | solution.py:332
Async XLA Ops:
  0.6 2.1 copy-start.3
  80.6 47.6 %all-to-all-start = ((f32[128,24,150]{2,1,0:T(8,128)}), f32[128,24,150]{2,1,0:T(8,128)S(1)}, u32[]{:S(2)}, u32[]{:S(2)}) async-start(f32[128,24,150]{2,1,0:T(8,128)} %bitcast.24), calls=%async_computation | async-start | bytes 6291456 | tf_op jit(solution)/shard_map/all_to_all | solution.py:308
  128.2 1.7 copy-start
  164.1 46.1 %all-to-all-start.1 = ((f32[128,24,150]{2,1,0:T(8,128)}), f32[128,24,150]{2,1,0:T(8,128)S(1)}, u32[]{:S(2)}, u32[]{:S(2)}) async-start(f32[128,24,150]{2,1,0:T(8,128)} %bitcast.30), calls=%async_computation.1 | async-start | bytes 6291456 | tf_op jit(solution)/shard_map/all_to_all | solution.py:312
  210.1 1.7 copy-start.1
  237.4 52.2 %copy-start.2 = (f32[150,32,128]{2,1,0:T(8,128)S(1)}, f32[150,32,128]{2,1,0:T(8,128)}, u32[]{:S(2)}) copy-start(f32[150,32,128]{2,1,0:T(8,128)} %param.7) | copy-start | bytes 7372804
